TPU v7x, 128 devices: a whole 4x4x4 slice. The times are simulated.
128 devices in a mesh: rep: 4 (over y), shard: 32 (over x, z, core).
Axes of the slice: x: 4, y: 4, z: 4, core: 2. Of those that a mesh axis runs over, the one named last changes fastest.
Arguments:
- short_tokens: bfloat16 [256, 64, 768], P(('rep', 'shard')), may hold values from -6 to 6
- long_tokens: bfloat16 [256, 256, 768], P(('rep', 'shard')), may hold values from -6 to 6
- short_lengths: int32 [256], P(('rep', 'shard')), may hold values from 16 to 64
- long_lengths: int32 [256], P(('rep', 'shard')), may hold values from 65 to 256
- short_cotangent: bfloat16 [256, 64, 768], P(('rep', 'shard')), may hold values from -6 to 6
- long_cotangent: bfloat16 [256, 256, 768], P(('rep', 'shard')), may hold values from -6 to 6
- input_weight: bfloat16 [768, 2304], P('shard'), may hold values from -0.21875 to 0.21875
- query_bias: bfloat16 [768], P('shard'), may hold values from -3 to 3
- value_bias: bfloat16 [768], P('shard'), may hold values from -1.1953125 to 1.1953125
- output_weight: bfloat16 [768, 768], P('shard'), may hold values from -0.625 to 0.625
- output_bias: bfloat16 [768], P('shard'), may hold values from -1.1953125 to 1.1953125
- first_gain: bfloat16 [768], P('shard'), may hold values from 0.5 to 1.5
- first_shift: bfloat16 [768], P('shard'), may hold values from -1.1953125 to 1.1953125
- up_weight: bfloat16 [768, 3072], P('shard'), may hold values from -0.21875 to 0.21875
- up_bias: bfloat16 [3072], P('shard'), may hold values from -3 to 3
- down_weight: bfloat16 [3072, 768], P('shard'), may hold values from -0.109375 to 0.109375
- down_bias: bfloat16 [768], P('shard'), may hold values from -1.1953125 to 1.1953125
- second_gain: bfloat16 [768], P('shard'), may hold values from 0.5 to 1.5
- second_shift: bfloat16 [768], P('shard'), may hold values from -1.1953125 to 1.1953125
Outputs:
- short_out: bfloat16 [256, 64, 768], P(('rep', 'shard'))
- long_out: bfloat16 [256, 256, 768], P(('rep', 'shard'))
- short_grad: float32 [256, 64, 768], P(('rep', 'shard'))
- long_grad: float32 [256, 256, 768], P(('rep', 'shard'))
- grad_input_weight: float32 [768, 2304], P('shard')
- grad_query_bias: float32 [768], P('shard')
- grad_value_bias: float32 [768], P('shard')
- grad_output_weight: float32 [768, 768], P('shard')
- grad_output_bias: float32 [768], P('shard')
- grad_first_gain: float32 [768], P('shard')
- grad_first_shift: float32 [768], P('shard')
- grad_up_weight: float32 [768, 3072], P('shard')
- grad_up_bias: float32 [3072], P('shard')
- grad_down_weight: float32 [3072, 768], P('shard')
- grad_down_bias: float32 [768], P('shard')
- grad_second_gain: float32 [768], P('shard')
- grad_second_shift: float32 [768], P('shard')
All inputs are finite; a program needn't handle non-finite values.
Results may differ from a plain program's by a relative error of at most 0.025.
Values may be sent and summed in bfloat16 or wider, within the bound.
No kernel may reach another device: no remote copies, remote signals or barrier semaphores. Data moves between devices by JAX's collectives and lax.ppermute only.
A program may use at most 192 MiB of HBM per device.

v0:
```python
import functools

import jax
import jax.numpy as jnp
from jax import lax
from jax.experimental import pallas as pl
from jax.experimental.pallas import tpu as pltpu
from jax.sharding import PartitionSpec as P

F32 = jnp.float32
BF16 = jnp.bfloat16
HEAD_DIM = 64
PAIR = 128
EPSILON = 1e-06
BACK_MIB = 58
QB, VB, OB, G1, S1, DB, G2, S2 = range(8)
RING = 4
CHIPS = RING * RING
SHARDS = 2 * CHIPS


def nn(a, b):
    return lax.dot_general(a, b, (((1,), (0,)), ((), ())), preferred_element_type=F32)


def nt(a, b):
    return lax.dot_general(a, b, (((1,), (1,)), ((), ())), preferred_element_type=F32)


def tn(a, b):
    return lax.dot_general(a, b, (((0,), (0,)), ((), ())), preferred_element_type=F32)


def iota(shape, dim):
    return lax.broadcasted_iota(jnp.int32, shape, dim)


def row_of(ref, i):
    return ref[i : i + 1, :].astype(F32)


def whole(*shape):
    return pl.BlockSpec(shape, lambda g, *_: (0,) * len(shape))


def params(mebibytes):
    return pltpu.CompilerParams(vmem_limit_bytes=mebibytes * 1024 * 1024)


def cost(flops, moved):
    return pl.CostEstimate(flops=int(flops), bytes_accessed=int(moved), transcendentals=0)


def places(pos, x, z):
    along_x, along_z = (x - pos[0]) & (RING - 1), (z - pos[1]) & (RING - 1)
    return along_x * RING + along_z, along_z * RING + along_x


def deal(keep, give, pos, value, at, each):
    first = pos[2] == 0
    for x in range(RING):
        for z in range(RING):
            p0, p1 = places(pos, x, z)
            low = 2 * (x * RING + z) * each
            even, odd = value[low : low + each], value[low + each : low + 2 * each]
            keep[jnp.where(first, p0, p1), at] = jnp.where(first, even, odd)
            give[jnp.where(first, p1, p0), at] = jnp.where(first, odd, even)


def spread(owners, width):
    each = width // owners
    at = iota((owners, width), 1)
    low = iota((owners, width), 0) * each
    return (at >= low) & (at < low + each)


def column_rest(rows, width, each):
    at = iota((1, width), 1)
    return jnp.broadcast_to(at - (at // each) * each, (rows, width))


def two_heads(pair):
    low_half = iota(pair.shape, 1) < HEAD_DIM
    zero = jnp.zeros_like(pair)
    return jnp.concatenate([jnp.where(low_half, pair, zero), jnp.where(low_half, zero, pair)], axis=0)


def own_lanes(stack):
    half = stack.shape[0] // 2
    return jnp.where(iota((half, stack.shape[1]), 1) < HEAD_DIM, stack[:half], stack[half:])


def normalized(hidden):
    center = hidden - jnp.mean(hidden, axis=-1, keepdims=True)
    spread_of = jnp.mean(center * center, axis=-1, keepdims=True)
    inverse = lax.rsqrt(spread_of + EPSILON)
    return center * inverse, inverse


def norm_back(scaled, unit, inverse):
    return inverse * (
        scaled
        - jnp.mean(scaled, axis=-1, keepdims=True)
        - unit * jnp.mean(scaled * unit, axis=-1, keepdims=True)
    )


def segments(dims):
    short_rows, long_count, long_length, _ = dims
    return [(0, short_rows, None)] + [
        (short_rows + i * long_length, long_length, i) for i in range(long_count)
    ]


def key_bias(slen, llen, short_length, rows, long_at):
    key = iota((rows, rows), 0)
    if long_at is not None:
        return jnp.where(key < llen[long_at], 0.0, -1e9).astype(F32)
    query = iota((rows, rows), 1)
    keep = jnp.zeros((rows, rows), jnp.bool_)
    for p in range(rows // short_length):
        low, high = p * short_length, (p + 1) * short_length
        keep = keep | ((key >= low) & (key < low + slen[p]) & (query >= low) & (query < high))
    return jnp.where(keep, 0.0, -1e9).astype(F32)


def valid_rows(slen, llen, dims):
    short_rows, long_count, long_length, short_length = dims
    parts = []
    at = iota((short_length, 1), 0)
    for p in range(short_rows // short_length):
        parts.append((at < slen[p]).astype(F32))
    at = iota((long_length, 1), 0)
    for p in range(long_count):
        parts.append((at < llen[p]).astype(F32))
    return jnp.concatenate(parts, axis=0)


def slabs_of(out, base, source, each, width):
    for j in range(source.shape[1] // width):
        out[base + j * each : base + (j + 1) * each] = source[:, j * width : (j + 1) * width]
    return base + source.shape[1] // width * each


def pack_body(wqkv, wo, wup, wdown, *rest):
    vectors, out = rest[:-1], rest[-1]
    each, width = wo.shape
    base = slabs_of(out, 0, wqkv, each, width)
    base = slabs_of(out, base, wo, each, width)
    out[base : base + 8] = jnp.zeros((8, width), BF16)
    for i, v in enumerate(vectors[:-1]):
        out[base : base + 1, i * each : (i + 1) * each] = v[...]
    out[base + 1 : base + 2, : vectors[-1].shape[1]] = vectors[-1][...]
    base = slabs_of(out, base + 8, wup, each, width)
    out[base:] = wdown[...]


def pack(wqkv, wo, wup, wdown, vectors, ub):
    each, width = wo.shape
    rows = wqkv.shape[1] // width * each + each + 8 + 2 * wdown.shape[0]
    return pl.pallas_call(
        pack_body,
        out_shape=jax.ShapeDtypeStruct((rows, width), BF16),
        compiler_params=params(58),
        name="pack",
    )(wqkv, wo, wup, wdown, *[v[None] for v in vectors], ub[None])


STEPS = (0, -1, 1, 2)


def gathered_at(pos, other, k, i):
    core = pos[2] ^ other
    x0, z0 = (pos[0] + STEPS[k]) & (RING - 1), (pos[1] + STEPS[i]) & (RING - 1)
    x1, z1 = (pos[0] + STEPS[i]) & (RING - 1), (pos[1] + STEPS[k]) & (RING - 1)
    return jnp.where(core == 0, (x0 * RING + z0) * 2, (x1 * RING + z1) * 2 + 1)


def arrivals(pos, pieces, target, sems, at):
    copies = []
    for other in range(2):
        for k in range(RING):
            for i in range(RING):
                n = (other * RING + k) * RING + i
                copies.append(
                    pltpu.make_async_copy(
                        pieces[other * RING + k].at[i, at], target.at[gathered_at(pos, other, k, i), at], sems.at[n]
                    )
                )
    return copies


def attention_forward_body(
    dims, slen, llen, pos, xs, xl, p0, p1, p2, p3, p4, p5, p6, p7,
    q_o, k_o, v_o, c_o, ps_o, pl_o, n_o, r_o, vecs_o, ub_o, gathered_o,
    x_all, total, wo_all, gathered, sems, out_sem,
):
    step = pl.program_id(0)
    short_rows, width = dims[0], x_all.shape[1]
    cols = q_o.shape[1]
    each = width // SHARDS
    keep_all = pltpu.make_async_copy(gathered, gathered_o, out_sem)

    @pl.when(step == 0)
    def _():
        copies = arrivals(pos, (p0, p1, p2, p3, p4, p5, p6, p7), gathered, sems, slice(None))
        for copy in copies:
            copy.start()
        x_all[:short_rows, :] = xs[...]
        x_all[short_rows:, :] = xl[...]
        total[...] = jnp.zeros_like(total)
        for copy in copies:
            copy.wait()
        keep_all.start()
        wo_all[...] = gathered[:, 3 * each : 4 * each].reshape(width, width)
        packed = gathered[:, 4 * each :]
        line = packed[:, 0, : 8 * each + 64]
        rest = column_rest(line.shape[1], width, each)
        mine = spread(SHARDS, width)
        for i in range(8):
            pick = (iota(rest.shape, 0) == rest + i * each).astype(BF16)
            row = jnp.sum(jnp.where(mine, nn(line, pick), 0.0), axis=0, keepdims=True)
            vecs_o[i : i + 1] = row.astype(BF16)
        inner = ub_o.shape[1]
        line = packed[:, 1, :128]
        pick = (iota((128, inner), 0) == column_rest(128, inner, inner // SHARDS)).astype(BF16)
        row = jnp.sum(jnp.where(spread(SHARDS, inner), nn(line, pick), 0.0), axis=0, keepdims=True)
        ub_o[...] = row.astype(BF16)

    x = x_all[...]
    at_cols = pl.ds(pl.multiple_of(step * cols, cols), cols)
    wq, wk, wv = (gathered[:, i * each : (i + 1) * each, at_cols].reshape(width, cols) for i in range(3))
    q_o[...] = (nn(x, wq) + vecs_o[QB : QB + 1, at_cols].astype(F32)).astype(BF16)
    k_o[...] = nn(x, wk).astype(BF16)
    v_o[...] = (nn(x, wv) + vecs_o[VB : VB + 1, at_cols].astype(F32)).astype(BF16)
    for first, rows, long_at in segments(dims):
        bias = key_bias(slen, llen, dims[3], rows, long_at)
        at = slice(first, first + rows)
        for pair in range(cols // PAIR):
            lanes = slice(pair * PAIR, (pair + 1) * PAIR)
            q = q_o[at, lanes] * jnp.asarray(HEAD_DIM**-0.5, BF16)
            scores = nt(two_heads(k_o[at, lanes]), q)
            probs = []
            for h in range(2):
                s = scores[h * rows : (h + 1) * rows] + bias
                e = jnp.exp(s - jnp.max(s, axis=0, keepdims=True))
                probs.append((e * (1.0 / jnp.sum(e, axis=0, keepdims=True))).astype(BF16))
            probs = jnp.concatenate(probs, axis=0)
            if long_at is None:
                ps_o[pair] = probs
            else:
                pl_o[long_at, pair] = probs
            c_o[at, lanes] = tn(probs, two_heads(v_o[at, lanes])).astype(BF16)
    total[...] += nn(c_o[...], wo_all[at_cols, :])

    @pl.when(step == pl.num_programs(0) - 1)
    def _():
        h = x_all[...].astype(F32) + (total[...] + row_of(vecs_o, OB))
        unit, inverse = normalized(h)
        n_o[...] = unit
        r_o[...] = inverse
        keep_all.wait()


def attention_forward(slen, llen, pos, xs, xl, pieces, inner, dims):
    rows, width = xs.shape[0] + xl.shape[0], xs.shape[1]
    short_rows, long_count, long_length, _ = dims
    step = 256
    steps, pairs = width // step, width // PAIR
    per = step // PAIR
    each_all = pieces[0].shape[1]
    cols = pl.BlockSpec((rows, step), lambda g, *_: (0, g))
    return pl.pallas_call(
        functools.partial(attention_forward_body, dims),
        grid_spec=pltpu.PrefetchScalarGridSpec(
            num_scalar_prefetch=3,
            grid=(steps,),
            in_specs=[
                whole(*xs.shape), whole(*xl.shape), *[pl.BlockSpec(memory_space=pl.ANY)] * 8,
            ],
            out_specs=[
                cols, cols, cols, cols,
                pl.BlockSpec((per, 2 * short_rows, short_rows), lambda g, *_: (g, 0, 0)),
                pl.BlockSpec((long_count, per, 2 * long_length, long_length), lambda g, *_: (0, g, 0, 0)),
                whole(rows, width), whole(rows, 1), whole(8, width), whole(1, inner),
                pl.BlockSpec(memory_space=pl.ANY),
            ],
            scratch_shapes=[
                pltpu.VMEM((rows, width), BF16), pltpu.VMEM((rows, width), F32), pltpu.VMEM((width, width), BF16),
                pltpu.VMEM((SHARDS, each_all, width), BF16), pltpu.SemaphoreType.DMA((SHARDS,)),
                pltpu.SemaphoreType.DMA(()),
            ],
        ),
        out_shape=[
            *[jax.ShapeDtypeStruct((rows, width), BF16)] * 4,
            jax.ShapeDtypeStruct((pairs, 2 * short_rows, short_rows), BF16),
            jax.ShapeDtypeStruct((long_count, pairs, 2 * long_length, long_length), BF16),
            jax.ShapeDtypeStruct((rows, width), F32),
            jax.ShapeDtypeStruct((rows, 1), F32),
            jax.ShapeDtypeStruct((8, width), BF16),
            jax.ShapeDtypeStruct((1, inner), BF16),
            jax.ShapeDtypeStruct((SHARDS, each_all, width), BF16),
        ],
        compiler_params=params(58),
        cost_estimate=cost(8 * rows * width * width, 20e6),
        name="attention_forward",
    )(slen, llen, pos, xs, xl, *pieces)


HBM = pl.BlockSpec(memory_space=pl.ANY)
ON_CHIP = pl.BlockSpec(memory_space=pltpu.VMEM)
SCALARS = pl.BlockSpec(memory_space=pltpu.SMEM)


class Copies:
    def __init__(self, sems):
        self.sems, self.used, self.open = sems, 0, []

    def start(self, source, target):
        copy = pltpu.make_async_copy(source, target, self.sems.at[self.used])
        self.used += 1
        copy.start()
        return copy

    def send(self, source, target):
        self.open.append(self.start(source, target))

    def finish(self):
        for copy in self.open:
            copy.wait()


def feed_body(
    dims, slen, llen, pos, unit1, cot_s, cot_l, inv1, ub, vecs, p0, p1, p2, p3, p4, p5, p6, p7,
    keep, give, outs_o, outl_o, gfs_o, gatt_o, sums_o, dub_o,
    wup, wdown, unit_v, cot_v, low_v, low_t, hidden, gelu_v, grad_v, gffn, out_v, gatt, valid_v,
    keep_dv, give_dv, keep_uv, give_uv, sems, piece_sems, down_sems, up_sems,
):
    short_rows = dims[0]
    rows, width = low_v.shape
    parts, block = hidden.shape[0], hidden.shape[2]
    each, tall = width // SHARDS, block * parts // SHARDS
    owners, lanes, tile = SHARDS // parts, 256, 128
    copies = Copies(sems)
    pieces = (p0, p1, p2, p3, p4, p5, p6, p7)
    unit_here = copies.start(unit1, unit_v)
    groups = [[], [], []]
    for other in range(2):
        for k in range(RING):
            for i in range(RING):
                n = (other * RING + k) * RING + i
                at = gathered_at(pos, other, k, i)
                source = pieces[other * RING + k]
                half = parts // 2
                targets = (wup.at[:half, at], wup.at[half:, at], wdown.at[at])
                sources = (source.at[i, :half], source.at[i, half:parts], source.at[i, parts:])
                for group, sem, src, target in zip(groups, range(3), sources, targets):
                    group.append(pltpu.make_async_copy(src, target, piece_sems.at[sem, n]))
    for copy in groups[0]:
        copy.start()
    valid_v[...] = valid_rows(slen, llen, dims)
    grad_v[...] = jnp.zeros_like(grad_v)
    unit_here.wait()

    @pl.loop(0, rows // tile)
    def _(r):
        at = pl.ds(pl.multiple_of(r * tile, tile), tile)
        low_v[at] = (unit_v[at] * row_of(vecs, G1) + row_of(vecs, S1)).astype(BF16)

    @pl.loop(0, parts)
    def _(j):
        for n in range(2):

            @pl.when(j == n * (parts // 2))
            def _():
                for copy in groups[n]:
                    copy.wait()
                for copy in groups[n + 1]:
                    copy.start()

        bias = ub[:, pl.ds(pl.multiple_of(j * block, block), block)].astype(F32)
        pre = nn(low_v[...], wup[j].reshape(width, block)) + bias
        cdf = 0.5 + 0.5 * lax.erf(pre * (0.5**0.5))
        density = jnp.exp(-0.5 * pre * pre) * (0.5 / jnp.pi) ** 0.5
        hidden[j] = (pre * cdf).astype(BF16)
        gelu_v[j] = (cdf + pre * density).astype(BF16)

    for copy in groups[2]:
        copy.wait()
    cots_here = copies.start(cot_s, cot_v.at[:short_rows]), copies.start(cot_l, cot_v.at[short_rows:])

    @pl.loop(0, parts)
    def _(j):
        grad_v[...] += nn(hidden[j], wdown[pl.ds(j * owners, owners)].reshape(block, width))

    for copy in cots_here:
        copy.wait()
    sums_o[...] = jnp.zeros_like(sums_o)

    @pl.loop(0, rows // tile)
    def _(r):
        at = pl.ds(pl.multiple_of(r * tile, tile), tile)
        first = unit_v[at] * row_of(vecs, G1) + row_of(vecs, S1)
        unit, inverse = normalized(first + (grad_v[at] + row_of(vecs, DB)))
        valid = valid_v[at]
        out_v[at] = ((unit * row_of(vecs, G2) + row_of(vecs, S2)) * valid).astype(BF16)
        cot = cot_v[at].astype(F32) * valid
        back = norm_back(cot * row_of(vecs, G2), unit, inverse)
        grad_v[at] = back
        low_back = back.astype(BF16)
        gffn[at] = low_back
        sums_o[DB : DB + 1] += jnp.sum(low_back.astype(F32), axis=0, keepdims=True)
        sums_o[G2 : G2 + 1] += jnp.sum(cot * unit, axis=0, keepdims=True)
        sums_o[S2 : S2 + 1] += jnp.sum(cot, axis=0, keepdims=True)

    copies.send(out_v.at[:short_rows], outs_o)
    copies.send(out_v.at[short_rows:], outl_o)
    on_first = pos[2] == 0

    def down_copies(at, p0, p1):
        return (
            pltpu.make_async_copy(keep_dv.at[at], keep.at[jnp.where(on_first, p0, p1), :parts], down_sems.at[0, at]),
            pltpu.make_async_copy(give_dv.at[at], give.at[jnp.where(on_first, p1, p0), :parts], down_sems.at[1, at]),
        )

    @pl.loop(0, RING)
    def _(x):
        grad = tn(hidden[x], gffn[...]).astype(BF16)
        for z in range(RING):
            place = x * RING + z
            even, odd = grad[2 * z * tall : (2 * z + 1) * tall], grad[(2 * z + 1) * tall : (2 * z + 2) * tall]
            keep_dv[place] = jnp.where(on_first, even, odd).reshape(parts, each, width)
            give_dv[place] = jnp.where(on_first, odd, even).reshape(parts, each, width)
            for copy in down_copies(place, *places(pos, x, z)):
                copy.start()

    def up_copies(j):
        return (
            pltpu.make_async_copy(keep_uv.at[j], keep.at[:, parts + j], up_sems.at[0, j]),
            pltpu.make_async_copy(give_uv.at[j], give.at[:, parts + j], up_sems.at[1, j]),
        )

    low_t[:width] = low_v[...].T
    low_t[width:] = jnp.ones((16, rows), BF16)

    @pl.loop(0, parts)
    def _(j):
        weight = wdown[pl.ds(j * owners, owners)].reshape(block, width)
        up = (nt(gffn[...], weight) * gelu_v[j].astype(F32)).astype(BF16)
        hidden[j] = up
        grad = nn(low_t[...], hidden[j])
        dub_o[:, pl.ds(pl.multiple_of(j * block, block), block)] = grad[width : width + 1]
        deal(keep_uv.at[j], give_uv.at[j], pos, grad[:width].astype(BF16), slice(None), each)
        for copy in up_copies(j):
            copy.start()

    @pl.loop(0, parts)
    def _(j):
        grad_v[...] += nt(hidden[j], wup[j].reshape(width, block))

    @pl.loop(0, rows // tile)
    def _(r):
        at = pl.ds(pl.multiple_of(r * tile, tile), tile)
        grad, unit = grad_v[at], unit_v[at]
        back = norm_back(grad * row_of(vecs, G1), unit, inv1[at])
        grad_v[at] = back
        low_back = back.astype(BF16)
        gatt[at] = low_back
        sums_o[OB : OB + 1] += jnp.sum(low_back.astype(F32), axis=0, keepdims=True)
        sums_o[G1 : G1 + 1] += jnp.sum(grad * unit, axis=0, keepdims=True)
        sums_o[S1 : S1 + 1] += jnp.sum(grad, axis=0, keepdims=True)

    copies.send(gatt, gatt_o)
    copies.send(grad_v, gfs_o)
    for at in range(CHIPS):
        for copy in down_copies(at, at, at):
            copy.wait()
    for j in range(parts):
        for copy in up_copies(j):
            copy.wait()
    copies.finish()


def feed(slen, llen, pos, unit1, cot_s, cot_l, inv1, ub, vecs, pieces, dims):
    rows, width = unit1.shape
    inner = ub.shape[1]
    parts = RING
    block, tall, each = inner // parts, inner // SHARDS, width // SHARDS
    down, up = (CHIPS, parts, each, width), (parts, CHIPS, each, width)
    return pl.pallas_call(
        functools.partial(feed_body, dims),
        in_specs=[SCALARS] * 3 + [HBM] * 3 + [ON_CHIP] * 3 + [HBM] * 8,
        out_specs=[HBM] * 6 + [ON_CHIP] * 2,
        scratch_shapes=[
            pltpu.VMEM((parts, SHARDS, each, width), BF16), pltpu.VMEM((SHARDS, parts, each, width), BF16),
            pltpu.VMEM((rows, width), F32), pltpu.VMEM((rows, width), BF16), pltpu.VMEM((rows, width), BF16),
            pltpu.VMEM((width + 16, rows), BF16), pltpu.VMEM((parts, rows, block), BF16),
            pltpu.VMEM((parts, rows, block), BF16), pltpu.VMEM((rows, width), F32), pltpu.VMEM((rows, width), BF16),
            pltpu.VMEM((rows, width), BF16), pltpu.VMEM((rows, width), BF16), pltpu.VMEM((rows, 1), F32),
            pltpu.VMEM(down, BF16), pltpu.VMEM(down, BF16), pltpu.VMEM(up, BF16), pltpu.VMEM(up, BF16),
            pltpu.SemaphoreType.DMA((8,)), pltpu.SemaphoreType.DMA((3, SHARDS)),
            pltpu.SemaphoreType.DMA((2, CHIPS)), pltpu.SemaphoreType.DMA((2, parts)),
        ],
        out_shape=[
            *[jax.ShapeDtypeStruct((CHIPS, 2 * parts, each, width), BF16)] * 2,
            jax.ShapeDtypeStruct(cot_s.shape, BF16),
            jax.ShapeDtypeStruct(cot_l.shape, BF16),
            jax.ShapeDtypeStruct((rows, width), F32),
            jax.ShapeDtypeStruct((rows, width), BF16),
            jax.ShapeDtypeStruct((8, width), F32),
            jax.ShapeDtypeStruct((1, inner), F32),
        ],
        compiler_params=params(58),
        cost_estimate=cost(12 * rows * width * inner, 30e6),
        name="feed",
    )(slen, llen, pos, unit1, cot_s, cot_l, inv1, ub, vecs, *pieces)


def attention_back_body(dims, gatt, wo_block, q, k, v, ps, plong, dq_o, dk_o, dv_o, gc, wo_all):
    step = pl.program_id(0)
    width, cols = gatt.shape[1], q.shape[1]
    at_cols = pl.ds(pl.multiple_of(step * cols, cols), cols)

    @pl.when(step == 0)
    def _():
        wo_all[...] = wo_block[...].reshape(width, width)

    gc[...] = nt(gatt[...], wo_all[at_cols, :]).astype(BF16)
    scale = HEAD_DIM**-0.5
    for first, rows, long_at in segments(dims):
        at = slice(first, first + rows)
        for pair in range(cols // PAIR):
            lanes = slice(pair * PAIR, (pair + 1) * PAIR)
            probs = ps[pair] if long_at is None else plong[long_at, pair]
            grad = gc[at, lanes]
            dp = nt(two_heads(v[at, lanes]), grad)
            ds = []
            for h in range(2):
                half = slice(h * rows, (h + 1) * rows)
                p = probs[half].astype(F32)
                d = dp[half]
                ds.append((p * (d - jnp.sum(d * p, axis=0, keepdims=True))).astype(BF16))
            ds = jnp.concatenate(ds, axis=0)
            dv_o[at, lanes] = own_lanes(nn(probs, grad)).astype(BF16)
            dk_o[at, lanes] = (own_lanes(nn(ds, q[at, lanes])) * scale).astype(BF16)
            dq_o[at, lanes] = (tn(ds, two_heads(k[at, lanes])) * scale).astype(BF16)


def attention_back(gatt, gathered, q, k, v, ps, plong, dims):
    rows, width = gatt.shape
    short_rows, long_count, long_length, _ = dims
    step = 256
    per = step // PAIR
    cols = pl.BlockSpec((rows, step), lambda g: (0, g))
    return pl.pallas_call(
        functools.partial(attention_back_body, dims),
        grid=(width // step,),
        in_specs=[
            whole(rows, width),
            pl.BlockSpec((SHARDS, width // SHARDS, width), lambda g: (0, 3, 0)),
            cols, cols, cols,
            pl.BlockSpec((per, 2 * short_rows, short_rows), lambda g: (g, 0, 0)),
            pl.BlockSpec((long_count, per, 2 * long_length, long_length), lambda g: (0, g, 0, 0)),
        ],
        out_specs=[cols, cols, cols],
        scratch_shapes=[pltpu.VMEM((rows, step), BF16), pltpu.VMEM((width, width), BF16)],
        out_shape=[jax.ShapeDtypeStruct((rows, width), BF16)] * 3,
        compiler_params=params(BACK_MIB),
        cost_estimate=cost(8 * rows * width * width, 15e6),
        name="attention_back",
    )(gatt, gathered, q, k, v, ps, plong)


def weight_back_body(
    dims, pos, gatt_cols, c, dq, dk, dv, xs, xl, sums_f, dub,
    keep, give,
    x_t, c_t, sums,
):
    step = pl.program_id(0)
    short_rows = dims[0]
    rows, width = c.shape
    cols = dq.shape[1]
    each = width // SHARDS
    at_cols = pl.ds(pl.multiple_of(step * cols, cols), cols)

    @pl.when(step == 0)
    def _():
        x_t[:width, :short_rows] = xs[...].T
        x_t[:width, short_rows:] = xl[...].T
        x_t[width:] = jnp.ones((16, rows), BF16)
        c_t[...] = c[...].T
        sums[...] = sums_f[...]

    deal(keep, give, pos, nn(c_t[...], gatt_cols[...]).astype(BF16), slice(3 * each, 4 * each), each)
    for i, d in enumerate((dq, dk, dv)):
        grad = nn(x_t[...], d[...])
        deal(keep, give, pos, grad[:width].astype(BF16), slice(i * each, (i + 1) * each), each)
        if i != 1:
            at = QB if i == 0 else VB
            sums[at : at + 1, at_cols] = grad[width : width + 1]
    keep[:, 4 * each :] = jnp.zeros((CHIPS, 8, cols), BF16)
    give[:, 4 * each :] = jnp.zeros((CHIPS, 8, cols), BF16)

    @pl.when(step == pl.num_programs(0) - 1)
    def _():
        mine = spread(SHARDS, width)
        rest = column_rest(cols, width, each)
        line = jnp.zeros((SHARDS, cols), F32)
        for i in range(8):
            put = (iota(rest.shape, 0) == rest + i * each).astype(BF16)
            line += nt(jnp.where(mine, sums[i : i + 1], 0.0).astype(BF16), put)
        inner = dub.shape[1]
        put = (iota((cols, inner), 0) == column_rest(cols, inner, inner // SHARDS)).astype(BF16)
        wide = nt(jnp.where(spread(SHARDS, inner), dub[...], 0.0).astype(BF16), put)
        both = jnp.concatenate([line[:, None], wide[:, None], jnp.zeros((SHARDS, 6, cols), F32)], axis=1)
        deal(keep, give, pos, both.reshape(SHARDS * 8, cols).astype(BF16), slice(4 * each, 4 * each + 8), 8)


def weight_back(pos, gatt, c, dq, dk, dv, xs, xl, sums_f, dub, dims):
    rows, width = gatt.shape
    each = width // SHARDS
    step = 256
    cols = pl.BlockSpec((rows, step), lambda g, *_: (0, g))
    dealt = pl.BlockSpec((CHIPS, 4 * each + 8, step), lambda g, *_: (0, 0, g))
    return pl.pallas_call(
        functools.partial(weight_back_body, dims),
        grid_spec=pltpu.PrefetchScalarGridSpec(
            num_scalar_prefetch=1,
            grid=(width // step,),
            in_specs=[
                cols, whole(rows, width), cols, cols, cols,
                whole(*xs.shape), whole(*xl.shape), whole(8, width), whole(*dub.shape),
            ],
            out_specs=[dealt, dealt],
            scratch_shapes=[
                pltpu.VMEM((width + 16, rows), BF16), pltpu.VMEM((width, rows), BF16), pltpu.VMEM((8, width), F32),
            ],
        ),
        out_shape=[jax.ShapeDtypeStruct((CHIPS, 4 * each + 8, width), BF16)] * 2,
        compiler_params=params(BACK_MIB),
        cost_estimate=cost(8 * rows * width * width, 12e6),
        name="weight_back",
    )(pos, gatt, c, dq, dk, dv, xs, xl, sums_f, dub)


def input_back_body(dims, gfs, dq, dk, dv, wq, wk, wv, gs_o, gl_o, total):
    step = pl.program_id(0)
    short_rows, width, cols = dims[0], gfs.shape[1], dq.shape[1]
    part = (
        nt(dq[...], wq[...].reshape(width, cols))
        + nt(dk[...], wk[...].reshape(width, cols))
        + nt(dv[...], wv[...].reshape(width, cols))
    )

    @pl.when(step == 0)
    def _():
        total[...] = gfs[...] + part

    @pl.when(step > 0)
    def _():
        total[...] += part

    @pl.when(step == pl.num_programs(0) - 1)
    def _():
        gs_o[...] = total[:short_rows]
        gl_o[...] = total[short_rows:]


def input_back(gfs, dq, dk, dv, gathered, dims):
    rows, width = gfs.shape
    each = width // SHARDS
    step = 256
    short_rows = dims[0]
    cols = pl.BlockSpec((rows, step), lambda g: (0, g))
    slab = lambda i: pl.BlockSpec((SHARDS, each, step), lambda g: (0, i, g))
    return pl.pallas_call(
        functools.partial(input_back_body, dims),
        grid=(width // step,),
        in_specs=[whole(rows, width), cols, cols, cols, slab(0), slab(1), slab(2)],
        out_specs=[whole(short_rows, width), whole(rows - short_rows, width)],
        scratch_shapes=[pltpu.VMEM((rows, width), F32)],
        out_shape=[
            jax.ShapeDtypeStruct((short_rows, width), F32),
            jax.ShapeDtypeStruct((rows - short_rows, width), F32),
        ],
        compiler_params=params(16),
        cost_estimate=cost(6 * rows * width * width, 12e6),
        name="input_back",
    )(gfs, dq, dk, dv, gathered, gathered, gathered)


def pair_sum(keep, got):
    parts = []
    for d in range(RING):
        at = slice(d * RING, (d + 1) * RING)
        parts.append((keep[at].astype(F32) + got[at].astype(F32)).astype(BF16))
    return parts


def four_sum(own, left, right, far):
    return (own.astype(F32) + far.astype(F32)) + (left.astype(F32) + right.astype(F32))


def turn(delta, stage):
    moves = []
    for x in range(RING):
        for z in range(RING):
            for core in range(2):
                to_x, to_z = x, z
                if (core == 0) == (stage == 0):
                    to_x = (x + delta) % RING
                else:
                    to_z = (z + delta) % RING
                moves.append(((x * RING + z) * 2 + core, (to_x * RING + to_z) * 2 + core))
    return moves


def swap_cores(v):
    return lax.ppermute(v, "shard", [(i, i ^ 1) for i in range(SHARDS)])


def around(v, stage):
    return tuple(lax.ppermute(v[d] if isinstance(v, (list, tuple)) else v, "shard", turn(d, stage)) for d in (1, 3, 2))


def both_cores(pieces):
    return (*pieces, *(swap_cores(p) for p in pieces))


def second_turn(own, left, right, far):
    parts = [four_sum(own[d], left[d], right[d], far[d]).astype(BF16) for d in range(RING)]
    own = four_sum(parts[0], *around(parts, 1)).astype(BF16)
    return own, *(lax.ppermute(own, "rep", [(i, (i + d) % RING) for i in range(RING)]) for d in (1, 3, 2))


def replica_sum(own, left, right, far, at):
    return (own[at].astype(F32) + far[at].astype(F32)) + (left[at].astype(F32) + right[at].astype(F32))


def finish_attention_body(own, left, right, far, wqkv_o, wo_o, *vector_os):
    each, width = wo_o.shape
    for j in range(wqkv_o.shape[1] // width):
        at = slice(j * each, (j + 1) * each)
        wqkv_o[:, j * width : (j + 1) * width] = replica_sum(own, left, right, far, at)
    wo_o[...] = replica_sum(own, left, right, far, slice(3 * each, 4 * each))
    last = replica_sum(own, left, right, far, slice(4 * each, 4 * each + 8))[:, width - 256 :]
    for i, o in enumerate(vector_os[:-1]):
        o[...] = last[0:1, i * each : (i + 1) * each]
    o = vector_os[-1]
    o[...] = last[1:2, : o.shape[1]]


def finish_attention(arrays, tall):
    width = arrays[0].shape[1]
    each = width // SHARDS
    return pl.pallas_call(
        finish_attention_body,
        out_shape=[
            jax.ShapeDtypeStruct((each, 3 * width), F32),
            jax.ShapeDtypeStruct((each, width), F32),
            *[jax.ShapeDtypeStruct((1, each), F32)] * 8,
            jax.ShapeDtypeStruct((1, tall), F32),
        ],
        compiler_params=params(4),
        name="finish_attention",
    )(*arrays)


def finish_feed_body(own, left, right, far, up_o, down_o):
    parts = own.shape[0] // 2
    each, width = own.shape[1:]
    for j in range(parts):
        down_o[j * each : (j + 1) * each] = replica_sum(own, left, right, far, j)
        up_o[:, j * width : (j + 1) * width] = replica_sum(own, left, right, far, parts + j)


def finish_feed(arrays, each, inner, tall):
    width = arrays[0].shape[2]
    return pl.pallas_call(
        finish_feed_body,
        out_shape=[jax.ShapeDtypeStruct((each, inner), F32), jax.ShapeDtypeStruct((tall, width), F32)],
        compiler_params=params(4),
        name="finish_feed",
    )(*arrays)


def on_device(
    short_tokens, long_tokens, short_lengths, long_lengths, short_cotangent, long_cotangent,
    input_weight, query_bias, value_bias, output_weight, output_bias, first_gain, first_shift,
    up_weight, up_bias, down_weight, down_bias, second_gain, second_shift,
):
    short_count, short_length, width = short_tokens.shape
    long_count, long_length, _ = long_tokens.shape
    dims = (short_count * short_length, long_count, long_length, short_length)
    each, inner, tall = width // SHARDS, up_weight.shape[1], down_weight.shape[0]
    xs, xl = short_tokens.reshape(-1, width), long_tokens.reshape(-1, width)
    cs, cl = short_cotangent.reshape(-1, width), long_cotangent.reshape(-1, width)
    index = lax.axis_index("shard")
    pos = jnp.stack([index // 8, (index // 2) % 4, index % 2]).astype(jnp.int32)

    packed = pack(
        input_weight, output_weight, up_weight, down_weight,
        (query_bias, value_bias, output_bias, first_gain, first_shift, down_bias, second_gain, second_shift),
        up_bias,
    )
    near = (packed, *around(packed, 1))
    cut = 4 * each + 8
    near_a = jnp.stack([n[:cut] for n in near])
    near_f = jnp.stack([n[cut:].reshape(-1, each, width) for n in near])
    around_a = around(near_a, 0)
    far_f = around(near_f, 0)
    pieces_a = both_cores((near_a, *around_a))
    xs, near_f = lax.optimization_barrier((xs, near_f))
    q, k, v, c, ps, plong, unit1, inv1, vecs, ub, gathered_a = attention_forward(
        short_lengths, long_lengths, pos, xs, xl, pieces_a, inner, dims
    )
    unit1, *far_f = lax.optimization_barrier((unit1, *far_f))
    keep_f, give_f, out_s, out_l, gfs, gatt, sums_f, dub = feed(
        short_lengths, long_lengths, pos, unit1, cs, cl, inv1, ub, vecs, both_cores((near_f, *far_f)), dims
    )
    dq, dk, dv = attention_back(gatt, gathered_a, q, k, v, ps, plong, dims)
    parts_f = pair_sum(keep_f, swap_cores(give_f))
    dv, *parts_f = lax.optimization_barrier((dv, *parts_f))
    around_f = around(parts_f, 0)
    keep_a, give_a = weight_back(pos, gatt, c, dq, dk, dv, xs, xl, sums_f, dub, dims)
    parts_a = pair_sum(keep_a, swap_cores(give_a))
    gfs, *parts_a = lax.optimization_barrier((gfs, *parts_a))
    around_a = around(parts_a, 0)
    grad_s, grad_l = input_back(gfs, dq, dk, dv, gathered_a, dims)
    grad_s, *around_a = lax.optimization_barrier((grad_s, *around_a))
    up, down = finish_feed(second_turn(parts_f[0], *around_f), each, inner, tall)
    w_in, w_out, *vectors = finish_attention(second_turn(parts_a[0], *around_a), tall)
    vectors = [x.reshape(-1) for x in vectors]
    return (
        out_s.reshape(short_tokens.shape), out_l.reshape(long_tokens.shape),
        grad_s.reshape(short_tokens.shape), grad_l.reshape(long_tokens.shape),
        w_in, vectors[QB], vectors[VB], w_out, vectors[OB], vectors[G1], vectors[S1],
        up, vectors[8], down, vectors[DB], vectors[G2], vectors[S2],
    )


def solution(mesh):
    rows, flat = P(("rep", "shard"), None, None), P("shard")
    tall = P("shard", None)
    return jax.shard_map(
        on_device,
        mesh=mesh,
        in_specs=(
            rows, rows, P(("rep", "shard")), P(("rep", "shard")), rows, rows,
            tall, flat, flat, tall, flat, flat, flat, tall, flat, tall, flat, flat, flat,
        ),
        out_specs=(
            rows, rows, rows, rows,
            tall, flat, flat, tall, flat, flat, flat, tall, flat, tall, flat, flat, flat,
        ),
        check_vma=False,
    )
```

profile of v0, /device:TPU:0, one launch (start us, length us, event | category | flops | bytes accessed | tf_op | source)
XLA Modules:
  0.0 215.2 jit_solution(3171278470883771920)
XLA Ops:
  0.7 2.0 pack.1
  2.7 4.0 %collective-permute-start.2 = (bf16[296,768]{1,0:T(8,128)(2,1)}, bf16[296,768]{1,0:T(8,128)(2,1)S(1)}, u32[]{:S(2)}, u32[]{:S(2)}) collective-permute-start(bf16[296,768]{1,0:T(8,128)(2,1)} %pack.1), channel_id=1, source_target_pairs={{0,4},{1,17},{2,6},{3,19},{4,0},{5,21},{6,2},{7,23},{8,12},{9,25},... | collective-permute-start | bytes 1363976 | tf_op jit(solution)/shard_map/ppermute | solution.py:723
  6.6 0.7 collective-permute-start.1
  7.3 1.3 collective-permute-start
  8.7 1.0 slice_bitcast_fusion.3
  9.6 3.7 %collective-permute-done.2 = bf16[296,768]{1,0:T(8,128)(2,1)S(1)} collective-permute-done((bf16[296,768]{1,0:T(8,128)(2,1)}, bf16[296,768]{1,0:T(8,128)(2,1)S(1)}, u32[]{:S(2)}, u32[]{:S(2)}) %collective-permute-start.2) | collective-permute-done | bytes 454688 | tf_op jit(solution)/shard_map/ppermute | solution.py:723
  13.4 5.8 %collective-permute-done.1 = bf16[296,768]{1,0:T(8,128)(2,1)S(1)} collective-permute-done((bf16[296,768]{1,0:T(8,128)(2,1)}, bf16[296,768]{1,0:T(8,128)(2,1)S(1)}, u32[]{:S(2)}, u32[]{:S(2)}) %collective-permute-start.1) | collective-permute-done | bytes 454688 | tf_op jit(solution)/shard_map/ppermute | solution.py:723
  19.3 3.1 %collective-permute-start.5 = (bf16[4,104,768]{2,1,0:T(8,128)(2,1)S(1)}, bf16[4,104,768]{2,1,0:T(8,128)(2,1)S(1)}, u32[]{:S(2)}, u32[]{:S(2)}) collective-permute-start(bf16[4,104,768]{2,1,0:T(8,128)(2,1)S(1)} %pad_maximum_fusion.1.p0), channel_id=1, source_target_pairs={{0,16},{1,5},{2,18},{3,7},{4,20},{5,1},{6,22},{7,3},{8,24},{9,13},... | collective-permute-start | bytes 1916936 | tf_op jit(solution)/shard_map/ppermute | solution.py:723
  22.4 1.1 collective-permute-start.4
  23.6 0.9 collective-permute-start.3
  24.5 7.0 %collective-permute-done.5.p3 = bf16[4,104,768]{2,1,0:T(8,128)(2,1)S(1)} collective-permute-done((bf16[4,104,768]{2,1,0:T(8,128)(2,1)S(1)}, bf16[4,104,768]{2,1,0:T(8,128)(2,1)S(1)}, u32[]{:S(2)}, u32[]{:S(2)}) %collective-permute-start.5) | collective-permute-done | bytes 639008 | tf_op jit(solution)/shard_map/ppermute | solution.py:723
  31.6 0.7 copy-done.16
  32.3 0.4 slice-done.4
  32.8 3.1 %collective-permute-start.12 = (bf16[4,8,24,768]{3,2,1,0:T(8,128)(2,1)S(1)}, bf16[4,8,24,768]{3,2,1,0:T(8,128)(2,1)S(1)}, u32[]{:S(2)}, u32[]{:S(2)}) collective-permute-start(bf16[4,8,24,768]{3,2,1,0:T(8,128)(2,1)S(1)} %pad_maximum_fusion.p0), channel_id=1, source_target_pairs={{0,16},{1,5},{2,18},{3,7},{4,20},{5,1},{6,22},{7,3},{8,24},{9,13},... | collective-permute-start | bytes 3538952 | tf_op jit(solution)/shard_map/ppermute | solution.py:723
  35.9 1.1 collective-permute-start.11
  37.1 1.4 collective-permute-done.4.p2
  38.4 1.4 collective-permute-start.10
  39.8 0.6 collective-permute-start.7
  40.6 0.6 pad_add_fusion.pos
  41.2 0.8 collective-permute-done.8.p6
  42.2 0.9 collective-permute-done.7.p5
  43.1 19.0 %attention_forward.1 = (bf16[640,768]{1,0:T(8,128)(2,1)}, bf16[640,768]{1,0:T(8,128)(2,1)}, bf16[640,768]{1,0:T(8,128)(2,1)}, bf16[640,768]{1,0:T(8,128)(2,1)}, ...) custom-call(s32[2]{0:T(128)} %slen.3, s32[2]{0:T(128)} %llen.3, ...), custom_call_target="tpu_custom_call" | custom-call | flops 3019898880 | bytes 20000000 | tf_op jit(solution)/shard_map/attention_forward/pallas_call | solution.py:273
  62.1 1.6 collective-permute-done.11.p2
  63.7 0.5 collective-permute-start.15
  64.3 2.5 %collective-permute-done.14.p5 = bf16[4,8,24,768]{3,2,1,0:T(8,128)(2,1)S(1)} collective-permute-done((bf16[4,8,24,768]{3,2,1,0:T(8,128)(2,1)}, bf16[4,8,24,768]{3,2,1,0:T(8,128)(2,1)S(1)}, u32[]{:S(2)}, u32[]{:S(2)}) %collective-permute-start.14) | collective-permute-done | bytes 1179680 | tf_op jit(solution)/shard_map/ppermute | solution.py:719
  66.8 3.4 %collective-permute-done.15.p6 = bf16[4,8,24,768]{3,2,1,0:T(8,128)(2,1)S(1)} collective-permute-done((bf16[4,8,24,768]{3,2,1,0:T(8,128)(2,1)}, bf16[4,8,24,768]{3,2,1,0:T(8,128)(2,1)S(1)}, u32[]{:S(2)}, u32[]{:S(2)}) %collective-permute-start.15) | collective-permute-done | bytes 1179680 | tf_op jit(solution)/shard_map/ppermute | solution.py:719
  70.2 1.0 copy-done.14
  71.2 1.0 copy-done.15
  72.2 37.2 %feed.1 = (bf16[16,8,24,768]{3,2,1,0:T(8,128)(2,1)}, bf16[16,8,24,768]{3,2,1,0:T(8,128)(2,1)}, bf16[128,768]{1,0:T(8,128)(2,1)}, bf16[512,768]{1,0:T(8,128)(2,1)...) custom-call(s32[2]{0:T(128)} %slen.3, s32[2]{0:T(128)} %llen.3, ...), custom_call_target="tpu_custom_call" | custom-call | flops 18119393280 | bytes 30000000 | tf_op jit(solution)/shard_map/feed/pallas_call | solution.py:490
  109.4 0.4 collective-permute-start.17
  109.9 11.8 %attention_back.1 = (bf16[640,768]{1,0:T(8,128)(2,1)}, bf16[640,768]{1,0:T(8,128)(2,1)}, bf16[640,768]{1,0:T(8,128)(2,1)}) custom-call(bf16[640,768]{1,0:T(8,128)(2,1)} %get-tuple-element.89.gatt.gatt_cols, bf16[32,104,768]{2,1,0:T(8,128)(2,1)} %get-tuple-element.91.wo_block.wq.wk.wv, bf16[640,768]{1,0:T(8,128)(2,1)} %get-tuple-element.92.q, ...), custom_call_target="tpu_custom_call" | custom-call | flops 3019898880 | bytes 15000000 | tf_op jit(solution)/shard_map/attention_back/pallas_call | solution.py:555
  121.8 3.9 %add_convert_fusion = (bf16[4,8,24,768]{3,2,1,0:T(8,128)(2,1)}, bf16[4,8,24,768]{3,2,1,0:T(8,128)(2,1)}, bf16[4,8,24,768]{3,2,1,0:T(8,128)(2,1)}, bf16[4,8,24,768]{3,2,1,0:T(8,128)(2,1)S(1)}) fusion(bf16[16,8,24,768]{3,2,1,0:T(8,128)(2,1)} %collective-permute-done.17, bf16[16,8,24,768]{3,2,1,0:T(8,128)(2,1)S(1)} %bitcast.66), kind=kLoop, calls=%fused_computation | loop fusion | flops 9437184 | bytes 14155776 | tf_op jit(solution)/shard_map/convert_element_type | solution.py:696
  125.7 11.4 %weight_back.1 = (bf16[16,104,768]{2,1,0:T(8,128)(2,1)}, bf16[16,104,768]{2,1,0:T(8,128)(2,1)}) custom-call(s32[3]{0:T(128)} %pad_add_fusion.pos, bf16[640,768]{1,0:T(8,128)(2,1)} %get-tuple-element.89.gatt.gatt_cols, bf16[640,768]{1,0:T(8,128)(2,1)} %get-tuple-element.90.c, bf16[640,768]{1,0:T(8,128)(2,1)} %get-tuple-element.97.dq, ...), custom_call_target="tpu_custom_call" | custom-call | flops 3019898880 | bytes 12000000 | tf_op jit(solution)/shard_map/weight_back/pallas_call | solution.py:625
  137.1 0.4 collective-permute-start.18
  137.5 2.9 %collective-permute-start.28 = (bf16[4,8,24,768]{3,2,1,0:T(8,128)(2,1)S(1)}, bf16[4,8,24,768]{3,2,1,0:T(8,128)(2,1)S(1)}, u32[]{:S(2)}, u32[]{:S(2)}) collective-permute-start(bf16[4,8,24,768]{3,2,1,0:T(8,128)(2,1)S(1)} %copy-done.7), channel_id=1, source_target_pairs={{0,16},{1,5},{2,18},{3,7},{4,20},{5,1},{6,22},{7,3},{8,24},{9,13},... | collective-permute-start | bytes 3538952 | tf_op jit(solution)/shard_map/ppermute | solution.py:723
  140.4 0.6 collective-permute-start.29
  141.0 2.6 %collective-permute-start.30 = (bf16[4,8,24,768]{3,2,1,0:T(8,128)(2,1)S(1)}, bf16[4,8,24,768]{3,2,1,0:T(8,128)(2,1)S(1)}, u32[]{:S(2)}, u32[]{:S(2)}) collective-permute-start(bf16[4,8,24,768]{3,2,1,0:T(8,128)(2,1)S(1)} %copy-done.5), channel_id=1, source_target_pairs={{0,24},{1,7},{2,26},{3,1},{4,28},{5,3},{6,30},{7,5},{8,0},{9,15},{... | collective-permute-start | bytes 3538952 | tf_op jit(solution)/shard_map/ppermute | solution.py:723
  143.6 2.4 %add_convert_fusion.4 = (bf16[4,104,768]{2,1,0:T(8,128)(2,1)S(1)}, bf16[4,104,768]{2,1,0:T(8,128)(2,1)S(1)}, bf16[4,104,768]{2,1,0:T(8,128)(2,1)S(1)}, bf16[4,104,768]{2,1,0:T(8,128)(2,1)S(1)}) fusion(bf16[16,104,768]{2,1,0:T(8,128)(2,1)S(1)} %collective-permute-done.18, bf16[16,104,768]{2,1,0:T(8,128)(2,1)} %get-tuple-element.105), kind=kLoop, calls=%fused_computation.4 | loop fusion | flops 5111808 | bytes 7667712 | tf_op jit(solution)/shard_map/convert_element_type | solution.py:696
  146.1 3.2 %collective-permute-start.20 = (bf16[4,104,768]{2,1,0:T(8,128)(2,1)S(1)}, bf16[4,104,768]{2,1,0:T(8,128)(2,1)S(1)}, u32[]{:S(2)}, u32[]{:S(2)}) collective-permute-start(bf16[4,104,768]{2,1,0:T(8,128)(2,1)S(1)} %get-tuple-element.110), channel_id=1, source_target_pairs={{0,24},{1,7},{2,26},{3,1},{4,28},{5,3},{6,30},{7,5},{8,0},{9,15},{... | collective-permute-start | bytes 1916936 | tf_op jit(solution)/shard_map/ppermute | solution.py:723
  149.4 5.9 %collective-permute-done.28 = bf16[4,8,24,768]{3,2,1,0:T(8,128)(2,1)S(1)} collective-permute-done((bf16[4,8,24,768]{3,2,1,0:T(8,128)(2,1)S(1)}, bf16[4,8,24,768]{3,2,1,0:T(8,128)(2,1)S(1)}, u32[]{:S(2)}, u32[]{:S(2)}) %collective-permute-start.28) | collective-permute-done | bytes 1179680 | tf_op jit(solution)/shard_map/ppermute | solution.py:723
  155.3 2.9 %collective-permute-start.21 = (bf16[4,104,768]{2,1,0:T(8,128)(2,1)S(1)}, bf16[4,104,768]{2,1,0:T(8,128)(2,1)S(1)}, u32[]{:S(2)}, u32[]{:S(2)}) collective-permute-start(bf16[4,104,768]{2,1,0:T(8,128)(2,1)S(1)} %get-tuple-element.111), channel_id=1, source_target_pairs={{0,16},{1,5},{2,18},{3,7},{4,20},{5,1},{6,22},{7,3},{8,24},{9,13},... | collective-permute-start | bytes 1916936 | tf_op jit(solution)/shard_map/ppermute | solution.py:723
  158.2 9.7 %collective-permute-done.29 = bf16[4,8,24,768]{3,2,1,0:T(8,128)(2,1)S(1)} collective-permute-done((bf16[4,8,24,768]{3,2,1,0:T(8,128)(2,1)S(1)}, bf16[4,8,24,768]{3,2,1,0:T(8,128)(2,1)S(1)}, u32[]{:S(2)}, u32[]{:S(2)}) %collective-permute-start.29) | collective-permute-done | bytes 1179680 | tf_op jit(solution)/shard_map/ppermute | solution.py:723
  167.8 0.4 fusion.5
  168.3 2.5 %collective-permute-start.31 = (bf16[8,24,768]{2,1,0:T(8,128)(2,1)S(1)}, bf16[8,24,768]{2,1,0:T(8,128)(2,1)S(1)}, u32[]{:S(2)}, u32[]{:S(2)}) collective-permute-start(bf16[8,24,768]{2,1,0:T(8,128)(2,1)S(1)} %get-tuple-element.143), channel_id=1, source_target_pairs={{0,4},{1,17},{2,6},{3,19},{4,0},{5,21},{6,2},{7,23},{8,12},{9,25},... | collective-permute-start | bytes 884744 | tf_op jit(solution)/shard_map/ppermute | solution.py:723
  170.8 1.2 collective-permute-start.33
  172.0 5.6 %collective-permute-done.19 = bf16[4,104,768]{2,1,0:T(8,128)(2,1)S(1)} collective-permute-done((bf16[4,104,768]{2,1,0:T(8,128)(2,1)S(1)}, bf16[4,104,768]{2,1,0:T(8,128)(2,1)S(1)}, u32[]{:S(2)}, u32[]{:S(2)}) %collective-permute-start.19) | collective-permute-done | bytes 639008 | tf_op jit(solution)/shard_map/ppermute | solution.py:723
  177.5 1.0 collective-permute-start.32
  178.5 5.5 %input_back.1 = (f32[128,768]{1,0:T(8,128)}, f32[512,768]{1,0:T(8,128)}) custom-call(f32[640,768]{1,0:T(8,128)S(1)} %copy-done, bf16[640,768]{1,0:T(8,128)(2,1)S(1)} %copy-done.1, bf16[640,768]{1,0:T(8,128)(2,1)S(1)} %copy-done.2, bf16[640,768]{1,0:T(8,128)(2,1)S(1)} %copy-done.3, bf16[32,104,768]{2,1,0:T(8,128)(2,1)S(1)} %bitcast.64, ...), custom_call_target="tpu_custom_call" | custom-call | flops 2264924160 | bytes 12000000 | tf_op jit(solution)/shard_map/input_back/pallas_call | solution.py:676
  184.0 3.9 %collective-permute-done.21 = bf16[4,104,768]{2,1,0:T(8,128)(2,1)S(1)} collective-permute-done((bf16[4,104,768]{2,1,0:T(8,128)(2,1)S(1)}, bf16[4,104,768]{2,1,0:T(8,128)(2,1)S(1)}, u32[]{:S(2)}, u32[]{:S(2)}) %collective-permute-start.21) | collective-permute-done | bytes 639008 | tf_op jit(solution)/shard_map/ppermute | solution.py:723
  188.1 2.5 %collective-permute-start.22 = (bf16[104,768]{1,0:T(8,128)(2,1)S(1)}, bf16[104,768]{1,0:T(8,128)(2,1)S(1)}, u32[]{:S(2)}, u32[]{:S(2)}) collective-permute-start(bf16[104,768]{1,0:T(8,128)(2,1)S(1)} %get-tuple-element.146), channel_id=1, source_target_pairs={{0,4},{1,17},{2,6},{3,19},{4,0},{5,21},{6,2},{7,23},{8,12},{9,25},... | collective-permute-start | bytes 479240 | tf_op jit(solution)/shard_map/ppermute | solution.py:723
  190.6 1.2 collective-permute-start.24
  191.8 0.8 collective-permute-start.23
  192.9 3.3 %collective-permute-start.36 = (bf16[8,24,768]{2,1,0:T(8,128)(2,1)S(1)}, bf16[8,24,768]{2,1,0:T(8,128)(2,1)S(1)}, u32[]{:S(2)}, u32[]{:S(2)}) collective-permute-start(bf16[8,24,768]{2,1,0:T(8,128)(2,1)S(1)} %fusion.1.own), channel_id=1, source_target_pairs={{0,64},{32,96},{64,0},{96,32},{1,65},{33,97},{65,1},{97,33},{2,66}... | collective-permute-start | bytes 884744 | tf_op jit(solution)/shard_map/ppermute | solution.py:733
  196.2 1.1 collective-permute-start.35
  197.3 1.0 collective-permute-start.34
  198.5 3.3 %collective-permute-start.27 = (bf16[104,768]{1,0:T(8,128)(2,1)S(1)}, bf16[104,768]{1,0:T(8,128)(2,1)S(1)}, u32[]{:S(2)}, u32[]{:S(2)}) collective-permute-start(bf16[104,768]{1,0:T(8,128)(2,1)S(1)} %fusion.3.own), channel_id=1, source_target_pairs={{0,64},{32,96},{64,0},{96,32},{1,65},{33,97},{65,1},{97,33},{2,66}... | collective-permute-start | bytes 479240 | tf_op jit(solution)/shard_map/ppermute | solution.py:733
  201.8 1.1 collective-permute-start.26
  202.8 1.8 collective-permute-done.36.far
  204.6 1.5 collective-permute-start.25
  206.1 4.9 %collective-permute-done.35.right = bf16[8,24,768]{2,1,0:T(8,128)(2,1)S(1)} collective-permute-done((bf16[8,24,768]{2,1,0:T(8,128)(2,1)S(1)}, bf16[8,24,768]{2,1,0:T(8,128)(2,1)S(1)}, u32[]{:S(2)}, u32[]{:S(2)}) %collective-permute-start.35) | collective-permute-done | bytes 294944 | tf_op jit(solution)/shard_map/ppermute | solution.py:733
  210.9 1.6 collective-permute-done.34.left
  212.5 0.9 finish_feed.1
  213.4 1.0 collective-permute-done.26.right
  214.4 0.8 finish_attention.1
  (86 shorter events, 1.7 us)
Async XLA Ops:
  2.7 10.7 %collective-permute-start.2 = (bf16[296,768]{1,0:T(8,128)(2,1)}, bf16[296,768]{1,0:T(8,128)(2,1)S(1)}, u32[]{:S(2)}, u32[]{:S(2)}) collective-permute-start(bf16[296,768]{1,0:T(8,128)(2,1)} %pack.1), channel_id=1, source_target_pairs={{0,4},{1,17},{2,6},{3,19},{4,0},{5,21},{6,2},{7,23},{8,12},{9,25},... | collective-permute-start | bytes 1363976 | tf_op jit(solution)/shard_map/ppermute | solution.py:723
  6.6 12.6 %collective-permute-start.1 = (bf16[296,768]{1,0:T(8,128)(2,1)}, bf16[296,768]{1,0:T(8,128)(2,1)S(1)}, u32[]{:S(2)}, u32[]{:S(2)}) collective-permute-start(bf16[296,768]{1,0:T(8,128)(2,1)} %pack.1), channel_id=1, source_target_pairs={{0,6},{1,25},{2,0},{3,27},{4,2},{5,29},{6,4},{7,31},{8,14},{9,1},{... | collective-permute-start | bytes 1363976 | tf_op jit(solution)/shard_map/ppermute | solution.py:723
  7.3 11.9 %collective-permute-start = (bf16[296,768]{1,0:T(8,128)(2,1)}, bf16[296,768]{1,0:T(8,128)(2,1)S(1)}, u32[]{:S(2)}, u32[]{:S(2)}) collective-permute-start(bf16[296,768]{1,0:T(8,128)(2,1)} %pack.1), channel_id=1, source_target_pairs={{0,2},{1,9},{2,4},{3,11},{4,6},{5,13},{6,0},{7,15},{8,10},{9,17},{... | collective-permute-start | bytes 1363976 | tf_op jit(solution)/shard_map/ppermute | solution.py:723
  9.6 21.8 %copy-start.4 = (bf16[296,768]{1,0:T(8,128)(2,1)S(1)}, bf16[296,768]{1,0:T(8,128)(2,1)}, u32[]{:S(2)}) copy-start(bf16[296,768]{1,0:T(8,128)(2,1)} %pack.1) | copy-start | bytes 1363972
  13.4 18.1 %copy-start.8 = (bf16[296,768]{1,0:T(8,128)(2,1)}, bf16[296,768]{1,0:T(8,128)(2,1)S(1)}, u32[]{:S(2)}) copy-start(bf16[296,768]{1,0:T(8,128)(2,1)S(1)} %collective-permute-done.2) | copy-start | bytes 1363972
  19.3 12.2 %copy-start.10 = (bf16[4,104,768]{2,1,0:T(8,128)(2,1)}, bf16[4,104,768]{2,1,0:T(8,128)(2,1)S(1)}, u32[]{:S(2)}) copy-start(bf16[4,104,768]{2,1,0:T(8,128)(2,1)S(1)} %pad_maximum_fusion.1.p0) | copy-start | bytes 1916932
  19.3 12.1 %collective-permute-start.5 = (bf16[4,104,768]{2,1,0:T(8,128)(2,1)S(1)}, bf16[4,104,768]{2,1,0:T(8,128)(2,1)S(1)}, u32[]{:S(2)}, u32[]{:S(2)}) collective-permute-start(bf16[4,104,768]{2,1,0:T(8,128)(2,1)S(1)} %pad_maximum_fusion.1.p0), channel_id=1, source_target_pairs={{0,16},{1,5},{2,18},{3,7},{4,20},{5,1},{6,22},{7,3},{8,24},{9,13},... | collective-permute-start | bytes 1916936 | tf_op jit(solution)/shard_map/ppermute | solution.py:723
  22.4 13.5 %collective-permute-start.6 = (bf16[4,104,768]{2,1,0:T(8,128)(2,1)S(1)}, bf16[4,104,768]{2,1,0:T(8,128)(2,1)S(1)}, u32[]{:S(2)}, u32[]{:S(2)}) collective-permute-start(bf16[4,104,768]{2,1,0:T(8,128)(2,1)S(1)} %pad_maximum_fusion.1.p0), channel_id=1, source_target_pairs={{0,1},{1,0},{2,3},{3,2},{4,5},{5,4},{6,7},{7,6},{8,9},{9,8},{10,11... | collective-permute-start | bytes 1916936 | tf_op jit(solution)/shard_map/ppermute | solution.py:719
  22.4 16.0 %collective-permute-start.4 = (bf16[4,104,768]{2,1,0:T(8,128)(2,1)S(1)}, bf16[4,104,768]{2,1,0:T(8,128)(2,1)}, u32[]{:S(2)}, u32[]{:S(2)}) collective-permute-start(bf16[4,104,768]{2,1,0:T(8,128)(2,1)S(1)} %pad_maximum_fusion.1.p0), channel_id=1, source_target_pairs={{0,24},{1,7},{2,26},{3,1},{4,28},{5,3},{6,30},{7,5},{8,0},{9,15},{... | collective-permute-start | bytes 1916936 | tf_op jit(solution)/shard_map/ppermute | solution.py:723
  23.6 16.2 %collective-permute-start.3 = (bf16[4,104,768]{2,1,0:T(8,128)(2,1)S(1)}, bf16[4,104,768]{2,1,0:T(8,128)(2,1)}, u32[]{:S(2)}, u32[]{:S(2)}) collective-permute-start(bf16[4,104,768]{2,1,0:T(8,128)(2,1)S(1)} %pad_maximum_fusion.1.p0), channel_id=1, source_target_pairs={{0,8},{1,3},{2,10},{3,5},{4,12},{5,7},{6,14},{7,1},{8,16},{9,11},{... | collective-permute-start | bytes 1916936 | tf_op jit(solution)/shard_map/ppermute | solution.py:723
  31.4 0.8 copy-start.16
  31.4 8.3 %collective-permute-start.9 = (bf16[4,104,768]{2,1,0:T(8,128)(2,1)S(1)}, bf16[4,104,768]{2,1,0:T(8,128)(2,1)S(1)}, u32[]{:S(2)}, u32[]{:S(2)}) collective-permute-start(bf16[4,104,768]{2,1,0:T(8,128)(2,1)S(1)} %collective-permute-done.5.p3), channel_id=1, source_target_pairs={{0,1},{1,0},{2,3},{3,2},{4,5},{5,4},{6,7},{7,6},{8,9},{9,8},{10,11... | collective-permute-start | bytes 1916936 | tf_op jit(solution)/shard_map/ppermute | solution.py:719
  31.5 1.2 slice-start.4
  32.8 29.3 %copy-start.9 = (bf16[4,8,24,768]{3,2,1,0:T(8,128)(2,1)}, bf16[4,8,24,768]{3,2,1,0:T(8,128)(2,1)S(1)}, u32[]{:S(2)}) copy-start(bf16[4,8,24,768]{3,2,1,0:T(8,128)(2,1)S(1)} %pad_maximum_fusion.p0) | copy-start | bytes 3538948
  32.8 29.3 %collective-permute-start.12 = (bf16[4,8,24,768]{3,2,1,0:T(8,128)(2,1)S(1)}, bf16[4,8,24,768]{3,2,1,0:T(8,128)(2,1)S(1)}, u32[]{:S(2)}, u32[]{:S(2)}) collective-permute-start(bf16[4,8,24,768]{3,2,1,0:T(8,128)(2,1)S(1)} %pad_maximum_fusion.p0), channel_id=1, source_target_pairs={{0,16},{1,5},{2,18},{3,7},{4,20},{5,1},{6,22},{7,3},{8,24},{9,13},... | collective-permute-start | bytes 3538952 | tf_op jit(solution)/shard_map/ppermute | solution.py:723
  35.9 3.9 %copy-start.17 = (bf16[4,104,768]{2,1,0:T(8,128)(2,1)}, bf16[4,104,768]{2,1,0:T(8,128)(2,1)S(1)}, u32[]{:S(2)}) copy-start(bf16[4,104,768]{2,1,0:T(8,128)(2,1)S(1)} %collective-permute-done.6.p4) | copy-start | bytes 1916932
  35.9 27.8 %collective-permute-start.11 = (bf16[4,8,24,768]{3,2,1,0:T(8,128)(2,1)S(1)}, bf16[4,8,24,768]{3,2,1,0:T(8,128)(2,1)}, u32[]{:S(2)}, u32[]{:S(2)}) collective-permute-start(bf16[4,8,24,768]{3,2,1,0:T(8,128)(2,1)S(1)} %pad_maximum_fusion.p0), channel_id=1, source_target_pairs={{0,24},{1,7},{2,26},{3,1},{4,28},{5,3},{6,30},{7,5},{8,0},{9,15},{... | collective-permute-start | bytes 3538952 | tf_op jit(solution)/shard_map/ppermute | solution.py:723
  38.4 25.3 %collective-permute-start.10 = (bf16[4,8,24,768]{3,2,1,0:T(8,128)(2,1)S(1)}, bf16[4,8,24,768]{3,2,1,0:T(8,128)(2,1)}, u32[]{:S(2)}, u32[]{:S(2)}) collective-permute-start(bf16[4,8,24,768]{3,2,1,0:T(8,128)(2,1)S(1)} %pad_maximum_fusion.p0), channel_id=1, source_target_pairs={{0,8},{1,3},{2,10},{3,5},{4,12},{5,7},{6,14},{7,1},{8,16},{9,11},{... | collective-permute-start | bytes 3538952 | tf_op jit(solution)/shard_map/ppermute | solution.py:723
  39.8 2.3 %collective-permute-start.8 = (bf16[4,104,768]{2,1,0:T(8,128)(2,1)}, bf16[4,104,768]{2,1,0:T(8,128)(2,1)S(1)}, u32[]{:S(2)}, u32[]{:S(2)}) collective-permute-start(bf16[4,104,768]{2,1,0:T(8,128)(2,1)} %collective-permute-done.4.p2), channel_id=1, source_target_pairs={{0,1},{1,0},{2,3},{3,2},{4,5},{5,4},{6,7},{7,6},{8,9},{9,8},{10,11... | collective-permute-start | bytes 1916936 | tf_op jit(solution)/shard_map/ppermute | solution.py:719
  39.8 0.8 copy-start.18
  39.8 3.3 %collective-permute-start.7 = (bf16[4,104,768]{2,1,0:T(8,128)(2,1)}, bf16[4,104,768]{2,1,0:T(8,128)(2,1)}, u32[]{:S(2)}, u32[]{:S(2)}) collective-permute-start(bf16[4,104,768]{2,1,0:T(8,128)(2,1)} %collective-permute-done.3.p1), channel_id=1, source_target_pairs={{0,1},{1,0},{2,3},{3,2},{4,5},{5,4},{6,7},{7,6},{8,9},{9,8},{10,11... | collective-permute-start | bytes 1916936 | tf_op jit(solution)/shard_map/ppermute | solution.py:719
  42.1 1.0 copy-start.19
  42.1 22.2 %collective-permute-start.13 = (bf16[4,8,24,768]{3,2,1,0:T(8,128)(2,1)S(1)}, bf16[4,8,24,768]{3,2,1,0:T(8,128)(2,1)S(1)}, u32[]{:S(2)}, u32[]{:S(2)}) collective-permute-start(bf16[4,8,24,768]{3,2,1,0:T(8,128)(2,1)S(1)} %pad_maximum_fusion.p0), channel_id=1, source_target_pairs={{0,1},{1,0},{2,3},{3,2},{4,5},{5,4},{6,7},{7,6},{8,9},{9,8},{10,11... | collective-permute-start | bytes 3538952 | tf_op jit(solution)/shard_map/ppermute | solution.py:719
  62.1 10.1 %copy-start.11 = (bf16[4,8,24,768]{3,2,1,0:T(8,128)(2,1)}, bf16[4,8,24,768]{3,2,1,0:T(8,128)(2,1)S(1)}, u32[]{:S(2)}) copy-start(bf16[4,8,24,768]{3,2,1,0:T(8,128)(2,1)S(1)} %collective-permute-done.12.p3) | copy-start | bytes 3538948
  63.7 3.1 %collective-permute-start.14 = (bf16[4,8,24,768]{3,2,1,0:T(8,128)(2,1)}, bf16[4,8,24,768]{3,2,1,0:T(8,128)(2,1)S(1)}, u32[]{:S(2)}, u32[]{:S(2)}) collective-permute-start(bf16[4,8,24,768]{3,2,1,0:T(8,128)(2,1)} %collective-permute-done.10.p1), channel_id=1, source_target_pairs={{0,1},{1,0},{2,3},{3,2},{4,5},{5,4},{6,7},{7,6},{8,9},{9,8},{10,11... | collective-permute-start | bytes 3538952 | tf_op jit(solution)/shard_map/ppermute | solution.py:719
  63.7 6.4 %collective-permute-start.15 = (bf16[4,8,24,768]{3,2,1,0:T(8,128)(2,1)}, bf16[4,8,24,768]{3,2,1,0:T(8,128)(2,1)S(1)}, u32[]{:S(2)}, u32[]{:S(2)}) collective-permute-start(bf16[4,8,24,768]{3,2,1,0:T(8,128)(2,1)} %collective-permute-done.11.p2), channel_id=1, source_target_pairs={{0,1},{1,0},{2,3},{3,2},{4,5},{5,4},{6,7},{7,6},{8,9},{9,8},{10,11... | collective-permute-start | bytes 3538952 | tf_op jit(solution)/shard_map/ppermute | solution.py:719
  64.3 5.9 %collective-permute-start.16 = (bf16[4,8,24,768]{3,2,1,0:T(8,128)(2,1)S(1)}, bf16[4,8,24,768]{3,2,1,0:T(8,128)(2,1)S(1)}, u32[]{:S(2)}, u32[]{:S(2)}) collective-permute-start(bf16[4,8,24,768]{3,2,1,0:T(8,128)(2,1)S(1)} %collective-permute-done.12.p3), channel_id=1, source_target_pairs={{0,1},{1,0},{2,3},{3,2},{4,5},{5,4},{6,7},{7,6},{8,9},{9,8},{10,11... | collective-permute-start | bytes 3538952 | tf_op jit(solution)/shard_map/ppermute | solution.py:719
  64.3 8.0 %copy-start.12 = (bf16[4,8,24,768]{3,2,1,0:T(8,128)(2,1)}, bf16[4,8,24,768]{3,2,1,0:T(8,128)(2,1)S(1)}, u32[]{:S(2)}) copy-start(bf16[4,8,24,768]{3,2,1,0:T(8,128)(2,1)S(1)} %collective-permute-done.13.p4) | copy-start | bytes 3538948
  66.8 5.4 %copy-start.13 = (bf16[4,8,24,768]{3,2,1,0:T(8,128)(2,1)}, bf16[4,8,24,768]{3,2,1,0:T(8,128)(2,1)S(1)}, u32[]{:S(2)}) copy-start(bf16[4,8,24,768]{3,2,1,0:T(8,128)(2,1)S(1)} %collective-permute-done.14.p5) | copy-start | bytes 3538948
  70.2 1.0 copy-start.14
  71.2 1.0 copy-start.15
  109.4 12.3 %collective-permute-start.17 = (bf16[16,8,24,768]{3,2,1,0:T(8,128)(2,1)}, bf16[16,8,24,768]{3,2,1,0:T(8,128)(2,1)}, u32[]{:S(2)}, u32[]{:S(2)}) collective-permute-start(bf16[16,8,24,768]{3,2,1,0:T(8,128)(2,1)} %get-tuple-element.101), channel_id=1, source_target_pairs={{0,1},{1,0},{2,3},{3,2},{4,5},{5,4},{6,7},{7,6},{8,9},{9,8},{10,11... | collective-permute-start | bytes 14155784 | tf_op jit(solution)/shard_map/ppermute | solution.py:719
  109.9 11.9 %slice-start.2 = ((s8[4718592]{0:T(1024)(128)(4,1)}), s8[4194304]{0:T(1024)(128)(4,1)S(1)}, s32[]{:S(2)}) async-start(s8[4718592]{0:T(1024)(128)(4,1)} %bitcast.65), calls=%async_computation.2 | async-start | bytes 8388608
  109.9 11.9 %slice-start.3 = ((s8[4718592]{0:T(1024)(128)(4,1)}), s8[524288]{0:T(1024)(128)(4,1)S(1)}, s32[]{:S(2)}) async-start(s8[4718592]{0:T(1024)(128)(4,1)} %bitcast.65), calls=%async_computation.3 | async-start | bytes 1048576
  125.7 11.8 %copy-start.7 = (bf16[4,8,24,768]{3,2,1,0:T(8,128)(2,1)S(1)}, bf16[4,8,24,768]{3,2,1,0:T(8,128)(2,1)}, u32[]{:S(2)}) copy-start(bf16[4,8,24,768]{3,2,1,0:T(8,128)(2,1)} %get-tuple-element.126) | copy-start | bytes 3538948
  125.7 14.7 %copy-start.6 = (bf16[4,8,24,768]{3,2,1,0:T(8,128)(2,1)S(1)}, bf16[4,8,24,768]{3,2,1,0:T(8,128)(2,1)}, u32[]{:S(2)}) copy-start(bf16[4,8,24,768]{3,2,1,0:T(8,128)(2,1)} %get-tuple-element.127) | copy-start | bytes 3538948
  125.7 15.3 %copy-start.5 = (bf16[4,8,24,768]{3,2,1,0:T(8,128)(2,1)S(1)}, bf16[4,8,24,768]{3,2,1,0:T(8,128)(2,1)}, u32[]{:S(2)}) copy-start(bf16[4,8,24,768]{3,2,1,0:T(8,128)(2,1)} %get-tuple-element.128) | copy-start | bytes 3538948
  137.1 6.5 %collective-permute-start.18 = (bf16[16,104,768]{2,1,0:T(8,128)(2,1)}, bf16[16,104,768]{2,1,0:T(8,128)(2,1)S(1)}, u32[]{:S(2)}, u32[]{:S(2)}) collective-permute-start(bf16[16,104,768]{2,1,0:T(8,128)(2,1)} %get-tuple-element.106), channel_id=1, source_target_pairs={{0,1},{1,0},{2,3},{3,2},{4,5},{5,4},{6,7},{7,6},{8,9},{9,8},{10,11... | collective-permute-start | bytes 7667720 | tf_op jit(solution)/shard_map/ppermute | solution.py:719
  137.5 17.8 %collective-permute-start.28 = (bf16[4,8,24,768]{3,2,1,0:T(8,128)(2,1)S(1)}, bf16[4,8,24,768]{3,2,1,0:T(8,128)(2,1)S(1)}, u32[]{:S(2)}, u32[]{:S(2)}) collective-permute-start(bf16[4,8,24,768]{3,2,1,0:T(8,128)(2,1)S(1)} %copy-done.7), channel_id=1, source_target_pairs={{0,16},{1,5},{2,18},{3,7},{4,20},{5,1},{6,22},{7,3},{8,24},{9,13},... | collective-permute-start | bytes 3538952 | tf_op jit(solution)/shard_map/ppermute | solution.py:723
  140.4 27.5 %collective-permute-start.29 = (bf16[4,8,24,768]{3,2,1,0:T(8,128)(2,1)S(1)}, bf16[4,8,24,768]{3,2,1,0:T(8,128)(2,1)S(1)}, u32[]{:S(2)}, u32[]{:S(2)}) collective-permute-start(bf16[4,8,24,768]{3,2,1,0:T(8,128)(2,1)S(1)} %copy-done.6), channel_id=1, source_target_pairs={{0,8},{1,3},{2,10},{3,5},{4,12},{5,7},{6,14},{7,1},{8,16},{9,11},{... | collective-permute-start | bytes 3538952 | tf_op jit(solution)/shard_map/ppermute | solution.py:723
  141.0 26.9 %collective-permute-start.30 = (bf16[4,8,24,768]{3,2,1,0:T(8,128)(2,1)S(1)}, bf16[4,8,24,768]{3,2,1,0:T(8,128)(2,1)S(1)}, u32[]{:S(2)}, u32[]{:S(2)}) collective-permute-start(bf16[4,8,24,768]{3,2,1,0:T(8,128)(2,1)S(1)} %copy-done.5), channel_id=1, source_target_pairs={{0,24},{1,7},{2,26},{3,1},{4,28},{5,3},{6,30},{7,5},{8,0},{9,15},{... | collective-permute-start | bytes 3538952 | tf_op jit(solution)/shard_map/ppermute | solution.py:723
  143.6 34.9 %slice-start = ((s8[5111808]{0:T(1024)(128)(4,1)}), s8[4194304]{0:T(1024)(128)(4,1)S(1)}, s32[]{:S(2)}) async-start(s8[5111808]{0:T(1024)(128)(4,1)} %bitcast.63), calls=%async_computation | async-start | bytes 8388608
  143.6 34.9 %slice-start.1 = ((s8[5111808]{0:T(1024)(128)(4,1)}), s8[917504]{0:T(1024)(128)(4,1)S(1)}, s32[]{:S(2)}) async-start(s8[5111808]{0:T(1024)(128)(4,1)} %bitcast.63), calls=%async_computation.1 | async-start | bytes 1835008
  143.6 34.9 %copy-start.3 = (bf16[640,768]{1,0:T(8,128)(2,1)S(1)}, bf16[640,768]{1,0:T(8,128)(2,1)}, u32[]{:S(2)}) copy-start(bf16[640,768]{1,0:T(8,128)(2,1)} %get-tuple-element.102.dv) | copy-start | bytes 2949124
  146.0 32.5 %copy-start = (f32[640,768]{1,0:T(8,128)S(1)}, f32[640,768]{1,0:T(8,128)}, u32[]{:S(2)}) copy-start(f32[640,768]{1,0:T(8,128)} %get-tuple-element.107.gfs) | copy-start | bytes 5898244
  146.0 32.5 %copy-start.1 = (bf16[640,768]{1,0:T(8,128)(2,1)S(1)}, bf16[640,768]{1,0:T(8,128)(2,1)}, u32[]{:S(2)}) copy-start(bf16[640,768]{1,0:T(8,128)(2,1)} %get-tuple-element.97.dq) | copy-start | bytes 2949124
  146.0 32.5 %copy-start.2 = (bf16[640,768]{1,0:T(8,128)(2,1)S(1)}, bf16[640,768]{1,0:T(8,128)(2,1)}, u32[]{:S(2)}) copy-start(bf16[640,768]{1,0:T(8,128)(2,1)} %get-tuple-element.98.dk) | copy-start | bytes 2949124
  146.1 31.5 %collective-permute-start.19 = (bf16[4,104,768]{2,1,0:T(8,128)(2,1)S(1)}, bf16[4,104,768]{2,1,0:T(8,128)(2,1)S(1)}, u32[]{:S(2)}, u32[]{:S(2)}) collective-permute-start(bf16[4,104,768]{2,1,0:T(8,128)(2,1)S(1)} %get-tuple-element.109), channel_id=1, source_target_pairs={{0,8},{1,3},{2,10},{3,5},{4,12},{5,7},{6,14},{7,1},{8,16},{9,11},{... | collective-permute-start | bytes 1916936 | tf_op jit(solution)/shard_map/ppermute | solution.py:723
  146.1 37.9 %collective-permute-start.20 = (bf16[4,104,768]{2,1,0:T(8,128)(2,1)S(1)}, bf16[4,104,768]{2,1,0:T(8,128)(2,1)S(1)}, u32[]{:S(2)}, u32[]{:S(2)}) collective-permute-start(bf16[4,104,768]{2,1,0:T(8,128)(2,1)S(1)} %get-tuple-element.110), channel_id=1, source_target_pairs={{0,24},{1,7},{2,26},{3,1},{4,28},{5,3},{6,30},{7,5},{8,0},{9,15},{... | collective-permute-start | bytes 1916936 | tf_op jit(solution)/shard_map/ppermute | solution.py:723
  155.3 32.6 %collective-permute-start.21 = (bf16[4,104,768]{2,1,0:T(8,128)(2,1)S(1)}, bf16[4,104,768]{2,1,0:T(8,128)(2,1)S(1)}, u32[]{:S(2)}, u32[]{:S(2)}) collective-permute-start(bf16[4,104,768]{2,1,0:T(8,128)(2,1)S(1)} %get-tuple-element.111), channel_id=1, source_target_pairs={{0,16},{1,5},{2,18},{3,7},{4,20},{5,1},{6,22},{7,3},{8,24},{9,13},... | collective-permute-start | bytes 1916936 | tf_op jit(solution)/shard_map/ppermute | solution.py:723
  168.3 23.6 %collective-permute-start.31 = (bf16[8,24,768]{2,1,0:T(8,128)(2,1)S(1)}, bf16[8,24,768]{2,1,0:T(8,128)(2,1)S(1)}, u32[]{:S(2)}, u32[]{:S(2)}) collective-permute-start(bf16[8,24,768]{2,1,0:T(8,128)(2,1)S(1)} %get-tuple-element.143), channel_id=1, source_target_pairs={{0,4},{1,17},{2,6},{3,19},{4,0},{5,21},{6,2},{7,23},{8,12},{9,25},... | collective-permute-start | bytes 884744 | tf_op jit(solution)/shard_map/ppermute | solution.py:723
  170.8 21.9 %collective-permute-start.33 = (bf16[8,24,768]{2,1,0:T(8,128)(2,1)S(1)}, bf16[8,24,768]{2,1,0:T(8,128)(2,1)S(1)}, u32[]{:S(2)}, u32[]{:S(2)}) collective-permute-start(bf16[8,24,768]{2,1,0:T(8,128)(2,1)S(1)} %get-tuple-element.144), channel_id=1, source_target_pairs={{0,6},{1,25},{2,0},{3,27},{4,2},{5,29},{6,4},{7,31},{8,14},{9,1},{... | collective-permute-start | bytes 884744 | tf_op jit(solution)/shard_map/ppermute | solution.py:723
  177.5 15.1 %collective-permute-start.32 = (bf16[8,24,768]{2,1,0:T(8,128)(2,1)S(1)}, bf16[8,24,768]{2,1,0:T(8,128)(2,1)S(1)}, u32[]{:S(2)}, u32[]{:S(2)}) collective-permute-start(bf16[8,24,768]{2,1,0:T(8,128)(2,1)S(1)} %get-tuple-element.145), channel_id=1, source_target_pairs={{0,2},{1,9},{2,4},{3,11},{4,6},{5,13},{6,0},{7,15},{8,10},{9,17},{... | collective-permute-start | bytes 884744 | tf_op jit(solution)/shard_map/ppermute | solution.py:723
  188.1 9.2 %collective-permute-start.22 = (bf16[104,768]{1,0:T(8,128)(2,1)S(1)}, bf16[104,768]{1,0:T(8,128)(2,1)S(1)}, u32[]{:S(2)}, u32[]{:S(2)}) collective-permute-start(bf16[104,768]{1,0:T(8,128)(2,1)S(1)} %get-tuple-element.146), channel_id=1, source_target_pairs={{0,4},{1,17},{2,6},{3,19},{4,0},{5,21},{6,2},{7,23},{8,12},{9,25},... | collective-permute-start | bytes 479240 | tf_op jit(solution)/shard_map/ppermute | solution.py:723
  190.6 7.6 %collective-permute-start.24 = (bf16[104,768]{1,0:T(8,128)(2,1)S(1)}, bf16[104,768]{1,0:T(8,128)(2,1)S(1)}, u32[]{:S(2)}, u32[]{:S(2)}) collective-permute-start(bf16[104,768]{1,0:T(8,128)(2,1)S(1)} %get-tuple-element.147), channel_id=1, source_target_pairs={{0,6},{1,25},{2,0},{3,27},{4,2},{5,29},{6,4},{7,31},{8,14},{9,1},{... | collective-permute-start | bytes 479240 | tf_op jit(solution)/shard_map/ppermute | solution.py:723
  191.8 6.5 %collective-permute-start.23 = (bf16[104,768]{1,0:T(8,128)(2,1)S(1)}, bf16[104,768]{1,0:T(8,128)(2,1)S(1)}, u32[]{:S(2)}, u32[]{:S(2)}) collective-permute-start(bf16[104,768]{1,0:T(8,128)(2,1)S(1)} %get-tuple-element.148), channel_id=1, source_target_pairs={{0,2},{1,9},{2,4},{3,11},{4,6},{5,13},{6,0},{7,15},{8,10},{9,17},{... | collective-permute-start | bytes 479240 | tf_op jit(solution)/shard_map/ppermute | solution.py:723
  192.9 11.6 %collective-permute-start.36 = (bf16[8,24,768]{2,1,0:T(8,128)(2,1)S(1)}, bf16[8,24,768]{2,1,0:T(8,128)(2,1)S(1)}, u32[]{:S(2)}, u32[]{:S(2)}) collective-permute-start(bf16[8,24,768]{2,1,0:T(8,128)(2,1)S(1)} %fusion.1.own), channel_id=1, source_target_pairs={{0,64},{32,96},{64,0},{96,32},{1,65},{33,97},{65,1},{97,33},{2,66}... | collective-permute-start | bytes 884744 | tf_op jit(solution)/shard_map/ppermute | solution.py:733
  196.2 14.7 %collective-permute-start.35 = (bf16[8,24,768]{2,1,0:T(8,128)(2,1)S(1)}, bf16[8,24,768]{2,1,0:T(8,128)(2,1)S(1)}, u32[]{:S(2)}, u32[]{:S(2)}) collective-permute-start(bf16[8,24,768]{2,1,0:T(8,128)(2,1)S(1)} %fusion.1.own), channel_id=1, source_target_pairs={{0,96},{32,0},{64,32},{96,64},{1,97},{33,1},{65,33},{97,65},{2,98}... | collective-permute-start | bytes 884744 | tf_op jit(solution)/shard_map/ppermute | solution.py:733
  197.3 15.2 %collective-permute-start.34 = (bf16[8,24,768]{2,1,0:T(8,128)(2,1)S(1)}, bf16[8,24,768]{2,1,0:T(8,128)(2,1)S(1)}, u32[]{:S(2)}, u32[]{:S(2)}) collective-permute-start(bf16[8,24,768]{2,1,0:T(8,128)(2,1)S(1)} %fusion.1.own), channel_id=1, source_target_pairs={{0,32},{32,64},{64,96},{96,0},{1,33},{33,65},{65,97},{97,1},{2,34}... | collective-permute-start | bytes 884744 | tf_op jit(solution)/shard_map/ppermute | solution.py:733
  198.5 15.0 %collective-permute-start.27 = (bf16[104,768]{1,0:T(8,128)(2,1)S(1)}, bf16[104,768]{1,0:T(8,128)(2,1)S(1)}, u32[]{:S(2)}, u32[]{:S(2)}) collective-permute-start(bf16[104,768]{1,0:T(8,128)(2,1)S(1)} %fusion.3.own), channel_id=1, source_target_pairs={{0,64},{32,96},{64,0},{96,32},{1,65},{33,97},{65,1},{97,33},{2,66}... | collective-permute-start | bytes 479240 | tf_op jit(solution)/shard_map/ppermute | solution.py:733
  201.8 12.7 %collective-permute-start.26 = (bf16[104,768]{1,0:T(8,128)(2,1)S(1)}, bf16[104,768]{1,0:T(8,128)(2,1)S(1)}, u32[]{:S(2)}, u32[]{:S(2)}) collective-permute-start(bf16[104,768]{1,0:T(8,128)(2,1)S(1)} %fusion.3.own), channel_id=1, source_target_pairs={{0,96},{32,0},{64,32},{96,64},{1,97},{33,1},{65,33},{97,65},{2,98}... | collective-permute-start | bytes 479240 | tf_op jit(solution)/shard_map/ppermute | solution.py:733
  204.6 9.9 %collective-permute-start.25 = (bf16[104,768]{1,0:T(8,128)(2,1)S(1)}, bf16[104,768]{1,0:T(8,128)(2,1)S(1)}, u32[]{:S(2)}, u32[]{:S(2)}) collective-permute-start(bf16[104,768]{1,0:T(8,128)(2,1)S(1)} %fusion.3.own), channel_id=1, source_target_pairs={{0,32},{32,64},{64,96},{96,0},{1,33},{33,65},{65,97},{97,1},{2,34}... | collective-permute-start | bytes 479240 | tf_op jit(solution)/shard_map/ppermute | solution.py:733
where the time goes:
time: 216 us; the launch traced here: 215 us
  Pallas kernels  88.6 us (41%)
  waiting for transfers between devices  61.4 us (28%)
  starting transfers between devices  51.4 us (24%)
  other arithmetic  8.23 us (4%)
  local copies, waits for them, and re-layouts  4.54 us (2%)
    ppermute x21, waiting for transfers between devices, around(): lax.ppermute(v[d] if isinstance(v, (list, tuple)) else v, 'shard', turn(d...  44.6 us
    ppermute x21, starting transfers between devices, around(): lax.ppermute(v[d] if isinstance(v, (list, tuple)) else v, 'shard', turn(d...  38.3 us
    pallas_call x1, Pallas kernels, feed(): pl.pallas_call(functools.partial(feed_body, dims), in_specs=[SCALARS] * 3...  37.2 us
    pallas_call x1, Pallas kernels, attention_forward(): pl.pallas_call(functools.partial(attention_forward_body, dims), grid_spec...  19 us
    pallas_call x1, Pallas kernels, attention_back(): pl.pallas_call(functools.partial(attention_back_body, dims), grid=(width...  11.8 us
    pallas_call x1, Pallas kernels, weight_back(): pl.pallas_call(functools.partial(weight_back_body, dims), grid_spec=pltpu...  11.4 us
    ppermute x6, starting transfers between devices, second_turn(): lax.ppermute(own, 'rep', [(i, (i + d) % RING) for i in range(RING)])  11.2 us
    ppermute x6, waiting for transfers between devices, second_turn(): lax.ppermute(own, 'rep', [(i, (i + d) % RING) for i in range(RING)])  9.14 us
  transfers between devices with their start and end apart: 37, of which 18 were waited for; matrix products, arithmetic and copies ran while one was open for 2% of the time, Pallas kernels for 17%

commit v1 on v0

--- a/solution.py
+++ b/solution.py
@@ -332,7 +332,7 @@
 
 def feed_body(
     dims, slen, llen, pos, unit1, cot_s, cot_l, inv1, ub, vecs, p0, p1, p2, p3, p4, p5, p6, p7,
-    keep, give, outs_o, outl_o, gfs_o, gatt_o, sums_o, dub_o,
+    keep, give, outs_o, outl_o, gfs_o, gatt_o, sums_o,
     wup, wdown, unit_v, cot_v, low_v, low_t, hidden, gelu_v, grad_v, gffn, out_v, gatt, valid_v,
     keep_dv, give_dv, keep_uv, give_uv, sems, piece_sems, down_sems, up_sems,
 ):
@@ -449,7 +449,7 @@
         up = (nt(gffn[...], weight) * gelu_v[j].astype(F32)).astype(BF16)
         hidden[j] = up
         grad = nn(low_t[...], hidden[j])
-        dub_o[:, pl.ds(pl.multiple_of(j * block, block), block)] = grad[width : width + 1]
+        sums_o[pl.ds(8 + j, 1)] = grad[width : width + 1]
         deal(keep_uv.at[j], give_uv.at[j], pos, grad[:width].astype(BF16), slice(None), each)
         for copy in up_copies(j):
             copy.start()
@@ -490,7 +490,7 @@
     return pl.pallas_call(
         functools.partial(feed_body, dims),
         in_specs=[SCALARS] * 3 + [HBM] * 3 + [ON_CHIP] * 3 + [HBM] * 8,
-        out_specs=[HBM] * 6 + [ON_CHIP] * 2,
+        out_specs=[HBM] * 6 + [ON_CHIP],
         scratch_shapes=[
             pltpu.VMEM((parts, SHARDS, each, width), BF16), pltpu.VMEM((SHARDS, parts, each, width), BF16),
             pltpu.VMEM((rows, width), F32), pltpu.VMEM((rows, width), BF16), pltpu.VMEM((rows, width), BF16),
@@ -507,8 +507,7 @@
             jax.ShapeDtypeStruct(cot_l.shape, BF16),
             jax.ShapeDtypeStruct((rows, width), F32),
             jax.ShapeDtypeStruct((rows, width), BF16),
-            jax.ShapeDtypeStruct((8, width), F32),
-            jax.ShapeDtypeStruct((1, inner), F32),
+            jax.ShapeDtypeStruct((16, width), F32),
         ],
         compiler_params=params(58),
         cost_estimate=cost(12 * rows * width * inner, 30e6),
@@ -516,7 +515,7 @@
     )(slen, llen, pos, unit1, cot_s, cot_l, inv1, ub, vecs, *pieces)
 
 
-def attention_back_body(dims, gatt, wo_block, q, k, v, ps, plong, dq_o, dk_o, dv_o, gc, wo_all):
+def attention_back_body(dims, gatt, wo_block, q, k, v, ps, plong, grads, gc, wo_all):
     step = pl.program_id(0)
     width, cols = gatt.shape[1], q.shape[1]
     at_cols = pl.ds(pl.multiple_of(step * cols, cols), cols)
@@ -541,9 +540,9 @@
                 d = dp[half]
                 ds.append((p * (d - jnp.sum(d * p, axis=0, keepdims=True))).astype(BF16))
             ds = jnp.concatenate(ds, axis=0)
-            dv_o[at, lanes] = own_lanes(nn(probs, grad)).astype(BF16)
-            dk_o[at, lanes] = (own_lanes(nn(ds, q[at, lanes])) * scale).astype(BF16)
-            dq_o[at, lanes] = (tn(ds, two_heads(k[at, lanes])) * scale).astype(BF16)
+            grads[2, at, lanes] = own_lanes(nn(probs, grad)).astype(BF16)
+            grads[1, at, lanes] = (own_lanes(nn(ds, q[at, lanes])) * scale).astype(BF16)
+            grads[0, at, lanes] = (tn(ds, two_heads(k[at, lanes])) * scale).astype(BF16)
 
 
 def attention_back(gatt, gathered, q, k, v, ps, plong, dims):
@@ -562,9 +561,9 @@
             pl.BlockSpec((per, 2 * short_rows, short_rows), lambda g: (g, 0, 0)),
             pl.BlockSpec((long_count, per, 2 * long_length, long_length), lambda g: (0, g, 0, 0)),
         ],
-        out_specs=[cols, cols, cols],
+        out_specs=pl.BlockSpec((3, rows, step), lambda g: (0, 0, g)),
         scratch_shapes=[pltpu.VMEM((rows, step), BF16), pltpu.VMEM((width, width), BF16)],
-        out_shape=[jax.ShapeDtypeStruct((rows, width), BF16)] * 3,
+        out_shape=jax.ShapeDtypeStruct((3, rows, width), BF16),
         compiler_params=params(BACK_MIB),
         cost_estimate=cost(8 * rows * width * width, 15e6),
         name="attention_back",
@@ -572,84 +571,117 @@
 
 
 def weight_back_body(
-    dims, pos, gatt_cols, c, dq, dk, dv, xs, xl, sums_f, dub,
-    keep, give,
-    x_t, c_t, sums,
+    pos, gatt, gatt_other, c, c_other, d, d_other, xs, xl, xs_other, xl_other, sums_own, sums_other,
+    o0, o1, o2, o3,
+    x_t, c_t, grad, sums,
 ):
     step = pl.program_id(0)
-    short_rows = dims[0]
     rows, width = c.shape
-    cols = dq.shape[1]
+    cols = gatt.shape[1]
     each = width // SHARDS
+    mine = CHIPS * each
+    on_first = pos[2] == 0
     at_cols = pl.ds(pl.multiple_of(step * cols, cols), cols)
+
+    def take(target, first, source):
+        turned = source[...].T
+        for i in range(CHIPS):
+            low = 2 * i * each
+            target[i * each : (i + 1) * each, first : first + turned.shape[1]] = jnp.where(
+                on_first, turned[low : low + each], turned[low + each : low + 2 * each]
+            )
 
     @pl.when(step == 0)
     def _():
-        x_t[:width, :short_rows] = xs[...].T
-        x_t[:width, short_rows:] = xl[...].T
-        x_t[width:] = jnp.ones((16, rows), BF16)
-        c_t[...] = c[...].T
-        sums[...] = sums_f[...]
-
-    deal(keep, give, pos, nn(c_t[...], gatt_cols[...]).astype(BF16), slice(3 * each, 4 * each), each)
-    for i, d in enumerate((dq, dk, dv)):
-        grad = nn(x_t[...], d[...])
-        deal(keep, give, pos, grad[:width].astype(BF16), slice(i * each, (i + 1) * each), each)
+        first = 0
+        for source in (xs, xl, xs_other, xl_other):
+            take(x_t, first, source)
+            first += source.shape[0]
+        x_t[mine:] = jnp.ones((16, 2 * rows), BF16)
+        take(c_t, 0, c)
+        take(c_t, rows, c_other)
+        sums[...] = sums_own[...] + sums_other[...]
+
+    def hand_out(value, at):
+        n = value.shape[0] // CHIPS
+        grad[:, :n] = value.reshape(CHIPS, n, cols)
+        for along, out in enumerate((o0, o1, o2, o3)):
+            for e in range(RING):
+                x0, z0 = (pos[0] + along) & (RING - 1), (pos[1] + e) & (RING - 1)
+                x1, z1 = (pos[0] + e) & (RING - 1), (pos[1] + along) & (RING - 1)
+                out[e, at : at + n] = grad[jnp.where(on_first, x0 * RING + z0, x1 * RING + z1), :n]
+
+    both = jnp.concatenate([gatt[...], gatt_other[...]], axis=0)
+    hand_out(nn(c_t[...], both).astype(BF16), 3 * each)
+    for i in range(3):
+        both = jnp.concatenate([d[i], d_other[i]], axis=0)
+        total = nn(x_t[...], both)
+        hand_out(total[:mine].astype(BF16), i * each)
         if i != 1:
             at = QB if i == 0 else VB
-            sums[at : at + 1, at_cols] = grad[width : width + 1]
-    keep[:, 4 * each :] = jnp.zeros((CHIPS, 8, cols), BF16)
-    give[:, 4 * each :] = jnp.zeros((CHIPS, 8, cols), BF16)
+            sums[at : at + 1, at_cols] = total[mine : mine + 1]
+    for out in (o0, o1, o2, o3):
+        out[:, 4 * each :] = jnp.zeros((RING, 8, cols), BF16)
 
     @pl.when(step == pl.num_programs(0) - 1)
     def _():
-        mine = spread(SHARDS, width)
+        owned = spread(SHARDS, width)
         rest = column_rest(cols, width, each)
         line = jnp.zeros((SHARDS, cols), F32)
         for i in range(8):
             put = (iota(rest.shape, 0) == rest + i * each).astype(BF16)
-            line += nt(jnp.where(mine, sums[i : i + 1], 0.0).astype(BF16), put)
-        inner = dub.shape[1]
-        put = (iota((cols, inner), 0) == column_rest(cols, inner, inner // SHARDS)).astype(BF16)
-        wide = nt(jnp.where(spread(SHARDS, inner), dub[...], 0.0).astype(BF16), put)
-        both = jnp.concatenate([line[:, None], wide[:, None], jnp.zeros((SHARDS, 6, cols), F32)], axis=1)
-        deal(keep, give, pos, both.reshape(SHARDS * 8, cols).astype(BF16), slice(4 * each, 4 * each + 8), 8)
-
-
-def weight_back(pos, gatt, c, dq, dk, dv, xs, xl, sums_f, dub, dims):
+            line += nt(jnp.where(owned, sums[i : i + 1], 0.0).astype(BF16), put)
+        parts = RING
+        place = width * parts // SHARDS
+        wide_owned = spread(SHARDS // parts, width)
+        put = (iota((cols, width), 0) == column_rest(cols, width, place)).astype(BF16)
+        wide = jnp.concatenate(
+            [nt(jnp.where(wide_owned, sums[8 + j : 9 + j], 0.0).astype(BF16), put) for j in range(parts)], axis=0
+        )
+        small = jnp.concatenate([line[:, None], wide[:, None], jnp.zeros((SHARDS, 6, cols), F32)], axis=1)
+        small = small.reshape(CHIPS, 2, 8, cols)
+        small = jnp.where(on_first, small[:, 0], small[:, 1])
+        hand_out(small.reshape(CHIPS * 8, cols).astype(BF16), 4 * each)
+
+
+def weight_back(pos, gatt, c, d, xs, xl, sums, others):
+    gatt_other, c_other, d_other, xs_other, xl_other, sums_other = others
     rows, width = gatt.shape
     each = width // SHARDS
     step = 256
     cols = pl.BlockSpec((rows, step), lambda g, *_: (0, g))
-    dealt = pl.BlockSpec((CHIPS, 4 * each + 8, step), lambda g, *_: (0, 0, g))
+    three = pl.BlockSpec((3, rows, step), lambda g, *_: (0, 0, g))
+    out = pl.BlockSpec((RING, 4 * each + 8, step), lambda g, *_: (0, 0, g))
     return pl.pallas_call(
-        functools.partial(weight_back_body, dims),
+        weight_back_body,
         grid_spec=pltpu.PrefetchScalarGridSpec(
             num_scalar_prefetch=1,
             grid=(width // step,),
             in_specs=[
-                cols, whole(rows, width), cols, cols, cols,
-                whole(*xs.shape), whole(*xl.shape), whole(8, width), whole(*dub.shape),
+                cols, cols, whole(rows, width), whole(rows, width), three, three,
+                whole(*xs.shape), whole(*xl.shape), whole(*xs.shape), whole(*xl.shape),
+                whole(16, width), whole(16, width),
             ],
-            out_specs=[dealt, dealt],
+            out_specs=[out] * RING,
             scratch_shapes=[
-                pltpu.VMEM((width + 16, rows), BF16), pltpu.VMEM((width, rows), BF16), pltpu.VMEM((8, width), F32),
+                pltpu.VMEM((width // 2 + 16, 2 * rows), BF16), pltpu.VMEM((width // 2, 2 * rows), BF16),
+                pltpu.VMEM((CHIPS, each, step), BF16), pltpu.VMEM((16, width), F32),
             ],
         ),
-        out_shape=[jax.ShapeDtypeStruct((CHIPS, 4 * each + 8, width), BF16)] * 2,
+        out_shape=[jax.ShapeDtypeStruct((RING, 4 * each + 8, width), BF16)] * RING,
         compiler_params=params(BACK_MIB),
         cost_estimate=cost(8 * rows * width * width, 12e6),
         name="weight_back",
-    )(pos, gatt, c, dq, dk, dv, xs, xl, sums_f, dub)
-
-
-def input_back_body(dims, gfs, dq, dk, dv, wq, wk, wv, gs_o, gl_o, total):
+    )(pos, gatt, gatt_other, c, c_other, d, d_other, xs, xl, xs_other, xl_other, sums, sums_other)
+
+
+def input_back_body(dims, gfs, d, wq, wk, wv, gs_o, gl_o, total):
     step = pl.program_id(0)
-    short_rows, width, cols = dims[0], gfs.shape[1], dq.shape[1]
+    short_rows, width, cols = dims[0], gfs.shape[1], d.shape[2]
     part = (
-        nt(dq[...], wq[...].reshape(width, cols))
-        + nt(dk[...], wk[...].reshape(width, cols))
-        + nt(dv[...], wv[...].reshape(width, cols))
+        nt(d[0], wq[...].reshape(width, cols))
+        + nt(d[1], wk[...].reshape(width, cols))
+        + nt(d[2], wv[...].reshape(width, cols))
     )
 
     @pl.when(step == 0)
@@ -666,17 +698,16 @@
         gl_o[...] = total[short_rows:]
 
 
-def input_back(gfs, dq, dk, dv, gathered, dims):
+def input_back(gfs, d, gathered, dims):
     rows, width = gfs.shape
     each = width // SHARDS
     step = 256
     short_rows = dims[0]
-    cols = pl.BlockSpec((rows, step), lambda g: (0, g))
     slab = lambda i: pl.BlockSpec((SHARDS, each, step), lambda g: (0, i, g))
     return pl.pallas_call(
         functools.partial(input_back_body, dims),
         grid=(width // step,),
-        in_specs=[whole(rows, width), cols, cols, cols, slab(0), slab(1), slab(2)],
+        in_specs=[whole(rows, width), pl.BlockSpec((3, rows, step), lambda g: (0, 0, g)), slab(0), slab(1), slab(2)],
         out_specs=[whole(short_rows, width), whole(rows - short_rows, width)],
         scratch_shapes=[pltpu.VMEM((rows, width), F32)],
         out_shape=[
@@ -686,7 +717,7 @@
         compiler_params=params(16),
         cost_estimate=cost(6 * rows * width * width, 12e6),
         name="input_back",
-    )(gfs, dq, dk, dv, gathered, gathered, gathered)
+    )(gfs, d, gathered, gathered, gathered)
 
 
 def pair_sum(keep, got):
@@ -815,18 +846,22 @@
         short_lengths, long_lengths, pos, xs, xl, pieces_a, inner, dims
     )
     unit1, *far_f = lax.optimization_barrier((unit1, *far_f))
-    keep_f, give_f, out_s, out_l, gfs, gatt, sums_f, dub = feed(
+    early = (swap_cores(c), swap_cores(xs), swap_cores(xl))
+    ub, *early = lax.optimization_barrier((ub, *early))
+    keep_f, give_f, out_s, out_l, gfs, gatt, sums = feed(
         short_lengths, long_lengths, pos, unit1, cs, cl, inv1, ub, vecs, both_cores((near_f, *far_f)), dims
     )
-    dq, dk, dv = attention_back(gatt, gathered_a, q, k, v, ps, plong, dims)
+    grads = attention_back(gatt, gathered_a, q, k, v, ps, plong, dims)
+    grads, gatt_other, sums_other = lax.optimization_barrier((grads, swap_cores(gatt), swap_cores(sums)))
+    others = (gatt_other, early[0], swap_cores(grads), *early[1:], sums_other)
     parts_f = pair_sum(keep_f, swap_cores(give_f))
-    dv, *parts_f = lax.optimization_barrier((dv, *parts_f))
+    c, *parts_f = lax.optimization_barrier((c, *parts_f))
     around_f = around(parts_f, 0)
-    keep_a, give_a = weight_back(pos, gatt, c, dq, dk, dv, xs, xl, sums_f, dub, dims)
-    parts_a = pair_sum(keep_a, swap_cores(give_a))
-    gfs, *parts_a = lax.optimization_barrier((gfs, *parts_a))
+    parts_a = weight_back(pos, gatt, c, grads, xs, xl, sums, others)
+    gfs, *both = lax.optimization_barrier((gfs, *parts_a, *around_f[:2]))
+    parts_a, around_f = both[:RING], (*both[RING:], around_f[2])
     around_a = around(parts_a, 0)
-    grad_s, grad_l = input_back(gfs, dq, dk, dv, gathered_a, dims)
+    grad_s, grad_l = input_back(gfs, grads, gathered_a, dims)
     grad_s, *around_a = lax.optimization_barrier((grad_s, *around_a))
     up, down = finish_feed(second_turn(parts_f[0], *around_f), each, inner, tall)
     w_in, w_out, *vectors = finish_attention(second_turn(parts_a[0], *around_a), tall)

time: 216 us -> 222 us (1.028)
  local copies, waits for them, and re-layouts: 4.54 us -> 9.3 us
  other arithmetic: 8.23 us -> 11.2 us
    unnamed x48, local copies, waits for them, and re-layouts: 3.08 us -> 8.24 us
    ppermute x21, waiting for transfers between devices: 44.6 us -> 48.1 us  [around(): lax.ppermute(v[d] if isinstance(v, (list, tuple)) else v, 'shard', turn(d...]
    ppermute x6, waiting for transfers between devices: 9.14 us -> 6.52 us  [second_turn(): lax.ppermute(own, 'rep', [(i, (i + d) % RING) for i in range(RING)])]
    ppermute x10 -> x15, waiting for transfers between devices: 7.66 us -> 6.75 us  [swap_cores(): return lax.ppermute(v, 'shard', [(i, i ^ 1) for i in range(SHARDS)])]
    convert_element_type x2 -> x1, other arithmetic: 6.32 us -> 6.09 us  [pair_sum(): parts.append((keep[at].astype(F32) + got[at].astype(F32)).astype(BF16))]
  transfers between devices with their start and end apart: 37 -> 42, of which waited for: 18 -> 17; matrix products, arithmetic and copies ran while one was open for 2% -> 5% of each run, Pallas kernels for 17% -> 22%
where the time goes in v1:
time: 222 us
  Pallas kernels  89 us (40%)
  waiting for transfers between devices  61.4 us (28%)
  starting transfers between devices  49.7 us (22%)
  other arithmetic  11.2 us (5%)
  local copies, waits for them, and re-layouts  9.3 us (4%)
    ppermute x21, waiting for transfers between devices, around(): lax.ppermute(v[d] if isinstance(v, (list, tuple)) else v, 'shard', turn(d...  48.1 us
    pallas_call x1, Pallas kernels, feed(): pl.pallas_call(functools.partial(feed_body, dims), in_specs=[SCALARS] * 3...  37.3 us
    ppermute x21, starting transfers between devices, around(): lax.ppermute(v[d] if isinstance(v, (list, tuple)) else v, 'shard', turn(d...  36.2 us
    pallas_call x1, Pallas kernels, attention_forward(): pl.pallas_call(functools.partial(attention_forward_body, dims), grid_spec...  19 us
    pallas_call x1, Pallas kernels, weight_back(): pl.pallas_call(weight_back_body, grid_spec=pltpu.PrefetchScalarGridSpec(n...  11.9 us
    pallas_call x1, Pallas kernels, attention_back(): pl.pallas_call(functools.partial(attention_back_body, dims), grid=(width...  11.7 us
    ppermute x6, starting transfers between devices, second_turn(): lax.ppermute(own, 'rep', [(i, (i + d) % RING) for i in range(RING)])  10.3 us
    unnamed x48, local copies, waits for them, and re-layouts  8.24 us
  transfers between devices with their start and end apart: 42, of which 17 were waited for; matrix products, arithmetic and copies ran while one was open for 5% of the time, Pallas kernels for 22%

profile of v1, /device:TPU:0, one launch (start us, length us, event | category | flops | bytes accessed | tf_op | source)
XLA Modules:
  0.0 221.6 jit_solution(12974599094582616894)
XLA Ops:
  0.7 2.0 pack.1
  2.7 4.0 %collective-permute-start.2 = (bf16[296,768]{1,0:T(8,128)(2,1)}, bf16[296,768]{1,0:T(8,128)(2,1)S(1)}, u32[]{:S(2)}, u32[]{:S(2)}) collective-permute-start(bf16[296,768]{1,0:T(8,128)(2,1)} %pack.1), channel_id=1, source_target_pairs={{0,4},{1,17},{2,6},{3,19},{4,0},{5,21},{6,2},{7,23},{8,12},{9,25},... | collective-permute-start | bytes 1363976 | tf_op jit(solution)/shard_map/ppermute | solution.py:754
  6.6 0.7 collective-permute-start.1
  7.3 1.3 collective-permute-start
  8.7 1.0 slice_bitcast_fusion.3
  9.6 3.7 %collective-permute-done.2 = bf16[296,768]{1,0:T(8,128)(2,1)S(1)} collective-permute-done((bf16[296,768]{1,0:T(8,128)(2,1)}, bf16[296,768]{1,0:T(8,128)(2,1)S(1)}, u32[]{:S(2)}, u32[]{:S(2)}) %collective-permute-start.2) | collective-permute-done | bytes 454688 | tf_op jit(solution)/shard_map/ppermute | solution.py:754
  13.4 5.8 %collective-permute-done.1 = bf16[296,768]{1,0:T(8,128)(2,1)S(1)} collective-permute-done((bf16[296,768]{1,0:T(8,128)(2,1)}, bf16[296,768]{1,0:T(8,128)(2,1)S(1)}, u32[]{:S(2)}, u32[]{:S(2)}) %collective-permute-start.1) | collective-permute-done | bytes 454688 | tf_op jit(solution)/shard_map/ppermute | solution.py:754
  19.3 3.1 %collective-permute-start.5 = (bf16[4,104,768]{2,1,0:T(8,128)(2,1)S(1)}, bf16[4,104,768]{2,1,0:T(8,128)(2,1)S(1)}, u32[]{:S(2)}, u32[]{:S(2)}) collective-permute-start(bf16[4,104,768]{2,1,0:T(8,128)(2,1)S(1)} %pad_maximum_fusion.1.p0), channel_id=1, source_target_pairs={{0,16},{1,5},{2,18},{3,7},{4,20},{5,1},{6,22},{7,3},{8,24},{9,13},... | collective-permute-start | bytes 1916936 | tf_op jit(solution)/shard_map/ppermute | solution.py:754
  22.4 1.1 collective-permute-start.4
  23.6 0.9 collective-permute-start.3
  24.5 7.0 %collective-permute-done.5.p3 = bf16[4,104,768]{2,1,0:T(8,128)(2,1)S(1)} collective-permute-done((bf16[4,104,768]{2,1,0:T(8,128)(2,1)S(1)}, bf16[4,104,768]{2,1,0:T(8,128)(2,1)S(1)}, u32[]{:S(2)}, u32[]{:S(2)}) %collective-permute-start.5) | collective-permute-done | bytes 639008 | tf_op jit(solution)/shard_map/ppermute | solution.py:754
  31.6 0.8 copy-done.16
  32.3 6.0 %collective-permute-done.4.p2 = bf16[4,104,768]{2,1,0:T(8,128)(2,1)S(1)} collective-permute-done((bf16[4,104,768]{2,1,0:T(8,128)(2,1)S(1)}, bf16[4,104,768]{2,1,0:T(8,128)(2,1)S(1)}, u32[]{:S(2)}, u32[]{:S(2)}) %collective-permute-start.4) | collective-permute-done | bytes 639008 | tf_op jit(solution)/shard_map/ppermute | solution.py:754
  38.5 0.7 copy-done.17
  39.2 2.0 collective-permute-start.12
  41.2 2.0 collective-permute-start.11
  43.4 0.5 collective-permute-start.15
  44.3 0.6 pad_add_fusion.pos
  44.9 0.7 collective-permute-done.7.p5
  45.8 0.7 copy-done.21
  46.5 19.0 %attention_forward.1 = (bf16[640,768]{1,0:T(8,128)(2,1)}, bf16[640,768]{1,0:T(8,128)(2,1)}, bf16[640,768]{1,0:T(8,128)(2,1)}, bf16[640,768]{1,0:T(8,128)(2,1)}, ...) custom-call(s32[2]{0:T(128)} %slen.3, s32[2]{0:T(128)} %llen.3, ...), custom_call_target="tpu_custom_call" | custom-call | flops 3019898880 | bytes 20000000 | tf_op jit(solution)/shard_map/attention_forward/pallas_call | solution.py:273
  65.7 4.0 %collective-permute-done.11.p2 = bf16[4,8,24,768]{3,2,1,0:T(8,128)(2,1)} collective-permute-done((bf16[4,8,24,768]{3,2,1,0:T(8,128)(2,1)S(1)}, bf16[4,8,24,768]{3,2,1,0:T(8,128)(2,1)}, u32[]{:S(2)}, u32[]{:S(2)}) %collective-permute-start.11) | collective-permute-done | bytes 1179680 | tf_op jit(solution)/shard_map/ppermute | solution.py:754
  69.7 0.5 collective-permute-start.18
  70.3 0.9 copy-done.9
  71.6 5.6 %collective-permute-done.13.c_other = bf16[640,768]{1,0:T(8,128)(2,1)S(1)} collective-permute-done((bf16[640,768]{1,0:T(8,128)(2,1)}, bf16[640,768]{1,0:T(8,128)(2,1)S(1)}, u32[]{:S(2)}, u32[]{:S(2)}) %collective-permute-start.13) | collective-permute-done | bytes 983072 | tf_op jit(solution)/shard_map/ppermute | solution.py:750
  77.6 0.6 copy-done.14
  78.2 0.5 copy-done.15
  78.7 37.3 %feed.1 = (bf16[16,8,24,768]{3,2,1,0:T(8,128)(2,1)}, bf16[16,8,24,768]{3,2,1,0:T(8,128)(2,1)}, bf16[128,768]{1,0:T(8,128)(2,1)}, bf16[512,768]{1,0:T(8,128)(2,1)...) custom-call(s32[2]{0:T(128)} %slen.3, s32[2]{0:T(128)} %llen.3, s32[3]{0:T(128)} %pad_add_fusion.pos, ...), custom_call_target="tpu_custom_call" | custom-call | flops 18119393280 | bytes 30000000 | tf_op jit(solution)/shard_map/feed/pallas_call | solution.py:490
  116.7 11.7 %attention_back.1.d = bf16[3,640,768]{2,1,0:T(8,128)(2,1)} custom-call(bf16[640,768]{1,0:T(8,128)(2,1)} %get-tuple-element.98.gatt, bf16[32,104,768]{2,1,0:T(8,128)(2,1)} %get-tuple-element.99.wo_block.wq.wk.wv, bf16[640,768]{1,0:T(8,128)(2,1)} %get-tuple-element.100.q, bf16[640,768]{1,0:T(8,128)(2,1)} %get-tuple-element.101.k, ...), custom_call_target="tpu_custom_call" | custom-call | flops 3019898880 | bytes 15000000 | tf_op jit(solution)/shard_map/attention_back/pallas_call | solution.py:554
  128.5 0.5 collective-permute-start.23
  129.0 2.1 copy-done.2
  131.1 6.1 %add_convert_fusion = (bf16[4,8,24,768]{3,2,1,0:T(8,128)(2,1)}, bf16[4,8,24,768]{3,2,1,0:T(8,128)(2,1)}, bf16[4,8,24,768]{3,2,1,0:T(8,128)(2,1)}, bf16[4,8,24,768]{3,2,1,0:T(8,128)(2,1)}) fusion(bf16[16,8,24,768]{3,2,1,0:T(8,128)(2,1)} %copy-done.2, bf16[16,8,24,768]{3,2,1,0:T(8,128)(2,1)} %get-tuple-element.107), kind=kLoop, calls=%fused_computation | loop fusion | flops 9437184 | bytes 14155776 | tf_op jit(solution)/shard_map/convert_element_type | solution.py:727
  137.2 1.4 collective-permute-start.24
  138.6 1.9 collective-permute-start.25
  140.5 0.8 collective-permute-start.35
  141.4 11.9 %weight_back.1 = (bf16[4,104,768]{2,1,0:T(8,128)(2,1)}, bf16[4,104,768]{2,1,0:T(8,128)(2,1)}, bf16[4,104,768]{2,1,0:T(8,128)(2,1)}, bf16[4,104,768]{2,1,0:T(8,128)(2,1)}) custom-call(s32[3]{0:T(128)} %pad_add_fusion.pos, bf16[640,768]{1,0:T(8,128)(2,1)} %get-tuple-element.98.gatt, bf16[640,768]{1,0:T(8,128)(2,1)} %copy-done.7, ...), custom_call_target="tpu_custom_call" | custom-call | flops 3019898880 | bytes 12000000 | tf_op jit(solution)/shard_map/weight_back/pallas_call | solution.py:655
  153.2 1.8 collective-permute-done.24
  155.0 12.2 %collective-permute-done.25 = bf16[4,8,24,768]{3,2,1,0:T(8,128)(2,1)} collective-permute-done((bf16[4,8,24,768]{3,2,1,0:T(8,128)(2,1)}, bf16[4,8,24,768]{3,2,1,0:T(8,128)(2,1)}, u32[]{:S(2)}, u32[]{:S(2)}) %collective-permute-start.25) | collective-permute-done | bytes 1179680 | tf_op jit(solution)/shard_map/ppermute | solution.py:754
  167.2 3.7 %collective-permute-start.27 = (bf16[4,104,768]{2,1,0:T(8,128)(2,1)}, bf16[4,104,768]{2,1,0:T(8,128)(2,1)S(1)}, u32[]{:S(2)}, u32[]{:S(2)}) collective-permute-start(bf16[4,104,768]{2,1,0:T(8,128)(2,1)} %get-tuple-element.124), channel_id=1, source_target_pairs={{0,24},{1,7},{2,26},{3,1},{4,28},{5,3},{6,30},{7,5},{8,0},{9,15},{... | collective-permute-start | bytes 1916936 | tf_op jit(solution)/shard_map/ppermute | solution.py:754
  170.9 1.5 collective-permute-start.28
  172.4 2.4 %fusion.5 = (bf16[8,24,768]{2,1,0:T(8,128)(2,1)S(1)}, bf16[8,24,768]{2,1,0:T(8,128)(2,1)S(1)}, bf16[8,24,768]{2,1,0:T(8,128)(2,1)S(1)}) fusion(bf16[4,8,24,768]{3,2,1,0:T(8,128)(2,1)} %collective-permute-done.35, bf16[4,8,24,768]{3,2,1,0:T(8,128)(2,1)} %collective-permute-done.25, bf16[4,8,24,768]{3,2,1,0:T(8,128)(2,1)} %collective-permute-done.24, ...), kind=kLoop, calls=%fused_computation.21 | loop fusion | flops 3538944 | bytes 4423680 | tf_op jit(solution)/shard_map/convert_element_type | solution.py:762
  174.7 2.5 %collective-permute-start.36 = (bf16[8,24,768]{2,1,0:T(8,128)(2,1)S(1)}, bf16[8,24,768]{2,1,0:T(8,128)(2,1)S(1)}, u32[]{:S(2)}, u32[]{:S(2)}) collective-permute-start(bf16[8,24,768]{2,1,0:T(8,128)(2,1)S(1)} %get-tuple-element.153), channel_id=1, source_target_pairs={{0,4},{1,17},{2,6},{3,19},{4,0},{5,21},{6,2},{7,23},{8,12},{9,25},... | collective-permute-start | bytes 884744 | tf_op jit(solution)/shard_map/ppermute | solution.py:754
  177.3 1.2 collective-permute-start.38
  178.4 3.0 %collective-permute-done.26 = bf16[4,104,768]{2,1,0:T(8,128)(2,1)S(1)} collective-permute-done((bf16[4,104,768]{2,1,0:T(8,128)(2,1)}, bf16[4,104,768]{2,1,0:T(8,128)(2,1)S(1)}, u32[]{:S(2)}, u32[]{:S(2)}) %collective-permute-start.26) | collective-permute-done | bytes 639008 | tf_op jit(solution)/shard_map/ppermute | solution.py:754
  181.4 1.3 collective-permute-start.37
  182.7 1.5 copy-done.1
  184.3 5.4 %input_back.1 = (f32[128,768]{1,0:T(8,128)}, f32[512,768]{1,0:T(8,128)}) custom-call(f32[640,768]{1,0:T(8,128)S(1)} %copy-done.1, bf16[3,640,768]{2,1,0:T(8,128)(2,1)S(1)} %copy-done, bf16[32,104,768]{2,1,0:T(8,128)(2,1)S(1)} %bitcast.64, bf16[32,104,768]{2,1,0:T(8,128)(2,1)S(1)} %bitcast.64, bf16[32,104,768]{2,1,0:T(8,128)(2,1)S(1)} %bitcast.64), custom_call_target="tpu_custom_call" | custom-call | flops 2264924160 | bytes 12000000 | tf_op jit(solution)/shard_map/input_back/pallas_call | solution.py:707
  189.6 1.6 collective-permute-done.27
  191.2 3.1 %collective-permute-done.28 = bf16[4,104,768]{2,1,0:T(8,128)(2,1)S(1)} collective-permute-done((bf16[4,104,768]{2,1,0:T(8,128)(2,1)}, bf16[4,104,768]{2,1,0:T(8,128)(2,1)S(1)}, u32[]{:S(2)}, u32[]{:S(2)}) %collective-permute-start.28) | collective-permute-done | bytes 639008 | tf_op jit(solution)/shard_map/ppermute | solution.py:754
  194.6 4.8 %collective-permute-start.29 = (bf16[104,768]{1,0:T(8,128)(2,1)S(1)}, bf16[104,768]{1,0:T(8,128)(2,1)S(1)}, u32[]{:S(2)}, u32[]{:S(2)}) collective-permute-start(bf16[104,768]{1,0:T(8,128)(2,1)S(1)} %get-tuple-element.156), channel_id=1, source_target_pairs={{0,4},{1,17},{2,6},{3,19},{4,0},{5,21},{6,2},{7,23},{8,12},{9,25},... | collective-permute-start | bytes 479240 | tf_op jit(solution)/shard_map/ppermute | solution.py:754
  199.3 2.0 collective-permute-start.30
  201.4 1.5 fusion.1.own
  202.9 3.3 %collective-permute-start.41 = (bf16[8,24,768]{2,1,0:T(8,128)(2,1)S(1)}, bf16[8,24,768]{2,1,0:T(8,128)(2,1)S(1)}, u32[]{:S(2)}, u32[]{:S(2)}) collective-permute-start(bf16[8,24,768]{2,1,0:T(8,128)(2,1)S(1)} %fusion.1.own), channel_id=1, source_target_pairs={{0,64},{32,96},{64,0},{96,32},{1,65},{33,97},{65,1},{97,33},{2,66}... | collective-permute-start | bytes 884744 | tf_op jit(solution)/shard_map/ppermute | solution.py:764
  206.2 1.1 collective-permute-start.40
  207.2 1.0 collective-permute-start.39
  208.3 0.9 collective-permute-start.34
  209.2 2.5 %collective-permute-start.33 = (bf16[104,768]{1,0:T(8,128)(2,1)S(1)}, bf16[104,768]{1,0:T(8,128)(2,1)S(1)}, u32[]{:S(2)}, u32[]{:S(2)}) collective-permute-start(bf16[104,768]{1,0:T(8,128)(2,1)S(1)} %fusion.3.own), channel_id=1, source_target_pairs={{0,96},{32,0},{64,32},{96,64},{1,97},{33,1},{65,33},{97,65},{2,98}... | collective-permute-start | bytes 479240 | tf_op jit(solution)/shard_map/ppermute | solution.py:764
  211.8 2.1 collective-permute-done.41.far
  213.9 1.6 collective-permute-start.32
  215.5 1.9 collective-permute-done.40.right
  217.4 1.5 collective-permute-done.39.left
  218.9 0.9 finish_feed.1
  219.8 1.0 collective-permute-done.33.right
  220.8 0.8 finish_attention.1
  (94 shorter events, 3.3 us)
Async XLA Ops:
  2.7 10.7 %collective-permute-start.2 = (bf16[296,768]{1,0:T(8,128)(2,1)}, bf16[296,768]{1,0:T(8,128)(2,1)S(1)}, u32[]{:S(2)}, u32[]{:S(2)}) collective-permute-start(bf16[296,768]{1,0:T(8,128)(2,1)} %pack.1), channel_id=1, source_target_pairs={{0,4},{1,17},{2,6},{3,19},{4,0},{5,21},{6,2},{7,23},{8,12},{9,25},... | collective-permute-start | bytes 1363976 | tf_op jit(solution)/shard_map/ppermute | solution.py:754
  6.6 12.6 %collective-permute-start.1 = (bf16[296,768]{1,0:T(8,128)(2,1)}, bf16[296,768]{1,0:T(8,128)(2,1)S(1)}, u32[]{:S(2)}, u32[]{:S(2)}) collective-permute-start(bf16[296,768]{1,0:T(8,128)(2,1)} %pack.1), channel_id=1, source_target_pairs={{0,6},{1,25},{2,0},{3,27},{4,2},{5,29},{6,4},{7,31},{8,14},{9,1},{... | collective-permute-start | bytes 1363976 | tf_op jit(solution)/shard_map/ppermute | solution.py:754
  7.3 11.9 %collective-permute-start = (bf16[296,768]{1,0:T(8,128)(2,1)}, bf16[296,768]{1,0:T(8,128)(2,1)S(1)}, u32[]{:S(2)}, u32[]{:S(2)}) collective-permute-start(bf16[296,768]{1,0:T(8,128)(2,1)} %pack.1), channel_id=1, source_target_pairs={{0,2},{1,9},{2,4},{3,11},{4,6},{5,13},{6,0},{7,15},{8,10},{9,17},{... | collective-permute-start | bytes 1363976 | tf_op jit(solution)/shard_map/ppermute | solution.py:754
  9.6 21.8 %copy-start.3 = (bf16[296,768]{1,0:T(8,128)(2,1)S(1)}, bf16[296,768]{1,0:T(8,128)(2,1)}, u32[]{:S(2)}) copy-start(bf16[296,768]{1,0:T(8,128)(2,1)} %pack.1) | copy-start | bytes 1363972
  13.4 18.1 %copy-start.4 = (bf16[296,768]{1,0:T(8,128)(2,1)}, bf16[296,768]{1,0:T(8,128)(2,1)S(1)}, u32[]{:S(2)}) copy-start(bf16[296,768]{1,0:T(8,128)(2,1)S(1)} %collective-permute-done.2) | copy-start | bytes 1363972
  19.3 12.2 %copy-start.11 = (bf16[4,104,768]{2,1,0:T(8,128)(2,1)}, bf16[4,104,768]{2,1,0:T(8,128)(2,1)S(1)}, u32[]{:S(2)}) copy-start(bf16[4,104,768]{2,1,0:T(8,128)(2,1)S(1)} %pad_maximum_fusion.1.p0) | copy-start | bytes 1916932
  19.3 12.1 %collective-permute-start.5 = (bf16[4,104,768]{2,1,0:T(8,128)(2,1)S(1)}, bf16[4,104,768]{2,1,0:T(8,128)(2,1)S(1)}, u32[]{:S(2)}, u32[]{:S(2)}) collective-permute-start(bf16[4,104,768]{2,1,0:T(8,128)(2,1)S(1)} %pad_maximum_fusion.1.p0), channel_id=1, source_target_pairs={{0,16},{1,5},{2,18},{3,7},{4,20},{5,1},{6,22},{7,3},{8,24},{9,13},... | collective-permute-start | bytes 1916936 | tf_op jit(solution)/shard_map/ppermute | solution.py:754
  22.4 15.9 %collective-permute-start.4 = (bf16[4,104,768]{2,1,0:T(8,128)(2,1)S(1)}, bf16[4,104,768]{2,1,0:T(8,128)(2,1)S(1)}, u32[]{:S(2)}, u32[]{:S(2)}) collective-permute-start(bf16[4,104,768]{2,1,0:T(8,128)(2,1)S(1)} %pad_maximum_fusion.1.p0), channel_id=1, source_target_pairs={{0,24},{1,7},{2,26},{3,1},{4,28},{5,3},{6,30},{7,5},{8,0},{9,15},{... | collective-permute-start | bytes 1916936 | tf_op jit(solution)/shard_map/ppermute | solution.py:754
  23.6 17.6 %collective-permute-start.6 = (bf16[4,104,768]{2,1,0:T(8,128)(2,1)S(1)}, bf16[4,104,768]{2,1,0:T(8,128)(2,1)S(1)}, u32[]{:S(2)}, u32[]{:S(2)}) collective-permute-start(bf16[4,104,768]{2,1,0:T(8,128)(2,1)S(1)} %pad_maximum_fusion.1.p0), channel_id=1, source_target_pairs={{0,1},{1,0},{2,3},{3,2},{4,5},{5,4},{6,7},{7,6},{8,9},{9,8},{10,11... | collective-permute-start | bytes 1916936 | tf_op jit(solution)/shard_map/ppermute | solution.py:750
  23.6 19.7 %collective-permute-start.3 = (bf16[4,104,768]{2,1,0:T(8,128)(2,1)S(1)}, bf16[4,104,768]{2,1,0:T(8,128)(2,1)}, u32[]{:S(2)}, u32[]{:S(2)}) collective-permute-start(bf16[4,104,768]{2,1,0:T(8,128)(2,1)S(1)} %pad_maximum_fusion.1.p0), channel_id=1, source_target_pairs={{0,8},{1,3},{2,10},{3,5},{4,12},{5,7},{6,14},{7,1},{8,16},{9,11},{... | collective-permute-start | bytes 1916936 | tf_op jit(solution)/shard_map/ppermute | solution.py:754
  31.4 11.8 %collective-permute-start.9 = (bf16[4,104,768]{2,1,0:T(8,128)(2,1)S(1)}, bf16[4,104,768]{2,1,0:T(8,128)(2,1)S(1)}, u32[]{:S(2)}, u32[]{:S(2)}) collective-permute-start(bf16[4,104,768]{2,1,0:T(8,128)(2,1)S(1)} %collective-permute-done.5.p3), channel_id=1, source_target_pairs={{0,1},{1,0},{2,3},{3,2},{4,5},{5,4},{6,7},{7,6},{8,9},{9,8},{10,11... | collective-permute-start | bytes 1916936 | tf_op jit(solution)/shard_map/ppermute | solution.py:750
  31.5 6.8 %slice-start.2 = ((bf16[296,768]{1,0:T(8,128)(2,1)}), bf16[192,768]{1,0:T(8,128)(2,1)S(1)}, s32[]{:S(2)}) async-start(bf16[296,768]{1,0:T(8,128)(2,1)} %copy-done.4), calls=%async_computation.2 | async-start | bytes 589824 | tf_op jit(solution)/shard_map/slice | solution.py:840
  38.3 0.9 copy-start.17
  38.3 5.1 %collective-permute-start.8 = (bf16[4,104,768]{2,1,0:T(8,128)(2,1)S(1)}, bf16[4,104,768]{2,1,0:T(8,128)(2,1)S(1)}, u32[]{:S(2)}, u32[]{:S(2)}) collective-permute-start(bf16[4,104,768]{2,1,0:T(8,128)(2,1)S(1)} %collective-permute-done.4.p2), channel_id=1, source_target_pairs={{0,1},{1,0},{2,3},{3,2},{4,5},{5,4},{6,7},{7,6},{8,9},{9,8},{10,11... | collective-permute-start | bytes 1916936 | tf_op jit(solution)/shard_map/ppermute | solution.py:750
  38.3 5.1 %copy-start.8 = (bf16[2,256,768]{2,1,0:T(8,128)(2,1)S(1)}, bf16[2,256,768]{2,1,0:T(8,128)(2,1)}, u32[]{:S(2)}) copy-start(bf16[2,256,768]{2,1,0:T(8,128)(2,1)} %param.20) | copy-start | bytes 2359300
  39.2 26.3 %copy-start.5 = (bf16[4,8,24,768]{3,2,1,0:T(8,128)(2,1)}, bf16[4,8,24,768]{3,2,1,0:T(8,128)(2,1)S(1)}, u32[]{:S(2)}) copy-start(bf16[4,8,24,768]{3,2,1,0:T(8,128)(2,1)S(1)} %pad_maximum_fusion.p0) | copy-start | bytes 3538948
  39.2 26.3 %collective-permute-start.12 = (bf16[4,8,24,768]{3,2,1,0:T(8,128)(2,1)S(1)}, bf16[4,8,24,768]{3,2,1,0:T(8,128)(2,1)}, u32[]{:S(2)}, u32[]{:S(2)}) collective-permute-start(bf16[4,8,24,768]{3,2,1,0:T(8,128)(2,1)S(1)} %pad_maximum_fusion.p0), channel_id=1, source_target_pairs={{0,16},{1,5},{2,18},{3,7},{4,20},{5,1},{6,22},{7,3},{8,24},{9,13},... | collective-permute-start | bytes 3538952 | tf_op jit(solution)/shard_map/ppermute | solution.py:754
  41.2 2.7 %copy-start.18 = (bf16[4,104,768]{2,1,0:T(8,128)(2,1)}, bf16[4,104,768]{2,1,0:T(8,128)(2,1)S(1)}, u32[]{:S(2)}) copy-start(bf16[4,104,768]{2,1,0:T(8,128)(2,1)S(1)} %collective-permute-done.6.p4) | copy-start | bytes 1916932
  41.2 28.4 %collective-permute-start.11 = (bf16[4,8,24,768]{3,2,1,0:T(8,128)(2,1)S(1)}, bf16[4,8,24,768]{3,2,1,0:T(8,128)(2,1)}, u32[]{:S(2)}, u32[]{:S(2)}) collective-permute-start(bf16[4,8,24,768]{3,2,1,0:T(8,128)(2,1)S(1)} %pad_maximum_fusion.p0), channel_id=1, source_target_pairs={{0,24},{1,7},{2,26},{3,1},{4,28},{5,3},{6,30},{7,5},{8,0},{9,15},{... | collective-permute-start | bytes 3538952 | tf_op jit(solution)/shard_map/ppermute | solution.py:754
  43.3 26.4 %collective-permute-start.10 = (bf16[4,8,24,768]{3,2,1,0:T(8,128)(2,1)S(1)}, bf16[4,8,24,768]{3,2,1,0:T(8,128)(2,1)}, u32[]{:S(2)}, u32[]{:S(2)}) collective-permute-start(bf16[4,8,24,768]{3,2,1,0:T(8,128)(2,1)S(1)} %pad_maximum_fusion.p0), channel_id=1, source_target_pairs={{0,8},{1,3},{2,10},{3,5},{4,12},{5,7},{6,14},{7,1},{8,16},{9,11},{... | collective-permute-start | bytes 3538952 | tf_op jit(solution)/shard_map/ppermute | solution.py:754
  43.3 2.4 %collective-permute-start.7 = (bf16[4,104,768]{2,1,0:T(8,128)(2,1)}, bf16[4,104,768]{2,1,0:T(8,128)(2,1)S(1)}, u32[]{:S(2)}, u32[]{:S(2)}) collective-permute-start(bf16[4,104,768]{2,1,0:T(8,128)(2,1)} %collective-permute-done.3.p1), channel_id=1, source_target_pairs={{0,1},{1,0},{2,3},{3,2},{4,5},{5,4},{6,7},{7,6},{8,9},{9,8},{10,11... | collective-permute-start | bytes 1916936 | tf_op jit(solution)/shard_map/ppermute | solution.py:750
  43.4 0.9 copy-start.20
  43.4 26.9 %collective-permute-start.15 = (bf16[512,768]{1,0:T(8,128)(2,1)S(1)}, bf16[512,768]{1,0:T(8,128)(2,1)S(1)}, u32[]{:S(2)}, u32[]{:S(2)}) collective-permute-start(bf16[512,768]{1,0:T(8,128)(2,1)S(1)} %bitcast.71), channel_id=1, source_target_pairs={{0,1},{1,0},{2,3},{3,2},{4,5},{5,4},{6,7},{7,6},{8,9},{9,8},{10,11... | collective-permute-start | bytes 2359304 | tf_op jit(solution)/shard_map/ppermute | solution.py:750
  45.6 24.5 %collective-permute-start.14 = (bf16[128,768]{1,0:T(8,128)(2,1)}, bf16[128,768]{1,0:T(8,128)(2,1)S(1)}, u32[]{:S(2)}, u32[]{:S(2)}) collective-permute-start(bf16[128,768]{1,0:T(8,128)(2,1)} %bitcast.72), channel_id=1, source_target_pairs={{0,1},{1,0},{2,3},{3,2},{4,5},{5,4},{6,7},{7,6},{8,9},{9,8},{10,11... | collective-permute-start | bytes 589832 | tf_op jit(solution)/shard_map/ppermute | solution.py:750
  65.5 11.7 %collective-permute-start.16 = (bf16[4,8,24,768]{3,2,1,0:T(8,128)(2,1)S(1)}, bf16[4,8,24,768]{3,2,1,0:T(8,128)(2,1)S(1)}, u32[]{:S(2)}, u32[]{:S(2)}) collective-permute-start(bf16[4,8,24,768]{3,2,1,0:T(8,128)(2,1)S(1)} %pad_maximum_fusion.p0), channel_id=1, source_target_pairs={{0,1},{1,0},{2,3},{3,2},{4,5},{5,4},{6,7},{7,6},{8,9},{9,8},{10,11... | collective-permute-start | bytes 3538952 | tf_op jit(solution)/shard_map/ppermute | solution.py:750
  69.7 7.5 %collective-permute-start.17 = (bf16[4,8,24,768]{3,2,1,0:T(8,128)(2,1)}, bf16[4,8,24,768]{3,2,1,0:T(8,128)(2,1)S(1)}, u32[]{:S(2)}, u32[]{:S(2)}) collective-permute-start(bf16[4,8,24,768]{3,2,1,0:T(8,128)(2,1)} %collective-permute-done.10.p1), channel_id=1, source_target_pairs={{0,1},{1,0},{2,3},{3,2},{4,5},{5,4},{6,7},{7,6},{8,9},{9,8},{10,11... | collective-permute-start | bytes 3538952 | tf_op jit(solution)/shard_map/ppermute | solution.py:750
  69.7 7.5 %collective-permute-start.18 = (bf16[4,8,24,768]{3,2,1,0:T(8,128)(2,1)}, bf16[4,8,24,768]{3,2,1,0:T(8,128)(2,1)}, u32[]{:S(2)}, u32[]{:S(2)}) collective-permute-start(bf16[4,8,24,768]{3,2,1,0:T(8,128)(2,1)} %collective-permute-done.11.p2), channel_id=1, source_target_pairs={{0,1},{1,0},{2,3},{3,2},{4,5},{5,4},{6,7},{7,6},{8,9},{9,8},{10,11... | collective-permute-start | bytes 3538952 | tf_op jit(solution)/shard_map/ppermute | solution.py:750
  70.2 45.8 %copy-start.12 = (bf16[128,768]{1,0:T(8,128)(2,1)}, bf16[128,768]{1,0:T(8,128)(2,1)S(1)}, u32[]{:S(2)}) copy-start(bf16[128,768]{1,0:T(8,128)(2,1)S(1)} %collective-permute-done.14.xs_other) | copy-start | bytes 589828
  70.2 7.5 %collective-permute-start.19 = (bf16[4,8,24,768]{3,2,1,0:T(8,128)(2,1)}, bf16[4,8,24,768]{3,2,1,0:T(8,128)(2,1)}, u32[]{:S(2)}, u32[]{:S(2)}) collective-permute-start(bf16[4,8,24,768]{3,2,1,0:T(8,128)(2,1)} %collective-permute-done.12.p3), channel_id=1, source_target_pairs={{0,1},{1,0},{2,3},{3,2},{4,5},{5,4},{6,7},{7,6},{8,9},{9,8},{10,11... | collective-permute-start | bytes 3538952 | tf_op jit(solution)/shard_map/ppermute | solution.py:750
  70.3 0.9 copy-start.9
  71.2 6.0 %collective-permute-start.13 = (bf16[640,768]{1,0:T(8,128)(2,1)}, bf16[640,768]{1,0:T(8,128)(2,1)S(1)}, u32[]{:S(2)}, u32[]{:S(2)}) collective-permute-start(bf16[640,768]{1,0:T(8,128)(2,1)} %get-tuple-element.109.c), channel_id=1, source_target_pairs={{0,1},{1,0},{2,3},{3,2},{4,5},{5,4},{6,7},{7,6},{8,9},{9,8},{10,11... | collective-permute-start | bytes 2949128 | tf_op jit(solution)/shard_map/ppermute | solution.py:750
  77.2 38.8 %copy-start.6 = (bf16[640,768]{1,0:T(8,128)(2,1)}, bf16[640,768]{1,0:T(8,128)(2,1)S(1)}, u32[]{:S(2)}) copy-start(bf16[640,768]{1,0:T(8,128)(2,1)S(1)} %collective-permute-done.13.c_other) | copy-start | bytes 2949124
  77.2 1.0 copy-start.14
  77.2 1.5 copy-start.15
  116.0 13.0 %collective-permute-start.22 = (bf16[16,8,24,768]{3,2,1,0:T(8,128)(2,1)}, bf16[16,8,24,768]{3,2,1,0:T(8,128)(2,1)S(1)}, u32[]{:S(2)}, u32[]{:S(2)}) collective-permute-start(bf16[16,8,24,768]{3,2,1,0:T(8,128)(2,1)} %get-tuple-element.108), channel_id=1, source_target_pairs={{0,1},{1,0},{2,3},{3,2},{4,5},{5,4},{6,7},{7,6},{8,9},{9,8},{10,11... | collective-permute-start | bytes 14155784 | tf_op jit(solution)/shard_map/ppermute | solution.py:750
  116.2 12.3 %collective-permute-start.20 = (bf16[640,768]{1,0:T(8,128)(2,1)}, bf16[640,768]{1,0:T(8,128)(2,1)S(1)}, u32[]{:S(2)}, u32[]{:S(2)}) collective-permute-start(bf16[640,768]{1,0:T(8,128)(2,1)} %get-tuple-element.98.gatt), channel_id=1, source_target_pairs={{0,1},{1,0},{2,3},{3,2},{4,5},{5,4},{6,7},{7,6},{8,9},{9,8},{10,11... | collective-permute-start | bytes 2949128 | tf_op jit(solution)/shard_map/ppermute | solution.py:750
  116.6 11.9 %collective-permute-start.21 = (f32[16,768]{1,0:T(8,128)}, f32[16,768]{1,0:T(8,128)S(1)}, u32[]{:S(2)}, u32[]{:S(2)}) collective-permute-start(f32[16,768]{1,0:T(8,128)} %get-tuple-element.105.sums_own), channel_id=1, source_target_pairs={{0,1},{1,0},{2,3},{3,2},{4,5},{5,4},{6,7},{7,6},{8,9},{9,8},{10,11... | collective-permute-start | bytes 147464 | tf_op jit(solution)/shard_map/ppermute | solution.py:750
  128.5 8.7 %copy-start.13 = (f32[16,768]{1,0:T(8,128)}, f32[16,768]{1,0:T(8,128)S(1)}, u32[]{:S(2)}) copy-start(f32[16,768]{1,0:T(8,128)S(1)} %collective-permute-done.21.sums_other) | copy-start | bytes 147460
  128.5 8.7 %copy-start.7 = (bf16[640,768]{1,0:T(8,128)(2,1)}, bf16[640,768]{1,0:T(8,128)(2,1)S(1)}, u32[]{:S(2)}) copy-start(bf16[640,768]{1,0:T(8,128)(2,1)S(1)} %collective-permute-done.20.gatt_other) | copy-start | bytes 2949124
  128.5 12.9 %collective-permute-start.23 = (bf16[3,640,768]{2,1,0:T(8,128)(2,1)}, bf16[3,640,768]{2,1,0:T(8,128)(2,1)}, u32[]{:S(2)}, u32[]{:S(2)}) collective-permute-start(bf16[3,640,768]{2,1,0:T(8,128)(2,1)} %attention_back.1.d), channel_id=1, source_target_pairs={{0,1},{1,0},{2,3},{3,2},{4,5},{5,4},{6,7},{7,6},{8,9},{9,8},{10,11... | collective-permute-start | bytes 8847368 | tf_op jit(solution)/shard_map/ppermute | solution.py:750
  129.0 2.1 copy-start.2
  131.1 51.6 %slice-start = ((s8[5111808]{0:T(1024)(128)(4,1)}), s8[4194304]{0:T(1024)(128)(4,1)S(1)}, s32[]{:S(2)}) async-start(s8[5111808]{0:T(1024)(128)(4,1)} %bitcast.63), calls=%async_computation | async-start | bytes 8388608
  137.2 45.5 %slice-start.1 = ((s8[5111808]{0:T(1024)(128)(4,1)}), s8[917504]{0:T(1024)(128)(4,1)S(1)}, s32[]{:S(2)}) async-start(s8[5111808]{0:T(1024)(128)(4,1)} %bitcast.63), calls=%async_computation.1 | async-start | bytes 1835008
  137.2 17.8 %collective-permute-start.24 = (bf16[4,8,24,768]{3,2,1,0:T(8,128)(2,1)}, bf16[4,8,24,768]{3,2,1,0:T(8,128)(2,1)}, u32[]{:S(2)}, u32[]{:S(2)}) collective-permute-start(bf16[4,8,24,768]{3,2,1,0:T(8,128)(2,1)} %get-tuple-element.119), channel_id=1, source_target_pairs={{0,8},{1,3},{2,10},{3,5},{4,12},{5,7},{6,14},{7,1},{8,16},{9,11},{... | collective-permute-start | bytes 3538952 | tf_op jit(solution)/shard_map/ppermute | solution.py:754
  138.6 28.6 %collective-permute-start.25 = (bf16[4,8,24,768]{3,2,1,0:T(8,128)(2,1)}, bf16[4,8,24,768]{3,2,1,0:T(8,128)(2,1)}, u32[]{:S(2)}, u32[]{:S(2)}) collective-permute-start(bf16[4,8,24,768]{3,2,1,0:T(8,128)(2,1)} %get-tuple-element.120), channel_id=1, source_target_pairs={{0,24},{1,7},{2,26},{3,1},{4,28},{5,3},{6,30},{7,5},{8,0},{9,15},{... | collective-permute-start | bytes 3538952 | tf_op jit(solution)/shard_map/ppermute | solution.py:754
  140.5 31.8 %collective-permute-start.35 = (bf16[4,8,24,768]{3,2,1,0:T(8,128)(2,1)}, bf16[4,8,24,768]{3,2,1,0:T(8,128)(2,1)}, u32[]{:S(2)}, u32[]{:S(2)}) collective-permute-start(bf16[4,8,24,768]{3,2,1,0:T(8,128)(2,1)} %get-tuple-element.140), channel_id=1, source_target_pairs={{0,16},{1,5},{2,18},{3,7},{4,20},{5,1},{6,22},{7,3},{8,24},{9,13},... | collective-permute-start | bytes 3538952 | tf_op jit(solution)/shard_map/ppermute | solution.py:754
  167.2 15.5 %copy-start = (bf16[3,640,768]{2,1,0:T(8,128)(2,1)S(1)}, bf16[3,640,768]{2,1,0:T(8,128)(2,1)}, u32[]{:S(2)}) copy-start(bf16[3,640,768]{2,1,0:T(8,128)(2,1)} %attention_back.1.d) | copy-start | bytes 8847364
  167.2 14.2 %collective-permute-start.26 = (bf16[4,104,768]{2,1,0:T(8,128)(2,1)}, bf16[4,104,768]{2,1,0:T(8,128)(2,1)S(1)}, u32[]{:S(2)}, u32[]{:S(2)}) collective-permute-start(bf16[4,104,768]{2,1,0:T(8,128)(2,1)} %get-tuple-element.123), channel_id=1, source_target_pairs={{0,8},{1,3},{2,10},{3,5},{4,12},{5,7},{6,14},{7,1},{8,16},{9,11},{... | collective-permute-start | bytes 1916936 | tf_op jit(solution)/shard_map/ppermute | solution.py:754
  167.2 24.0 %collective-permute-start.27 = (bf16[4,104,768]{2,1,0:T(8,128)(2,1)}, bf16[4,104,768]{2,1,0:T(8,128)(2,1)S(1)}, u32[]{:S(2)}, u32[]{:S(2)}) collective-permute-start(bf16[4,104,768]{2,1,0:T(8,128)(2,1)} %get-tuple-element.124), channel_id=1, source_target_pairs={{0,24},{1,7},{2,26},{3,1},{4,28},{5,3},{6,30},{7,5},{8,0},{9,15},{... | collective-permute-start | bytes 1916936 | tf_op jit(solution)/shard_map/ppermute | solution.py:754
  170.9 23.4 %collective-permute-start.28 = (bf16[4,104,768]{2,1,0:T(8,128)(2,1)}, bf16[4,104,768]{2,1,0:T(8,128)(2,1)S(1)}, u32[]{:S(2)}, u32[]{:S(2)}) collective-permute-start(bf16[4,104,768]{2,1,0:T(8,128)(2,1)} %get-tuple-element.125), channel_id=1, source_target_pairs={{0,16},{1,5},{2,18},{3,7},{4,20},{5,1},{6,22},{7,3},{8,24},{9,13},... | collective-permute-start | bytes 1916936 | tf_op jit(solution)/shard_map/ppermute | solution.py:754
  174.7 24.6 %collective-permute-start.36 = (bf16[8,24,768]{2,1,0:T(8,128)(2,1)S(1)}, bf16[8,24,768]{2,1,0:T(8,128)(2,1)S(1)}, u32[]{:S(2)}, u32[]{:S(2)}) collective-permute-start(bf16[8,24,768]{2,1,0:T(8,128)(2,1)S(1)} %get-tuple-element.153), channel_id=1, source_target_pairs={{0,4},{1,17},{2,6},{3,19},{4,0},{5,21},{6,2},{7,23},{8,12},{9,25},... | collective-permute-start | bytes 884744 | tf_op jit(solution)/shard_map/ppermute | solution.py:754
  177.3 24.1 %collective-permute-start.38 = (bf16[8,24,768]{2,1,0:T(8,128)(2,1)S(1)}, bf16[8,24,768]{2,1,0:T(8,128)(2,1)S(1)}, u32[]{:S(2)}, u32[]{:S(2)}) collective-permute-start(bf16[8,24,768]{2,1,0:T(8,128)(2,1)S(1)} %get-tuple-element.154), channel_id=1, source_target_pairs={{0,6},{1,25},{2,0},{3,27},{4,2},{5,29},{6,4},{7,31},{8,14},{9,1},{... | collective-permute-start | bytes 884744 | tf_op jit(solution)/shard_map/ppermute | solution.py:754
  181.4 19.9 %collective-permute-start.37 = (bf16[8,24,768]{2,1,0:T(8,128)(2,1)S(1)}, bf16[8,24,768]{2,1,0:T(8,128)(2,1)S(1)}, u32[]{:S(2)}, u32[]{:S(2)}) collective-permute-start(bf16[8,24,768]{2,1,0:T(8,128)(2,1)S(1)} %get-tuple-element.155), channel_id=1, source_target_pairs={{0,2},{1,9},{2,4},{3,11},{4,6},{5,13},{6,0},{7,15},{8,10},{9,17},{... | collective-permute-start | bytes 884744 | tf_op jit(solution)/shard_map/ppermute | solution.py:754
  182.7 1.5 copy-start.1
  184.3 10.0 %copy-start.10 = (bf16[4,104,768]{2,1,0:T(8,128)(2,1)S(1)}, bf16[4,104,768]{2,1,0:T(8,128)(2,1)}, u32[]{:S(2)}) copy-start(bf16[4,104,768]{2,1,0:T(8,128)(2,1)} %get-tuple-element.128) | copy-start | bytes 1916932
  194.6 12.7 %collective-permute-start.29 = (bf16[104,768]{1,0:T(8,128)(2,1)S(1)}, bf16[104,768]{1,0:T(8,128)(2,1)S(1)}, u32[]{:S(2)}, u32[]{:S(2)}) collective-permute-start(bf16[104,768]{1,0:T(8,128)(2,1)S(1)} %get-tuple-element.156), channel_id=1, source_target_pairs={{0,4},{1,17},{2,6},{3,19},{4,0},{5,21},{6,2},{7,23},{8,12},{9,25},... | collective-permute-start | bytes 479240 | tf_op jit(solution)/shard_map/ppermute | solution.py:754
  199.3 8.8 %collective-permute-start.31 = (bf16[104,768]{1,0:T(8,128)(2,1)S(1)}, bf16[104,768]{1,0:T(8,128)(2,1)S(1)}, u32[]{:S(2)}, u32[]{:S(2)}) collective-permute-start(bf16[104,768]{1,0:T(8,128)(2,1)S(1)} %get-tuple-element.157), channel_id=1, source_target_pairs={{0,6},{1,25},{2,0},{3,27},{4,2},{5,29},{6,4},{7,31},{8,14},{9,1},{... | collective-permute-start | bytes 479240 | tf_op jit(solution)/shard_map/ppermute | solution.py:754
  199.3 8.8 %collective-permute-start.30 = (bf16[104,768]{1,0:T(8,128)(2,1)S(1)}, bf16[104,768]{1,0:T(8,128)(2,1)S(1)}, u32[]{:S(2)}, u32[]{:S(2)}) collective-permute-start(bf16[104,768]{1,0:T(8,128)(2,1)S(1)} %get-tuple-element.158), channel_id=1, source_target_pairs={{0,2},{1,9},{2,4},{3,11},{4,6},{5,13},{6,0},{7,15},{8,10},{9,17},{... | collective-permute-start | bytes 479240 | tf_op jit(solution)/shard_map/ppermute | solution.py:754
  202.9 11.0 %collective-permute-start.41 = (bf16[8,24,768]{2,1,0:T(8,128)(2,1)S(1)}, bf16[8,24,768]{2,1,0:T(8,128)(2,1)S(1)}, u32[]{:S(2)}, u32[]{:S(2)}) collective-permute-start(bf16[8,24,768]{2,1,0:T(8,128)(2,1)S(1)} %fusion.1.own), channel_id=1, source_target_pairs={{0,64},{32,96},{64,0},{96,32},{1,65},{33,97},{65,1},{97,33},{2,66}... | collective-permute-start | bytes 884744 | tf_op jit(solution)/shard_map/ppermute | solution.py:764
  206.2 11.2 %collective-permute-start.40 = (bf16[8,24,768]{2,1,0:T(8,128)(2,1)S(1)}, bf16[8,24,768]{2,1,0:T(8,128)(2,1)S(1)}, u32[]{:S(2)}, u32[]{:S(2)}) collective-permute-start(bf16[8,24,768]{2,1,0:T(8,128)(2,1)S(1)} %fusion.1.own), channel_id=1, source_target_pairs={{0,96},{32,0},{64,32},{96,64},{1,97},{33,1},{65,33},{97,65},{2,98}... | collective-permute-start | bytes 884744 | tf_op jit(solution)/shard_map/ppermute | solution.py:764
  207.2 11.6 %collective-permute-start.39 = (bf16[8,24,768]{2,1,0:T(8,128)(2,1)S(1)}, bf16[8,24,768]{2,1,0:T(8,128)(2,1)S(1)}, u32[]{:S(2)}, u32[]{:S(2)}) collective-permute-start(bf16[8,24,768]{2,1,0:T(8,128)(2,1)S(1)} %fusion.1.own), channel_id=1, source_target_pairs={{0,32},{32,64},{64,96},{96,0},{1,33},{33,65},{65,97},{97,1},{2,34}... | collective-permute-start | bytes 884744 | tf_op jit(solution)/shard_map/ppermute | solution.py:764
  208.3 11.5 %collective-permute-start.34 = (bf16[104,768]{1,0:T(8,128)(2,1)S(1)}, bf16[104,768]{1,0:T(8,128)(2,1)S(1)}, u32[]{:S(2)}, u32[]{:S(2)}) collective-permute-start(bf16[104,768]{1,0:T(8,128)(2,1)S(1)} %fusion.3.own), channel_id=1, source_target_pairs={{0,64},{32,96},{64,0},{96,32},{1,65},{33,97},{65,1},{97,33},{2,66}... | collective-permute-start | bytes 479240 | tf_op jit(solution)/shard_map/ppermute | solution.py:764
  209.2 11.6 %collective-permute-start.33 = (bf16[104,768]{1,0:T(8,128)(2,1)S(1)}, bf16[104,768]{1,0:T(8,128)(2,1)S(1)}, u32[]{:S(2)}, u32[]{:S(2)}) collective-permute-start(bf16[104,768]{1,0:T(8,128)(2,1)S(1)} %fusion.3.own), channel_id=1, source_target_pairs={{0,96},{32,0},{64,32},{96,64},{1,97},{33,1},{65,33},{97,65},{2,98}... | collective-permute-start | bytes 479240 | tf_op jit(solution)/shard_map/ppermute | solution.py:764
  213.9 6.9 %collective-permute-start.32 = (bf16[104,768]{1,0:T(8,128)(2,1)S(1)}, bf16[104,768]{1,0:T(8,128)(2,1)S(1)}, u32[]{:S(2)}, u32[]{:S(2)}) collective-permute-start(bf16[104,768]{1,0:T(8,128)(2,1)S(1)} %fusion.3.own), channel_id=1, source_target_pairs={{0,32},{32,64},{64,96},{96,0},{1,33},{33,65},{65,97},{97,1},{2,34}... | collective-permute-start | bytes 479240 | tf_op jit(solution)/shard_map/ppermute | solution.py:764
  (3 other events, 2.5 us)

commit v2 on v1

--- a/solution.py
+++ b/solution.py
@@ -758,10 +758,42 @@
     return (*pieces, *(swap_cores(p) for p in pieces))
 
 
-def second_turn(own, left, right, far):
-    parts = [four_sum(own[d], left[d], right[d], far[d]).astype(BF16) for d in range(RING)]
+def across_replicas(v):
+    return tuple(
+        lax.ppermute(v[d] if isinstance(v, (list, tuple)) else v, "rep", [(i, (i + d) % RING) for i in range(RING)])
+        for d in (1, 3, 2)
+    )
+
+
+def second_turn(parts):
     own = four_sum(parts[0], *around(parts, 1)).astype(BF16)
-    return own, *(lax.ppermute(own, "rep", [(i, (i + d) % RING) for i in range(RING)]) for d in (1, 3, 2))
+    return own, *across_replicas(own)
+
+
+def first_sums(own, left, right, far):
+    return [four_sum(own[d], left[d], right[d], far[d]).astype(BF16) for d in range(RING)]
+
+
+def far_pieces(keep, got, replica):
+    at, share = slice(2 * RING, 3 * RING), keep.shape[1] // RING
+    pieces = []
+    for d in range(RING):
+        low = ((replica + d) % RING) * share
+        cut = lambda v: lax.dynamic_slice_in_dim(v[at], low, share, axis=1).astype(F32)
+        pieces.append((cut(keep) + cut(got)).astype(BF16))
+    return pieces
+
+
+def first_sums_shared(own, left, right, far, replica):
+    share = far.shape[1]
+    sums = []
+    for d in range(RING):
+        near = own[d].astype(F32) + (left[d].astype(F32) + right[d].astype(F32))
+        near = near.reshape(RING, share, *near.shape[1:])
+        mine = lax.broadcasted_iota(jnp.int32, near.shape, 0) == replica
+        total = near + jnp.where(mine, far[d].astype(F32)[None], 0.0)
+        sums.append(total.reshape(own.shape[1:]).astype(BF16))
+    return sums
 
 
 def replica_sum(own, left, right, far, at):
@@ -834,7 +866,9 @@
         (query_bias, value_bias, output_bias, first_gain, first_shift, down_bias, second_gain, second_shift),
         up_bias,
     )
-    near = (packed, *around(packed, 1))
+    *near, xs_other, xl_other = lax.optimization_barrier(
+        (packed, *around(packed, 1), swap_cores(xs), swap_cores(xl))
+    )
     cut = 4 * each + 8
     near_a = jnp.stack([n[:cut] for n in near])
     near_f = jnp.stack([n[cut:].reshape(-1, each, width) for n in near])
@@ -846,25 +880,33 @@
         short_lengths, long_lengths, pos, xs, xl, pieces_a, inner, dims
     )
     unit1, *far_f = lax.optimization_barrier((unit1, *far_f))
-    early = (swap_cores(c), swap_cores(xs), swap_cores(xl))
-    ub, *early = lax.optimization_barrier((ub, *early))
+    ub, c_other = lax.optimization_barrier((ub, swap_cores(c)))
     keep_f, give_f, out_s, out_l, gfs, gatt, sums = feed(
         short_lengths, long_lengths, pos, unit1, cs, cl, inv1, ub, vecs, both_cores((near_f, *far_f)), dims
     )
     grads = attention_back(gatt, gathered_a, q, k, v, ps, plong, dims)
-    grads, gatt_other, sums_other = lax.optimization_barrier((grads, swap_cores(gatt), swap_cores(sums)))
-    others = (gatt_other, early[0], swap_cores(grads), *early[1:], sums_other)
-    parts_f = pair_sum(keep_f, swap_cores(give_f))
-    c, *parts_f = lax.optimization_barrier((c, *parts_f))
-    around_f = around(parts_f, 0)
+    got_f, gatt_other, sums_other, grads = lax.optimization_barrier(
+        (swap_cores(give_f), swap_cores(gatt), swap_cores(sums), grads)
+    )
+    grads_other = swap_cores(grads)
+    replica = lax.axis_index("rep")
+    parts_f = pair_sum(keep_f, got_f)
+    shares = far_pieces(keep_f, got_f, replica)
+    parts_f[2] = shares[0]
+    grads_other, *parts_f = lax.optimization_barrier((grads_other, *parts_f, *shares[1:]))
+    parts_f, shares = parts_f[:RING], [parts_f[2], *parts_f[RING:]]
+    near_sums = [lax.ppermute(parts_f[d], "shard", turn(d, 0)) for d in (1, 3)]
+    far_sum = four_sum(shares[0], *across_replicas(shares)).astype(BF16)
+    others = (gatt_other, c_other, grads_other, xs_other, xl_other, sums_other)
     parts_a = weight_back(pos, gatt, c, grads, xs, xl, sums, others)
-    gfs, *both = lax.optimization_barrier((gfs, *parts_a, *around_f[:2]))
-    parts_a, around_f = both[:RING], (*both[RING:], around_f[2])
+    gfs, *both = lax.optimization_barrier((gfs, *parts_a, *near_sums, far_sum))
+    parts_a, near_sums, far_sum = both[:RING], both[RING:-1], both[-1]
+    far_f = lax.ppermute(far_sum, "shard", turn(2, 0))
     around_a = around(parts_a, 0)
     grad_s, grad_l = input_back(gfs, grads, gathered_a, dims)
     grad_s, *around_a = lax.optimization_barrier((grad_s, *around_a))
-    up, down = finish_feed(second_turn(parts_f[0], *around_f), each, inner, tall)
-    w_in, w_out, *vectors = finish_attention(second_turn(parts_a[0], *around_a), tall)
+    up, down = finish_feed(second_turn(first_sums_shared(parts_f[0], *near_sums, far_f, replica)), each, inner, tall)
+    w_in, w_out, *vectors = finish_attention(second_turn(first_sums(parts_a[0], *around_a)), tall)
     vectors = [x.reshape(-1) for x in vectors]
     return (
         out_s.reshape(short_tokens.shape), out_l.reshape(long_tokens.shape),

time: 222 us -> 234 us (1.054); the launches traced: 222 us -> 230 us
  starting transfers between devices: 49.7 us -> 58.6 us
  waiting for transfers between devices: 61.4 us -> 56.7 us
  local copies, waits for them, and re-layouts: 9.3 us -> 12 us
    ppermute x6 -> x12, starting transfers between devices: 10.3 us -> 26.1 us  [the longest x9 13 us: across_replicas(): lax.ppermute(v[d] if isinstance(v, (list, tuple)) else v, 'rep', [(i, (i...]
    ppermute x21 -> x18, waiting for transfers between devices: 48.1 us -> 33 us  [around(): lax.ppermute(v[d] if isinstance(v, (list, tuple)) else v, 'shard', turn(d...]
    ppermute x6 -> x12, waiting for transfers between devices: 6.52 us -> 14.4 us  [the longest x9 11.6 us: across_replicas(): lax.ppermute(v[d] if isinstance(v, (list, tuple)) else v, 'rep', [(i, (i...]
    ppermute x21 -> x18, starting transfers between devices: 36.2 us -> 29.8 us  [around(): lax.ppermute(v[d] if isinstance(v, (list, tuple)) else v, 'shard', turn(d...]
    convert_element_type x2 -> x4, other arithmetic: 2.61 us -> 6.09 us  [the longest x1 2.05 us: on_device(): far_sum = four_sum(shares[0], *across_replicas(shares)).astype(BF16)]
    convert_element_type x1, other arithmetic: 6.09 us -> 3.04 us  [pair_sum(): parts.append((keep[at].astype(F32) + got[at].astype(F32)).astype(BF16))]
    slice x0 -> x2, local copies, waits for them, and re-layouts: none -> 2.84 us  [far_pieces(): v[at]]
    ppermute x15, waiting for transfers between devices: 6.75 us -> 9.27 us  [swap_cores(): return lax.ppermute(v, 'shard', [(i, i ^ 1) for i in range(SHARDS)])]
  transfers between devices with their start and end apart: 42 -> 45, of which waited for: 17 -> 16; matrix products, arithmetic and copies ran while one was open for 5% -> 7% of each run, Pallas kernels for 22% -> 22%
where the time goes in v2:
time: 234 us; the launch traced here: 230 us
  Pallas kernels  88.9 us (38%)
  starting transfers between devices  58.6 us (25%)
  waiting for transfers between devices  56.7 us (24%)
  other arithmetic  12.5 us (5%)
  local copies, waits for them, and re-layouts  12 us (5%)
    pallas_call x1, Pallas kernels, feed(): pl.pallas_call(functools.partial(feed_body, dims), in_specs=[SCALARS] * 3...  37.3 us
    ppermute x18, waiting for transfers between devices, around(): lax.ppermute(v[d] if isinstance(v, (list, tuple)) else v, 'shard', turn(d...  33 us
    ppermute x18, starting transfers between devices, around(): lax.ppermute(v[d] if isinstance(v, (list, tuple)) else v, 'shard', turn(d...  29.8 us
    pallas_call x1, Pallas kernels, attention_forward(): pl.pallas_call(functools.partial(attention_forward_body, dims), grid_spec...  19 us
    ppermute x9, starting transfers between devices, across_replicas(): lax.ppermute(v[d] if isinstance(v, (list, tuple)) else v, 'rep', [(i, (i...  13 us
    ppermute x2, starting transfers between devices, on_device(): near_sums = [lax.ppermute(parts_f[d], 'shard', turn(d, 0)) for d in (1, 3)]  12.8 us
    pallas_call x1, Pallas kernels, weight_back(): pl.pallas_call(weight_back_body, grid_spec=pltpu.PrefetchScalarGridSpec(n...  11.8 us
    pallas_call x1, Pallas kernels, attention_back(): pl.pallas_call(functools.partial(attention_back_body, dims), grid=(width...  11.7 us
  transfers between devices with their start and end apart: 45, of which 16 were waited for; matrix products, arithmetic and copies ran while one was open for 7% of the time, Pallas kernels for 22%

profile of v2, /device:TPU:0, one launch (start us, length us, event | category | flops | bytes accessed | tf_op | source)
XLA Modules:
  0.0 230.1 jit_solution(18244449809102786900)
XLA Ops:
  0.8 2.0 pack.1
  2.8 2.0 collective-permute-start
  4.8 2.1 collective-permute-start.1
  6.9 1.9 collective-permute-start.2
  8.8 1.6 collective-permute-done.3.xs_other
  10.4 3.1 %collective-permute-done = bf16[296,768]{1,0:T(8,128)(2,1)S(1)} collective-permute-done((bf16[296,768]{1,0:T(8,128)(2,1)}, bf16[296,768]{1,0:T(8,128)(2,1)S(1)}, u32[]{:S(2)}, u32[]{:S(2)}) %collective-permute-start) | collective-permute-done | bytes 454688 | tf_op jit(solution)/shard_map/ppermute | solution.py:754
  13.5 4.6 %collective-permute-done.1 = bf16[296,768]{1,0:T(8,128)(2,1)S(1)} collective-permute-done((bf16[296,768]{1,0:T(8,128)(2,1)}, bf16[296,768]{1,0:T(8,128)(2,1)S(1)}, u32[]{:S(2)}, u32[]{:S(2)}) %collective-permute-start.1) | collective-permute-done | bytes 454688 | tf_op jit(solution)/shard_map/ppermute | solution.py:754
  18.1 1.8 collective-permute-done.2
  19.9 1.1 slice_bitcast_fusion.2
  21.1 2.8 %collective-permute-start.6 = (bf16[4,104,768]{2,1,0:T(8,128)(2,1)S(1)}, bf16[4,104,768]{2,1,0:T(8,128)(2,1)S(1)}, u32[]{:S(2)}, u32[]{:S(2)}) collective-permute-start(bf16[4,104,768]{2,1,0:T(8,128)(2,1)S(1)} %pad_maximum_fusion.1.p0), channel_id=1, source_target_pairs={{0,24},{1,7},{2,26},{3,1},{4,28},{5,3},{6,30},{7,5},{8,0},{9,15},{... | collective-permute-start | bytes 1916936 | tf_op jit(solution)/shard_map/ppermute | solution.py:754
  23.9 0.8 collective-permute-start.7
  24.7 0.9 collective-permute-start.5
  25.6 13.1 %collective-permute-done.6.p2 = bf16[4,104,768]{2,1,0:T(8,128)(2,1)S(1)} collective-permute-done((bf16[4,104,768]{2,1,0:T(8,128)(2,1)S(1)}, bf16[4,104,768]{2,1,0:T(8,128)(2,1)S(1)}, u32[]{:S(2)}, u32[]{:S(2)}) %collective-permute-start.6) | collective-permute-done | bytes 639008 | tf_op jit(solution)/shard_map/ppermute | solution.py:754
  38.8 0.8 copy-done.18
  40.2 3.7 %collective-permute-start.13 = (bf16[4,8,24,768]{3,2,1,0:T(8,128)(2,1)S(1)}, bf16[4,8,24,768]{3,2,1,0:T(8,128)(2,1)}, u32[]{:S(2)}, u32[]{:S(2)}) collective-permute-start(bf16[4,8,24,768]{3,2,1,0:T(8,128)(2,1)S(1)} %pad_maximum_fusion.p0), channel_id=1, source_target_pairs={{0,24},{1,7},{2,26},{3,1},{4,28},{5,3},{6,30},{7,5},{8,0},{9,15},{... | collective-permute-start | bytes 3538952 | tf_op jit(solution)/shard_map/ppermute | solution.py:754
  43.9 1.5 collective-permute-start.14
  45.4 0.8 copy-done.19
  46.2 0.8 copy-done.20
  47.1 0.6 pad_add_fusion.pos
  47.8 0.9 collective-permute-done.9.p5
  48.7 19.0 %attention_forward.1 = (bf16[640,768]{1,0:T(8,128)(2,1)}, bf16[640,768]{1,0:T(8,128)(2,1)}, bf16[640,768]{1,0:T(8,128)(2,1)}, bf16[640,768]{1,0:T(8,128)(2,1)}, ...) custom-call(s32[2]{0:T(128)} %slen.3, s32[2]{0:T(128)} %llen.3, ...), custom_call_target="tpu_custom_call" | custom-call | flops 3019898880 | bytes 20000000 | tf_op jit(solution)/shard_map/attention_forward/pallas_call | solution.py:273
  67.7 2.5 %collective-permute-done.13.p2 = bf16[4,8,24,768]{3,2,1,0:T(8,128)(2,1)} collective-permute-done((bf16[4,8,24,768]{3,2,1,0:T(8,128)(2,1)S(1)}, bf16[4,8,24,768]{3,2,1,0:T(8,128)(2,1)}, u32[]{:S(2)}, u32[]{:S(2)}) %collective-permute-start.13) | collective-permute-done | bytes 1179680 | tf_op jit(solution)/shard_map/ppermute | solution.py:754
  70.3 1.9 collective-permute-done.14.p3
  72.7 0.7 collective-permute-start.15
  73.5 6.3 %collective-permute-done.15.c_other = bf16[640,768]{1,0:T(8,128)(2,1)S(1)} collective-permute-done((bf16[640,768]{1,0:T(8,128)(2,1)}, bf16[640,768]{1,0:T(8,128)(2,1)S(1)}, u32[]{:S(2)}, u32[]{:S(2)}) %collective-permute-start.15) | collective-permute-done | bytes 983072 | tf_op jit(solution)/shard_map/ppermute | solution.py:750
  80.2 0.6 copy-done.16
  81.2 37.3 %feed.1 = (bf16[16,8,24,768]{3,2,1,0:T(8,128)(2,1)}, bf16[16,8,24,768]{3,2,1,0:T(8,128)(2,1)}, bf16[128,768]{1,0:T(8,128)(2,1)}, bf16[512,768]{1,0:T(8,128)(2,1)...) custom-call(s32[2]{0:T(128)} %slen.3, s32[2]{0:T(128)} %llen.3, s32[3]{0:T(128)} %pad_add_fusion.pos, ...), custom_call_target="tpu_custom_call" | custom-call | flops 18119393280 | bytes 30000000 | tf_op jit(solution)/shard_map/feed/pallas_call | solution.py:490
  119.3 11.7 %attention_back.1.d = bf16[3,640,768]{2,1,0:T(8,128)(2,1)} custom-call(bf16[640,768]{1,0:T(8,128)(2,1)} %get-tuple-element.111.gatt, bf16[32,104,768]{2,1,0:T(8,128)(2,1)} %get-tuple-element.114.wo_block.wq.wk.wv, bf16[640,768]{1,0:T(8,128)(2,1)} %get-tuple-element.115.q, bf16[640,768]{1,0:T(8,128)(2,1)} %get-tuple-element.116.k, ...), custom_call_target="tpu_custom_call" | custom-call | flops 3019898880 | bytes 15000000 | tf_op jit(solution)/shard_map/attention_back/pallas_call | solution.py:554
  131.5 1.3 slice.162
  132.9 1.5 slice.163
  134.8 0.8 copy-done.3
  135.6 3.0 %add_convert_fusion = (bf16[4,8,24,768]{3,2,1,0:T(8,128)(2,1)S(1)}, bf16[4,8,24,768]{3,2,1,0:T(8,128)(2,1)S(1)}, bf16[4,8,24,768]{3,2,1,0:T(8,128)(2,1)S(1)}) fusion(bf16[16,8,24,768]{3,2,1,0:T(8,128)(2,1)} %collective-permute-done.20, bf16[16,8,24,768]{3,2,1,0:T(8,128)(2,1)S(1)} %copy-done.3), kind=kLoop, calls=%fused_computation | loop fusion | flops 7077888 | bytes 10616832 | tf_op jit(solution)/shard_map/convert_element_type | solution.py:727
  138.6 11.0 %collective-permute-start.24 = (bf16[4,8,24,768]{3,2,1,0:T(8,128)(2,1)S(1)}, bf16[4,8,24,768]{3,2,1,0:T(8,128)(2,1)}, u32[]{:S(2)}, u32[]{:S(2)}) collective-permute-start(bf16[4,8,24,768]{3,2,1,0:T(8,128)(2,1)S(1)} %get-tuple-element.133), channel_id=1, source_target_pairs={{0,8},{1,3},{2,10},{3,5},{4,12},{5,7},{6,14},{7,1},{8,16},{9,11},{... | collective-permute-start | bytes 3538952 | tf_op jit(solution)/shard_map/ppermute | solution.py:898
  149.6 1.8 collective-permute-start.25
  151.4 3.2 %collective-permute-start.26 = (bf16[4,2,24,768]{3,2,1,0:T(8,128)(2,1)S(1)}, bf16[4,2,24,768]{3,2,1,0:T(8,128)(2,1)S(1)}, u32[]{:S(2)}, u32[]{:S(2)}) collective-permute-start(bf16[4,2,24,768]{3,2,1,0:T(8,128)(2,1)S(1)} %get-tuple-element.136), channel_id=1, source_target_pairs={{0,64},{32,96},{64,0},{96,32},{1,65},{33,97},{65,1},{97,33},{2,66}... | collective-permute-start | bytes 884744 | tf_op jit(solution)/shard_map/ppermute | solution.py:763
  154.6 0.7 collective-permute-start.27
  155.3 2.6 %collective-permute-start.28 = (bf16[4,2,24,768]{3,2,1,0:T(8,128)(2,1)S(1)}, bf16[4,2,24,768]{3,2,1,0:T(8,128)(2,1)}, u32[]{:S(2)}, u32[]{:S(2)}) collective-permute-start(bf16[4,2,24,768]{3,2,1,0:T(8,128)(2,1)S(1)} %get-tuple-element.138), channel_id=1, source_target_pairs={{0,96},{32,0},{64,32},{96,64},{1,97},{33,1},{65,33},{97,65},{2,98}... | collective-permute-start | bytes 884744 | tf_op jit(solution)/shard_map/ppermute | solution.py:763
  157.8 11.8 %weight_back.1 = (bf16[4,104,768]{2,1,0:T(8,128)(2,1)}, bf16[4,104,768]{2,1,0:T(8,128)(2,1)}, bf16[4,104,768]{2,1,0:T(8,128)(2,1)}, bf16[4,104,768]{2,1,0:T(8,128)(2,1)}) custom-call(s32[3]{0:T(128)} %pad_add_fusion.pos, bf16[640,768]{1,0:T(8,128)(2,1)} %get-tuple-element.111.gatt, bf16[640,768]{1,0:T(8,128)(2,1)} %copy-done.8, ...), custom_call_target="tpu_custom_call" | custom-call | flops 3019898880 | bytes 12000000 | tf_op jit(solution)/shard_map/weight_back/pallas_call | solution.py:655
  169.7 0.7 copy-done.12
  170.4 2.1 add_convert_fusion.4
  172.8 1.2 collective-permute-start.29
  173.9 2.0 collective-permute-start.30
  176.0 2.0 collective-permute-start.31
  178.2 2.8 %collective-permute-done.38 = bf16[4,2,24,768]{3,2,1,0:T(8,128)(2,1)S(1)} collective-permute-done((bf16[4,2,24,768]{3,2,1,0:T(8,128)(2,1)}, bf16[4,2,24,768]{3,2,1,0:T(8,128)(2,1)S(1)}, u32[]{:S(2)}, u32[]{:S(2)}) %collective-permute-start.38) | collective-permute-done | bytes 294944 | tf_op jit(solution)/shard_map/ppermute | solution.py:904
  181.0 2.0 fusion.5
  183.6 2.4 %copy-done = bf16[32,104,768]{2,1,0:T(8,128)(2,1)S(1)} copy-done((bf16[32,104,768]{2,1,0:T(8,128)(2,1)S(1)}, bf16[32,104,768]{2,1,0:T(8,128)(2,1)}, u32[]{:S(2)}) %copy-start) | copy-done | bytes 5111832
  186.1 5.4 %input_back.1 = (f32[128,768]{1,0:T(8,128)}, f32[512,768]{1,0:T(8,128)}) custom-call(f32[640,768]{1,0:T(8,128)S(1)} %copy-done.2, bf16[3,640,768]{2,1,0:T(8,128)(2,1)S(1)} %copy-done.1, bf16[32,104,768]{2,1,0:T(8,128)(2,1)S(1)} %copy-done, bf16[32,104,768]{2,1,0:T(8,128)(2,1)S(1)} %copy-done, bf16[32,104,768]{2,1,0:T(8,128)(2,1)S(1)} %copy-done), custom_call_target="tpu_custom_call" | custom-call | flops 2264924160 | bytes 12000000 | tf_op jit(solution)/shard_map/input_back/pallas_call | solution.py:707
  191.4 2.2 collective-permute-start.40
  193.6 1.4 collective-permute-start.41
  195.1 6.0 %collective-permute-done.31 = bf16[4,104,768]{2,1,0:T(8,128)(2,1)} collective-permute-done((bf16[4,104,768]{2,1,0:T(8,128)(2,1)}, bf16[4,104,768]{2,1,0:T(8,128)(2,1)}, u32[]{:S(2)}, u32[]{:S(2)}) %collective-permute-start.31) | collective-permute-done | bytes 639008 | tf_op jit(solution)/shard_map/ppermute | solution.py:754
  201.0 1.7 fusion.11
  202.9 3.2 %collective-permute-start.33 = (bf16[104,768]{1,0:T(8,128)(2,1)S(1)}, bf16[104,768]{1,0:T(8,128)(2,1)S(1)}, u32[]{:S(2)}, u32[]{:S(2)}) collective-permute-start(bf16[104,768]{1,0:T(8,128)(2,1)S(1)} %get-tuple-element.175), channel_id=1, source_target_pairs={{0,2},{1,9},{2,4},{3,11},{4,6},{5,13},{6,0},{7,15},{8,10},{9,17},{... | collective-permute-start | bytes 479240 | tf_op jit(solution)/shard_map/ppermute | solution.py:754
  206.1 1.3 collective-permute-start.34
  207.4 1.3 add_convert_fusion.3.own
  208.8 3.2 %collective-permute-start.43 = (bf16[8,24,768]{2,1,0:T(8,128)(2,1)S(1)}, bf16[8,24,768]{2,1,0:T(8,128)(2,1)S(1)}, u32[]{:S(2)}, u32[]{:S(2)}) collective-permute-start(bf16[8,24,768]{2,1,0:T(8,128)(2,1)S(1)} %add_convert_fusion.3.own), channel_id=1, source_target_pairs={{0,96},{32,0},{64,32},{96,64},{1,97},{33,1},{65,33},{97,65},{2,98}... | collective-permute-start | bytes 884744 | tf_op jit(solution)/shard_map/ppermute | solution.py:763
  212.0 1.2 fusion.9.own
  213.3 0.9 collective-permute-start.35
  214.2 2.4 %collective-permute-start.36 = (bf16[104,768]{1,0:T(8,128)(2,1)S(1)}, bf16[104,768]{1,0:T(8,128)(2,1)S(1)}, u32[]{:S(2)}, u32[]{:S(2)}) collective-permute-start(bf16[104,768]{1,0:T(8,128)(2,1)S(1)} %fusion.9.own), channel_id=1, source_target_pairs={{0,96},{32,0},{64,32},{96,64},{1,97},{33,1},{65,33},{97,65},{2,98}... | collective-permute-start | bytes 479240 | tf_op jit(solution)/shard_map/ppermute | solution.py:763
  216.6 5.8 %collective-permute-done.42.left = bf16[8,24,768]{2,1,0:T(8,128)(2,1)S(1)} collective-permute-done((bf16[8,24,768]{2,1,0:T(8,128)(2,1)S(1)}, bf16[8,24,768]{2,1,0:T(8,128)(2,1)S(1)}, u32[]{:S(2)}, u32[]{:S(2)}) %collective-permute-start.42) | collective-permute-done | bytes 294944 | tf_op jit(solution)/shard_map/ppermute | solution.py:763
  222.4 0.9 finish_feed.1
  223.3 0.7 collective-permute-done.35.left
  224.1 1.0 collective-permute-done.36.right
  225.1 4.1 %collective-permute-done.37.far = bf16[104,768]{1,0:T(8,128)(2,1)S(1)} collective-permute-done((bf16[104,768]{1,0:T(8,128)(2,1)S(1)}, bf16[104,768]{1,0:T(8,128)(2,1)S(1)}, u32[]{:S(2)}, u32[]{:S(2)}) %collective-permute-start.37) | collective-permute-done | bytes 159776 | tf_op jit(solution)/shard_map/ppermute | solution.py:763
  229.1 0.8 finish_attention.1
  (101 shorter events, 5.4 us)
Async XLA Ops:
  0.7 19.2 %collective-permute-start.4 = (bf16[512,768]{1,0:T(8,128)(2,1)}, bf16[512,768]{1,0:T(8,128)(2,1)S(1)}, u32[]{:S(2)}, u32[]{:S(2)}) collective-permute-start(bf16[512,768]{1,0:T(8,128)(2,1)} %bitcast.112), channel_id=1, source_target_pairs={{0,1},{1,0},{2,3},{3,2},{4,5},{5,4},{6,7},{7,6},{8,9},{9,8},{10,11... | collective-permute-start | bytes 2359304 | tf_op jit(solution)/shard_map/ppermute | solution.py:750
  2.8 10.7 %collective-permute-start = (bf16[296,768]{1,0:T(8,128)(2,1)}, bf16[296,768]{1,0:T(8,128)(2,1)S(1)}, u32[]{:S(2)}, u32[]{:S(2)}) collective-permute-start(bf16[296,768]{1,0:T(8,128)(2,1)} %pack.1), channel_id=1, source_target_pairs={{0,2},{1,9},{2,4},{3,11},{4,6},{5,13},{6,0},{7,15},{8,10},{9,17},{... | collective-permute-start | bytes 1363976 | tf_op jit(solution)/shard_map/ppermute | solution.py:754
  4.8 13.3 %collective-permute-start.1 = (bf16[296,768]{1,0:T(8,128)(2,1)}, bf16[296,768]{1,0:T(8,128)(2,1)S(1)}, u32[]{:S(2)}, u32[]{:S(2)}) collective-permute-start(bf16[296,768]{1,0:T(8,128)(2,1)} %pack.1), channel_id=1, source_target_pairs={{0,6},{1,25},{2,0},{3,27},{4,2},{5,29},{6,4},{7,31},{8,14},{9,1},{... | collective-permute-start | bytes 1363976 | tf_op jit(solution)/shard_map/ppermute | solution.py:754
  6.9 13.0 %collective-permute-start.2 = (bf16[296,768]{1,0:T(8,128)(2,1)}, bf16[296,768]{1,0:T(8,128)(2,1)S(1)}, u32[]{:S(2)}, u32[]{:S(2)}) collective-permute-start(bf16[296,768]{1,0:T(8,128)(2,1)} %pack.1), channel_id=1, source_target_pairs={{0,4},{1,17},{2,6},{3,19},{4,0},{5,21},{6,2},{7,23},{8,12},{9,25},... | collective-permute-start | bytes 1363976 | tf_op jit(solution)/shard_map/ppermute | solution.py:754
  8.8 30.0 %copy-start.4 = (bf16[296,768]{1,0:T(8,128)(2,1)S(1)}, bf16[296,768]{1,0:T(8,128)(2,1)}, u32[]{:S(2)}) copy-start(bf16[296,768]{1,0:T(8,128)(2,1)} %pack.1) | copy-start | bytes 1363972
  8.8 1.7 collective-permute-start.3
  10.4 10.6 %copy-start.13 = (bf16[128,768]{1,0:T(8,128)(2,1)}, bf16[128,768]{1,0:T(8,128)(2,1)S(1)}, u32[]{:S(2)}) copy-start(bf16[128,768]{1,0:T(8,128)(2,1)S(1)} %collective-permute-done.3.xs_other) | copy-start | bytes 589828
  13.5 25.2 %copy-start.5 = (bf16[296,768]{1,0:T(8,128)(2,1)}, bf16[296,768]{1,0:T(8,128)(2,1)S(1)}, u32[]{:S(2)}) copy-start(bf16[296,768]{1,0:T(8,128)(2,1)S(1)} %collective-permute-done) | copy-start | bytes 1363972
  19.8 1.2 copy-start.9
  21.1 17.8 %copy-start.11 = (bf16[4,104,768]{2,1,0:T(8,128)(2,1)}, bf16[4,104,768]{2,1,0:T(8,128)(2,1)S(1)}, u32[]{:S(2)}) copy-start(bf16[4,104,768]{2,1,0:T(8,128)(2,1)S(1)} %pad_maximum_fusion.1.p0) | copy-start | bytes 1916932
  21.1 17.6 %collective-permute-start.6 = (bf16[4,104,768]{2,1,0:T(8,128)(2,1)S(1)}, bf16[4,104,768]{2,1,0:T(8,128)(2,1)S(1)}, u32[]{:S(2)}, u32[]{:S(2)}) collective-permute-start(bf16[4,104,768]{2,1,0:T(8,128)(2,1)S(1)} %pad_maximum_fusion.1.p0), channel_id=1, source_target_pairs={{0,24},{1,7},{2,26},{3,1},{4,28},{5,3},{6,30},{7,5},{8,0},{9,15},{... | collective-permute-start | bytes 1916936 | tf_op jit(solution)/shard_map/ppermute | solution.py:754
  23.9 16.3 %collective-permute-start.7 = (bf16[4,104,768]{2,1,0:T(8,128)(2,1)S(1)}, bf16[4,104,768]{2,1,0:T(8,128)(2,1)}, u32[]{:S(2)}, u32[]{:S(2)}) collective-permute-start(bf16[4,104,768]{2,1,0:T(8,128)(2,1)S(1)} %pad_maximum_fusion.1.p0), channel_id=1, source_target_pairs={{0,16},{1,5},{2,18},{3,7},{4,20},{5,1},{6,22},{7,3},{8,24},{9,13},... | collective-permute-start | bytes 1916936 | tf_op jit(solution)/shard_map/ppermute | solution.py:754
  24.7 19.2 %collective-permute-start.5 = (bf16[4,104,768]{2,1,0:T(8,128)(2,1)S(1)}, bf16[4,104,768]{2,1,0:T(8,128)(2,1)}, u32[]{:S(2)}, u32[]{:S(2)}) collective-permute-start(bf16[4,104,768]{2,1,0:T(8,128)(2,1)S(1)} %pad_maximum_fusion.1.p0), channel_id=1, source_target_pairs={{0,8},{1,3},{2,10},{3,5},{4,12},{5,7},{6,14},{7,1},{8,16},{9,11},{... | collective-permute-start | bytes 1916936 | tf_op jit(solution)/shard_map/ppermute | solution.py:754
  25.6 19.8 %collective-permute-start.8 = (bf16[4,104,768]{2,1,0:T(8,128)(2,1)S(1)}, bf16[4,104,768]{2,1,0:T(8,128)(2,1)S(1)}, u32[]{:S(2)}, u32[]{:S(2)}) collective-permute-start(bf16[4,104,768]{2,1,0:T(8,128)(2,1)S(1)} %pad_maximum_fusion.1.p0), channel_id=1, source_target_pairs={{0,1},{1,0},{2,3},{3,2},{4,5},{5,4},{6,7},{7,6},{8,9},{9,8},{10,11... | collective-permute-start | bytes 1916936 | tf_op jit(solution)/shard_map/ppermute | solution.py:750
  38.7 6.7 %collective-permute-start.10 = (bf16[4,104,768]{2,1,0:T(8,128)(2,1)S(1)}, bf16[4,104,768]{2,1,0:T(8,128)(2,1)S(1)}, u32[]{:S(2)}, u32[]{:S(2)}) collective-permute-start(bf16[4,104,768]{2,1,0:T(8,128)(2,1)S(1)} %collective-permute-done.6.p2), channel_id=1, source_target_pairs={{0,1},{1,0},{2,3},{3,2},{4,5},{5,4},{6,7},{7,6},{8,9},{9,8},{10,11... | collective-permute-start | bytes 1916936 | tf_op jit(solution)/shard_map/ppermute | solution.py:750
  38.8 1.2 slice-start
  40.1 27.6 %copy-start.6 = (bf16[4,8,24,768]{3,2,1,0:T(8,128)(2,1)}, bf16[4,8,24,768]{3,2,1,0:T(8,128)(2,1)S(1)}, u32[]{:S(2)}) copy-start(bf16[4,8,24,768]{3,2,1,0:T(8,128)(2,1)S(1)} %pad_maximum_fusion.p0) | copy-start | bytes 3538948
  40.1 27.6 %collective-permute-start.12 = (bf16[4,8,24,768]{3,2,1,0:T(8,128)(2,1)S(1)}, bf16[4,8,24,768]{3,2,1,0:T(8,128)(2,1)S(1)}, u32[]{:S(2)}, u32[]{:S(2)}) collective-permute-start(bf16[4,8,24,768]{3,2,1,0:T(8,128)(2,1)S(1)} %pad_maximum_fusion.p0), channel_id=1, source_target_pairs={{0,8},{1,3},{2,10},{3,5},{4,12},{5,7},{6,14},{7,1},{8,16},{9,11},{... | collective-permute-start | bytes 3538952 | tf_op jit(solution)/shard_map/ppermute | solution.py:754
  40.2 30.1 %collective-permute-start.13 = (bf16[4,8,24,768]{3,2,1,0:T(8,128)(2,1)S(1)}, bf16[4,8,24,768]{3,2,1,0:T(8,128)(2,1)}, u32[]{:S(2)}, u32[]{:S(2)}) collective-permute-start(bf16[4,8,24,768]{3,2,1,0:T(8,128)(2,1)S(1)} %pad_maximum_fusion.p0), channel_id=1, source_target_pairs={{0,24},{1,7},{2,26},{3,1},{4,28},{5,3},{6,30},{7,5},{8,0},{9,15},{... | collective-permute-start | bytes 3538952 | tf_op jit(solution)/shard_map/ppermute | solution.py:754
  43.9 28.3 %collective-permute-start.14 = (bf16[4,8,24,768]{3,2,1,0:T(8,128)(2,1)S(1)}, bf16[4,8,24,768]{3,2,1,0:T(8,128)(2,1)}, u32[]{:S(2)}, u32[]{:S(2)}) collective-permute-start(bf16[4,8,24,768]{3,2,1,0:T(8,128)(2,1)S(1)} %pad_maximum_fusion.p0), channel_id=1, source_target_pairs={{0,16},{1,5},{2,18},{3,7},{4,20},{5,1},{6,22},{7,3},{8,24},{9,13},... | collective-permute-start | bytes 3538952 | tf_op jit(solution)/shard_map/ppermute | solution.py:754
  45.4 2.3 collective-permute-start.11
  46.2 2.5 %collective-permute-start.9 = (bf16[4,104,768]{2,1,0:T(8,128)(2,1)}, bf16[4,104,768]{2,1,0:T(8,128)(2,1)}, u32[]{:S(2)}, u32[]{:S(2)}) collective-permute-start(bf16[4,104,768]{2,1,0:T(8,128)(2,1)} %collective-permute-done.5.p1), channel_id=1, source_target_pairs={{0,1},{1,0},{2,3},{3,2},{4,5},{5,4},{6,7},{7,6},{8,9},{9,8},{10,11... | collective-permute-start | bytes 1916936 | tf_op jit(solution)/shard_map/ppermute | solution.py:750
  47.7 1.0 copy-start.21
  47.7 32.1 %collective-permute-start.16 = (bf16[4,8,24,768]{3,2,1,0:T(8,128)(2,1)S(1)}, bf16[4,8,24,768]{3,2,1,0:T(8,128)(2,1)S(1)}, u32[]{:S(2)}, u32[]{:S(2)}) collective-permute-start(bf16[4,8,24,768]{3,2,1,0:T(8,128)(2,1)S(1)} %pad_maximum_fusion.p0), channel_id=1, source_target_pairs={{0,1},{1,0},{2,3},{3,2},{4,5},{5,4},{6,7},{7,6},{8,9},{9,8},{10,11... | collective-permute-start | bytes 3538952 | tf_op jit(solution)/shard_map/ppermute | solution.py:750
  67.7 12.5 %copy-start.15 = (bf16[4,8,24,768]{3,2,1,0:T(8,128)(2,1)}, bf16[4,8,24,768]{3,2,1,0:T(8,128)(2,1)S(1)}, u32[]{:S(2)}) copy-start(bf16[4,8,24,768]{3,2,1,0:T(8,128)(2,1)S(1)} %collective-permute-done.12.p1) | copy-start | bytes 3538948
  72.2 7.5 %collective-permute-start.17 = (bf16[4,8,24,768]{3,2,1,0:T(8,128)(2,1)S(1)}, bf16[4,8,24,768]{3,2,1,0:T(8,128)(2,1)S(1)}, u32[]{:S(2)}, u32[]{:S(2)}) collective-permute-start(bf16[4,8,24,768]{3,2,1,0:T(8,128)(2,1)S(1)} %collective-permute-done.12.p1), channel_id=1, source_target_pairs={{0,1},{1,0},{2,3},{3,2},{4,5},{5,4},{6,7},{7,6},{8,9},{9,8},{10,11... | collective-permute-start | bytes 3538952 | tf_op jit(solution)/shard_map/ppermute | solution.py:750
  72.2 7.5 %collective-permute-start.18 = (bf16[4,8,24,768]{3,2,1,0:T(8,128)(2,1)}, bf16[4,8,24,768]{3,2,1,0:T(8,128)(2,1)}, u32[]{:S(2)}, u32[]{:S(2)}) collective-permute-start(bf16[4,8,24,768]{3,2,1,0:T(8,128)(2,1)} %collective-permute-done.13.p2), channel_id=1, source_target_pairs={{0,1},{1,0},{2,3},{3,2},{4,5},{5,4},{6,7},{7,6},{8,9},{9,8},{10,11... | collective-permute-start | bytes 3538952 | tf_op jit(solution)/shard_map/ppermute | solution.py:750
  72.7 7.5 %collective-permute-start.19 = (bf16[4,8,24,768]{3,2,1,0:T(8,128)(2,1)}, bf16[4,8,24,768]{3,2,1,0:T(8,128)(2,1)}, u32[]{:S(2)}, u32[]{:S(2)}) collective-permute-start(bf16[4,8,24,768]{3,2,1,0:T(8,128)(2,1)} %collective-permute-done.14.p3), channel_id=1, source_target_pairs={{0,1},{1,0},{2,3},{3,2},{4,5},{5,4},{6,7},{7,6},{8,9},{9,8},{10,11... | collective-permute-start | bytes 3538952 | tf_op jit(solution)/shard_map/ppermute | solution.py:750
  72.7 7.0 %collective-permute-start.15 = (bf16[640,768]{1,0:T(8,128)(2,1)}, bf16[640,768]{1,0:T(8,128)(2,1)S(1)}, u32[]{:S(2)}, u32[]{:S(2)}) collective-permute-start(bf16[640,768]{1,0:T(8,128)(2,1)} %get-tuple-element.101.c), channel_id=1, source_target_pairs={{0,1},{1,0},{2,3},{3,2},{4,5},{5,4},{6,7},{7,6},{8,9},{9,8},{10,11... | collective-permute-start | bytes 2949128 | tf_op jit(solution)/shard_map/ppermute | solution.py:750
  79.7 38.8 %copy-start.7 = (bf16[640,768]{1,0:T(8,128)(2,1)}, bf16[640,768]{1,0:T(8,128)(2,1)S(1)}, u32[]{:S(2)}) copy-start(bf16[640,768]{1,0:T(8,128)(2,1)S(1)} %collective-permute-done.15.c_other) | copy-start | bytes 2949124
  79.7 1.1 copy-start.16
  79.7 1.5 copy-start.17
  118.6 12.5 %collective-permute-start.20 = (bf16[16,8,24,768]{3,2,1,0:T(8,128)(2,1)}, bf16[16,8,24,768]{3,2,1,0:T(8,128)(2,1)}, u32[]{:S(2)}, u32[]{:S(2)}) collective-permute-start(bf16[16,8,24,768]{3,2,1,0:T(8,128)(2,1)} %get-tuple-element.112), channel_id=1, source_target_pairs={{0,1},{1,0},{2,3},{3,2},{4,5},{5,4},{6,7},{7,6},{8,9},{9,8},{10,11... | collective-permute-start | bytes 14155784 | tf_op jit(solution)/shard_map/ppermute | solution.py:750
  118.8 12.2 %collective-permute-start.21 = (bf16[640,768]{1,0:T(8,128)(2,1)}, bf16[640,768]{1,0:T(8,128)(2,1)S(1)}, u32[]{:S(2)}, u32[]{:S(2)}) collective-permute-start(bf16[640,768]{1,0:T(8,128)(2,1)} %get-tuple-element.111.gatt), channel_id=1, source_target_pairs={{0,1},{1,0},{2,3},{3,2},{4,5},{5,4},{6,7},{7,6},{8,9},{9,8},{10,11... | collective-permute-start | bytes 2949128 | tf_op jit(solution)/shard_map/ppermute | solution.py:750
  119.1 11.9 %collective-permute-start.22 = (f32[16,768]{1,0:T(8,128)}, f32[16,768]{1,0:T(8,128)S(1)}, u32[]{:S(2)}, u32[]{:S(2)}) collective-permute-start(f32[16,768]{1,0:T(8,128)} %get-tuple-element.113.sums_own), channel_id=1, source_target_pairs={{0,1},{1,0},{2,3},{3,2},{4,5},{5,4},{6,7},{7,6},{8,9},{9,8},{10,11... | collective-permute-start | bytes 147464 | tf_op jit(solution)/shard_map/ppermute | solution.py:750
  131.0 1.8 copy-start.14
  131.0 1.8 copy-start.8
  131.1 7.6 %collective-permute-start.23 = (bf16[3,640,768]{2,1,0:T(8,128)(2,1)}, bf16[3,640,768]{2,1,0:T(8,128)(2,1)}, u32[]{:S(2)}, u32[]{:S(2)}) collective-permute-start(bf16[3,640,768]{2,1,0:T(8,128)(2,1)} %attention_back.1.d), channel_id=1, source_target_pairs={{0,1},{1,0},{2,3},{3,2},{4,5},{5,4},{6,7},{7,6},{8,9},{9,8},{10,11... | collective-permute-start | bytes 8847368 | tf_op jit(solution)/shard_map/ppermute | solution.py:750
  132.9 2.7 %copy-start.3 = (bf16[16,8,24,768]{3,2,1,0:T(8,128)(2,1)S(1)}, bf16[16,8,24,768]{3,2,1,0:T(8,128)(2,1)}, u32[]{:S(2)}) copy-start(bf16[16,8,24,768]{3,2,1,0:T(8,128)(2,1)} %get-tuple-element.123) | copy-start | bytes 14155780
  138.6 33.8 %collective-permute-start.24 = (bf16[4,8,24,768]{3,2,1,0:T(8,128)(2,1)S(1)}, bf16[4,8,24,768]{3,2,1,0:T(8,128)(2,1)}, u32[]{:S(2)}, u32[]{:S(2)}) collective-permute-start(bf16[4,8,24,768]{3,2,1,0:T(8,128)(2,1)S(1)} %get-tuple-element.133), channel_id=1, source_target_pairs={{0,8},{1,3},{2,10},{3,5},{4,12},{5,7},{6,14},{7,1},{8,16},{9,11},{... | collective-permute-start | bytes 3538952 | tf_op jit(solution)/shard_map/ppermute | solution.py:898
  149.6 22.9 %collective-permute-start.25 = (bf16[4,8,24,768]{3,2,1,0:T(8,128)(2,1)S(1)}, bf16[4,8,24,768]{3,2,1,0:T(8,128)(2,1)}, u32[]{:S(2)}, u32[]{:S(2)}) collective-permute-start(bf16[4,8,24,768]{3,2,1,0:T(8,128)(2,1)S(1)} %get-tuple-element.134), channel_id=1, source_target_pairs={{0,24},{1,7},{2,26},{3,1},{4,28},{5,3},{6,30},{7,5},{8,0},{9,15},{... | collective-permute-start | bytes 3538952 | tf_op jit(solution)/shard_map/ppermute | solution.py:898
  151.4 18.2 %collective-permute-start.26 = (bf16[4,2,24,768]{3,2,1,0:T(8,128)(2,1)S(1)}, bf16[4,2,24,768]{3,2,1,0:T(8,128)(2,1)S(1)}, u32[]{:S(2)}, u32[]{:S(2)}) collective-permute-start(bf16[4,2,24,768]{3,2,1,0:T(8,128)(2,1)S(1)} %get-tuple-element.136), channel_id=1, source_target_pairs={{0,64},{32,96},{64,0},{96,32},{1,65},{33,97},{65,1},{97,33},{2,66}... | collective-permute-start | bytes 884744 | tf_op jit(solution)/shard_map/ppermute | solution.py:763
  154.6 15.1 %collective-permute-start.27 = (bf16[4,2,24,768]{3,2,1,0:T(8,128)(2,1)S(1)}, bf16[4,2,24,768]{3,2,1,0:T(8,128)(2,1)S(1)}, u32[]{:S(2)}, u32[]{:S(2)}) collective-permute-start(bf16[4,2,24,768]{3,2,1,0:T(8,128)(2,1)S(1)} %get-tuple-element.137), channel_id=1, source_target_pairs={{0,32},{32,64},{64,96},{96,0},{1,33},{33,65},{65,97},{97,1},{2,34}... | collective-permute-start | bytes 884744 | tf_op jit(solution)/shard_map/ppermute | solution.py:763
  155.3 15.1 %collective-permute-start.28 = (bf16[4,2,24,768]{3,2,1,0:T(8,128)(2,1)S(1)}, bf16[4,2,24,768]{3,2,1,0:T(8,128)(2,1)}, u32[]{:S(2)}, u32[]{:S(2)}) collective-permute-start(bf16[4,2,24,768]{3,2,1,0:T(8,128)(2,1)S(1)} %get-tuple-element.138), channel_id=1, source_target_pairs={{0,96},{32,0},{64,32},{96,64},{1,97},{33,1},{65,33},{97,65},{2,98}... | collective-permute-start | bytes 884744 | tf_op jit(solution)/shard_map/ppermute | solution.py:763
  170.4 13.2 %copy-start.2 = (f32[640,768]{1,0:T(8,128)S(1)}, f32[640,768]{1,0:T(8,128)}, u32[]{:S(2)}) copy-start(f32[640,768]{1,0:T(8,128)} %get-tuple-element.139.gfs) | copy-start | bytes 5898244
  172.4 8.5 %collective-permute-start.38 = (bf16[4,2,24,768]{3,2,1,0:T(8,128)(2,1)}, bf16[4,2,24,768]{3,2,1,0:T(8,128)(2,1)S(1)}, u32[]{:S(2)}, u32[]{:S(2)}) collective-permute-start(bf16[4,2,24,768]{3,2,1,0:T(8,128)(2,1)} %add_convert_fusion.4), channel_id=1, source_target_pairs={{0,16},{1,5},{2,18},{3,7},{4,20},{5,1},{6,22},{7,3},{8,24},{9,13},... | collective-permute-start | bytes 884744 | tf_op jit(solution)/shard_map/ppermute | solution.py:904
  172.8 20.9 %collective-permute-start.29 = (bf16[4,104,768]{2,1,0:T(8,128)(2,1)}, bf16[4,104,768]{2,1,0:T(8,128)(2,1)}, u32[]{:S(2)}, u32[]{:S(2)}) collective-permute-start(bf16[4,104,768]{2,1,0:T(8,128)(2,1)} %get-tuple-element.141), channel_id=1, source_target_pairs={{0,8},{1,3},{2,10},{3,5},{4,12},{5,7},{6,14},{7,1},{8,16},{9,11},{... | collective-permute-start | bytes 1916936 | tf_op jit(solution)/shard_map/ppermute | solution.py:754
  173.9 21.1 %collective-permute-start.30 = (bf16[4,104,768]{2,1,0:T(8,128)(2,1)}, bf16[4,104,768]{2,1,0:T(8,128)(2,1)}, u32[]{:S(2)}, u32[]{:S(2)}) collective-permute-start(bf16[4,104,768]{2,1,0:T(8,128)(2,1)} %get-tuple-element.142), channel_id=1, source_target_pairs={{0,24},{1,7},{2,26},{3,1},{4,28},{5,3},{6,30},{7,5},{8,0},{9,15},{... | collective-permute-start | bytes 1916936 | tf_op jit(solution)/shard_map/ppermute | solution.py:754
  176.0 25.0 %collective-permute-start.31 = (bf16[4,104,768]{2,1,0:T(8,128)(2,1)}, bf16[4,104,768]{2,1,0:T(8,128)(2,1)}, u32[]{:S(2)}, u32[]{:S(2)}) collective-permute-start(bf16[4,104,768]{2,1,0:T(8,128)(2,1)} %get-tuple-element.143), channel_id=1, source_target_pairs={{0,16},{1,5},{2,18},{3,7},{4,20},{5,1},{6,22},{7,3},{8,24},{9,13},... | collective-permute-start | bytes 1916936 | tf_op jit(solution)/shard_map/ppermute | solution.py:754
  181.0 2.6 %copy-start.1 = (bf16[3,640,768]{2,1,0:T(8,128)(2,1)S(1)}, bf16[3,640,768]{2,1,0:T(8,128)(2,1)}, u32[]{:S(2)}) copy-start(bf16[3,640,768]{2,1,0:T(8,128)(2,1)} %attention_back.1.d) | copy-start | bytes 8847364
  183.1 23.0 %collective-permute-start.39 = (bf16[8,24,768]{2,1,0:T(8,128)(2,1)S(1)}, bf16[8,24,768]{2,1,0:T(8,128)(2,1)S(1)}, u32[]{:S(2)}, u32[]{:S(2)}) collective-permute-start(bf16[8,24,768]{2,1,0:T(8,128)(2,1)S(1)} %get-tuple-element.170), channel_id=1, source_target_pairs={{0,4},{1,17},{2,6},{3,19},{4,0},{5,21},{6,2},{7,23},{8,12},{9,25},... | collective-permute-start | bytes 884744 | tf_op jit(solution)/shard_map/ppermute | solution.py:754
  183.6 2.5 %copy-start = (bf16[32,104,768]{2,1,0:T(8,128)(2,1)S(1)}, bf16[32,104,768]{2,1,0:T(8,128)(2,1)}, u32[]{:S(2)}) copy-start(bf16[32,104,768]{2,1,0:T(8,128)(2,1)} %get-tuple-element.114.wo_block.wq.wk.wv) | copy-start | bytes 15335428
  186.1 15.0 %copy-start.10 = (bf16[4,104,768]{2,1,0:T(8,128)(2,1)S(1)}, bf16[4,104,768]{2,1,0:T(8,128)(2,1)}, u32[]{:S(2)}) copy-start(bf16[4,104,768]{2,1,0:T(8,128)(2,1)} %get-tuple-element.146) | copy-start | bytes 1916932
  191.4 15.9 %collective-permute-start.40 = (bf16[8,24,768]{2,1,0:T(8,128)(2,1)S(1)}, bf16[8,24,768]{2,1,0:T(8,128)(2,1)S(1)}, u32[]{:S(2)}, u32[]{:S(2)}) collective-permute-start(bf16[8,24,768]{2,1,0:T(8,128)(2,1)S(1)} %get-tuple-element.172), channel_id=1, source_target_pairs={{0,2},{1,9},{2,4},{3,11},{4,6},{5,13},{6,0},{7,15},{8,10},{9,17},{... | collective-permute-start | bytes 884744 | tf_op jit(solution)/shard_map/ppermute | solution.py:754
  193.6 13.8 %collective-permute-start.41 = (bf16[8,24,768]{2,1,0:T(8,128)(2,1)S(1)}, bf16[8,24,768]{2,1,0:T(8,128)(2,1)S(1)}, u32[]{:S(2)}, u32[]{:S(2)}) collective-permute-start(bf16[8,24,768]{2,1,0:T(8,128)(2,1)S(1)} %get-tuple-element.171), channel_id=1, source_target_pairs={{0,6},{1,25},{2,0},{3,27},{4,2},{5,29},{6,4},{7,31},{8,14},{9,1},{... | collective-permute-start | bytes 884744 | tf_op jit(solution)/shard_map/ppermute | solution.py:754
  202.7 9.3 %collective-permute-start.32 = (bf16[104,768]{1,0:T(8,128)(2,1)S(1)}, bf16[104,768]{1,0:T(8,128)(2,1)S(1)}, u32[]{:S(2)}, u32[]{:S(2)}) collective-permute-start(bf16[104,768]{1,0:T(8,128)(2,1)S(1)} %get-tuple-element.173), channel_id=1, source_target_pairs={{0,4},{1,17},{2,6},{3,19},{4,0},{5,21},{6,2},{7,23},{8,12},{9,25},... | collective-permute-start | bytes 479240 | tf_op jit(solution)/shard_map/ppermute | solution.py:754
  202.9 9.1 %collective-permute-start.33 = (bf16[104,768]{1,0:T(8,128)(2,1)S(1)}, bf16[104,768]{1,0:T(8,128)(2,1)S(1)}, u32[]{:S(2)}, u32[]{:S(2)}) collective-permute-start(bf16[104,768]{1,0:T(8,128)(2,1)S(1)} %get-tuple-element.175), channel_id=1, source_target_pairs={{0,2},{1,9},{2,4},{3,11},{4,6},{5,13},{6,0},{7,15},{8,10},{9,17},{... | collective-permute-start | bytes 479240 | tf_op jit(solution)/shard_map/ppermute | solution.py:754
  206.1 5.9 %collective-permute-start.34 = (bf16[104,768]{1,0:T(8,128)(2,1)S(1)}, bf16[104,768]{1,0:T(8,128)(2,1)S(1)}, u32[]{:S(2)}, u32[]{:S(2)}) collective-permute-start(bf16[104,768]{1,0:T(8,128)(2,1)S(1)} %get-tuple-element.174), channel_id=1, source_target_pairs={{0,6},{1,25},{2,0},{3,27},{4,2},{5,29},{6,4},{7,31},{8,14},{9,1},{... | collective-permute-start | bytes 479240 | tf_op jit(solution)/shard_map/ppermute | solution.py:754
  208.7 13.6 %collective-permute-start.42 = (bf16[8,24,768]{2,1,0:T(8,128)(2,1)S(1)}, bf16[8,24,768]{2,1,0:T(8,128)(2,1)S(1)}, u32[]{:S(2)}, u32[]{:S(2)}) collective-permute-start(bf16[8,24,768]{2,1,0:T(8,128)(2,1)S(1)} %add_convert_fusion.3.own), channel_id=1, source_target_pairs={{0,32},{32,64},{64,96},{96,0},{1,33},{33,65},{65,97},{97,1},{2,34}... | collective-permute-start | bytes 884744 | tf_op jit(solution)/shard_map/ppermute | solution.py:763
  208.8 13.6 %collective-permute-start.43 = (bf16[8,24,768]{2,1,0:T(8,128)(2,1)S(1)}, bf16[8,24,768]{2,1,0:T(8,128)(2,1)S(1)}, u32[]{:S(2)}, u32[]{:S(2)}) collective-permute-start(bf16[8,24,768]{2,1,0:T(8,128)(2,1)S(1)} %add_convert_fusion.3.own), channel_id=1, source_target_pairs={{0,96},{32,0},{64,32},{96,64},{1,97},{33,1},{65,33},{97,65},{2,98}... | collective-permute-start | bytes 884744 | tf_op jit(solution)/shard_map/ppermute | solution.py:763
  212.0 10.3 %collective-permute-start.44 = (bf16[8,24,768]{2,1,0:T(8,128)(2,1)S(1)}, bf16[8,24,768]{2,1,0:T(8,128)(2,1)S(1)}, u32[]{:S(2)}, u32[]{:S(2)}) collective-permute-start(bf16[8,24,768]{2,1,0:T(8,128)(2,1)S(1)} %add_convert_fusion.3.own), channel_id=1, source_target_pairs={{0,64},{32,96},{64,0},{96,32},{1,65},{33,97},{65,1},{97,33},{2,66}... | collective-permute-start | bytes 884744 | tf_op jit(solution)/shard_map/ppermute | solution.py:763
  213.3 10.8 %collective-permute-start.35 = (bf16[104,768]{1,0:T(8,128)(2,1)S(1)}, bf16[104,768]{1,0:T(8,128)(2,1)S(1)}, u32[]{:S(2)}, u32[]{:S(2)}) collective-permute-start(bf16[104,768]{1,0:T(8,128)(2,1)S(1)} %fusion.9.own), channel_id=1, source_target_pairs={{0,32},{32,64},{64,96},{96,0},{1,33},{33,65},{65,97},{97,1},{2,34}... | collective-permute-start | bytes 479240 | tf_op jit(solution)/shard_map/ppermute | solution.py:763
  214.2 10.9 %collective-permute-start.36 = (bf16[104,768]{1,0:T(8,128)(2,1)S(1)}, bf16[104,768]{1,0:T(8,128)(2,1)S(1)}, u32[]{:S(2)}, u32[]{:S(2)}) collective-permute-start(bf16[104,768]{1,0:T(8,128)(2,1)S(1)} %fusion.9.own), channel_id=1, source_target_pairs={{0,96},{32,0},{64,32},{96,64},{1,97},{33,1},{65,33},{97,65},{2,98}... | collective-permute-start | bytes 479240 | tf_op jit(solution)/shard_map/ppermute | solution.py:763
  222.4 6.8 %collective-permute-start.37 = (bf16[104,768]{1,0:T(8,128)(2,1)S(1)}, bf16[104,768]{1,0:T(8,128)(2,1)S(1)}, u32[]{:S(2)}, u32[]{:S(2)}) collective-permute-start(bf16[104,768]{1,0:T(8,128)(2,1)S(1)} %fusion.9.own), channel_id=1, source_target_pairs={{0,64},{32,96},{64,0},{96,32},{1,65},{33,97},{65,1},{97,33},{2,66}... | collective-permute-start | bytes 479240 | tf_op jit(solution)/shard_map/ppermute | solution.py:763
  (4 other events, 3.3 us)

commit v3 on v0

--- a/solution.py
+++ b/solution.py
@@ -65,6 +65,22 @@
             even, odd = value[low : low + each], value[low + each : low + 2 * each]
             keep[jnp.where(first, p0, p1), at] = jnp.where(first, even, odd)
             give[jnp.where(first, p1, p0), at] = jnp.where(first, odd, even)
+
+
+def deal_apart(keep, gives, spare, pos, value, at, each):
+    first = pos[2] == 0
+    for x in range(RING):
+        for z in range(RING):
+            p0, p1 = places(pos, x, z)
+            low = 2 * (x * RING + z) * each
+            even, odd = value[low : low + each], value[low + each : low + 2 * each]
+            keep[jnp.where(first, p0, p1), at] = jnp.where(first, even, odd)
+            spare[x * RING + z, :each] = jnp.where(first, odd, even)
+    for a, give in enumerate(gives):
+        for b in range(RING):
+            xa, zb = (pos[0] + a) & (RING - 1), (pos[1] + b) & (RING - 1)
+            xb, za = (pos[0] + b) & (RING - 1), (pos[1] + a) & (RING - 1)
+            give[b, at] = spare[jnp.where(first, xb * RING + za, xa * RING + zb), :each]
 
 
 def spread(owners, width):
@@ -573,9 +589,10 @@
 
 def weight_back_body(
     dims, pos, gatt_cols, c, dq, dk, dv, xs, xl, sums_f, dub,
-    keep, give,
-    x_t, c_t, sums,
+    keep, g0, g1, g2, g3,
+    x_t, c_t, sums, spare,
 ):
+    gives = (g0, g1, g2, g3)
     step = pl.program_id(0)
     short_rows = dims[0]
     rows, width = c.shape
@@ -591,15 +608,16 @@
         c_t[...] = c[...].T
         sums[...] = sums_f[...]
 
-    deal(keep, give, pos, nn(c_t[...], gatt_cols[...]).astype(BF16), slice(3 * each, 4 * each), each)
+    deal_apart(keep, gives, spare, pos, nn(c_t[...], gatt_cols[...]).astype(BF16), slice(3 * each, 4 * each), each)
     for i, d in enumerate((dq, dk, dv)):
         grad = nn(x_t[...], d[...])
-        deal(keep, give, pos, grad[:width].astype(BF16), slice(i * each, (i + 1) * each), each)
+        deal_apart(keep, gives, spare, pos, grad[:width].astype(BF16), slice(i * each, (i + 1) * each), each)
         if i != 1:
             at = QB if i == 0 else VB
             sums[at : at + 1, at_cols] = grad[width : width + 1]
     keep[:, 4 * each :] = jnp.zeros((CHIPS, 8, cols), BF16)
-    give[:, 4 * each :] = jnp.zeros((CHIPS, 8, cols), BF16)
+    for give in gives:
+        give[:, 4 * each :] = jnp.zeros((RING, 8, cols), BF16)
 
     @pl.when(step == pl.num_programs(0) - 1)
     def _():
@@ -613,7 +631,7 @@
         put = (iota((cols, inner), 0) == column_rest(cols, inner, inner // SHARDS)).astype(BF16)
         wide = nt(jnp.where(spread(SHARDS, inner), dub[...], 0.0).astype(BF16), put)
         both = jnp.concatenate([line[:, None], wide[:, None], jnp.zeros((SHARDS, 6, cols), F32)], axis=1)
-        deal(keep, give, pos, both.reshape(SHARDS * 8, cols).astype(BF16), slice(4 * each, 4 * each + 8), 8)
+        deal_apart(keep, gives, spare, pos, both.reshape(SHARDS * 8, cols).astype(BF16), slice(4 * each, 4 * each + 8), 8)
 
 
 def weight_back(pos, gatt, c, dq, dk, dv, xs, xl, sums_f, dub, dims):
@@ -631,12 +649,16 @@
                 cols, whole(rows, width), cols, cols, cols,
                 whole(*xs.shape), whole(*xl.shape), whole(8, width), whole(*dub.shape),
             ],
-            out_specs=[dealt, dealt],
+            out_specs=[dealt, *[pl.BlockSpec((RING, 4 * each + 8, step), lambda g, *_: (0, 0, g))] * RING],
             scratch_shapes=[
                 pltpu.VMEM((width + 16, rows), BF16), pltpu.VMEM((width, rows), BF16), pltpu.VMEM((8, width), F32),
+                pltpu.VMEM((CHIPS, each, step), BF16),
             ],
         ),
-        out_shape=[jax.ShapeDtypeStruct((CHIPS, 4 * each + 8, width), BF16)] * 2,
+        out_shape=[
+            jax.ShapeDtypeStruct((CHIPS, 4 * each + 8, width), BF16),
+            *[jax.ShapeDtypeStruct((RING, 4 * each + 8, width), BF16)] * RING,
+        ],
         compiler_params=params(BACK_MIB),
         cost_estimate=cost(8 * rows * width * width, 12e6),
         name="weight_back",
@@ -697,6 +719,12 @@
     return parts
 
 
+def pair_sum_apart(keep, gots):
+    return [
+        (keep[d * RING : (d + 1) * RING].astype(F32) + got.astype(F32)).astype(BF16) for d, got in enumerate(gots)
+    ]
+
+
 def four_sum(own, left, right, far):
     return (own.astype(F32) + far.astype(F32)) + (left.astype(F32) + right.astype(F32))
 
@@ -729,7 +757,10 @@
 
 def second_turn(own, left, right, far):
     parts = [four_sum(own[d], left[d], right[d], far[d]).astype(BF16) for d in range(RING)]
-    own = four_sum(parts[0], *around(parts, 1)).astype(BF16)
+    return four_sum(parts[0], *around(parts, 1)).astype(BF16)
+
+
+def across_replicas(own):
     return own, *(lax.ppermute(own, "rep", [(i, (i + d) % RING) for i in range(RING)]) for d in (1, 3, 2))
 
 
@@ -822,14 +853,18 @@
     parts_f = pair_sum(keep_f, swap_cores(give_f))
     dv, *parts_f = lax.optimization_barrier((dv, *parts_f))
     around_f = around(parts_f, 0)
-    keep_a, give_a = weight_back(pos, gatt, c, dq, dk, dv, xs, xl, sums_f, dub, dims)
-    parts_a = pair_sum(keep_a, swap_cores(give_a))
+    keep_a, *gives_a = weight_back(pos, gatt, c, dq, dk, dv, xs, xl, sums_f, dub, dims)
+    keep_a, *around_f = lax.optimization_barrier((keep_a, *around_f))
+    parts_a = pair_sum_apart(keep_a, [swap_cores(give) for give in gives_a])
     gfs, *parts_a = lax.optimization_barrier((gfs, *parts_a))
     around_a = around(parts_a, 0)
     grad_s, grad_l = input_back(gfs, dq, dk, dv, gathered_a, dims)
     grad_s, *around_a = lax.optimization_barrier((grad_s, *around_a))
-    up, down = finish_feed(second_turn(parts_f[0], *around_f), each, inner, tall)
-    w_in, w_out, *vectors = finish_attention(second_turn(parts_a[0], *around_a), tall)
+    own_f = second_turn(parts_f[0], *around_f)
+    own_f, *around_a = lax.optimization_barrier((own_f, *around_a))
+    up, down = finish_feed(across_replicas(own_f), each, inner, tall)
+    own_a = second_turn(parts_a[0], *around_a)
+    w_in, w_out, *vectors = finish_attention(across_replicas(own_a), tall)
     vectors = [x.reshape(-1) for x in vectors]
     return (
         out_s.reshape(short_tokens.shape), out_l.reshape(long_tokens.shape),

time: 216 us -> 212 us (0.981)
  starting transfers between devices: 51.4 us -> 47 us
    ppermute x21, starting transfers between devices: 38.3 us -> 33.9 us  [around(): lax.ppermute(v[d] if isinstance(v, (list, tuple)) else v, 'shard', turn(d...]
    convert_element_type x2 -> x1, other arithmetic: 6.32 us -> 3.89 us  [pair_sum(): parts.append((keep[at].astype(F32) + got[at].astype(F32)).astype(BF16))]
    convert_element_type x2 -> x3, other arithmetic: 0.42 us -> 2.83 us  [the longest x1 2.41 us: pair_sum_apart(): (keep[d * RING:(d + 1) * RING].astype(F32) + got.astype(F32)).astype(BF16)]
    ppermute x10 -> x13, waiting for transfers between devices: 7.66 us -> 7.67 us  [swap_cores(): return lax.ppermute(v, 'shard', [(i, i ^ 1) for i in range(SHARDS)])]
  transfers between devices with their start and end apart: 37 -> 40, of which waited for: 18 -> 22; matrix products, arithmetic and copies ran while one was open for 2% -> 2% of each run, Pallas kernels for 17% -> 23%
where the time goes in v3:
time: 212 us
  Pallas kernels  88.4 us (42%)
  waiting for transfers between devices  62.5 us (29%)
  starting transfers between devices  47 us (22%)
  other arithmetic  8.21 us (4%)
  local copies, waits for them, and re-layouts  4.52 us (2%)
    ppermute x21, waiting for transfers between devices, around(): lax.ppermute(v[d] if isinstance(v, (list, tuple)) else v, 'shard', turn(d...  45.8 us
    pallas_call x1, Pallas kernels, feed(): pl.pallas_call(functools.partial(feed_body, dims), in_specs=[SCALARS] * 3...  37.3 us
    ppermute x21, starting transfers between devices, around(): lax.ppermute(v[d] if isinstance(v, (list, tuple)) else v, 'shard', turn(d...  33.9 us
    pallas_call x1, Pallas kernels, attention_forward(): pl.pallas_call(functools.partial(attention_forward_body, dims), grid_spec...  19 us
    pallas_call x1, Pallas kernels, attention_back(): pl.pallas_call(functools.partial(attention_back_body, dims), grid=(width...  11.8 us
    pallas_call x1, Pallas kernels, weight_back(): pl.pallas_call(functools.partial(weight_back_body, dims), grid_spec=pltpu...  11.2 us
    ppermute x6, starting transfers between devices, across_replicas(): lax.ppermute(own, 'rep', [(i, (i + d) % RING) for i in range(RING)])  11.1 us
    ppermute x6, waiting for transfers between devices, across_replicas(): lax.ppermute(own, 'rep', [(i, (i + d) % RING) for i in range(RING)])  9 us
  transfers between devices with their start and end apart: 40, of which 22 were waited for; matrix products, arithmetic and copies ran while one was open for 2% of the time, Pallas kernels for 23%

profile of v3, /device:TPU:0, one launch (start us, length us, event | category | flops | bytes accessed | tf_op | source)
XLA Modules:
  0.0 211.7 jit_solution(10134432787638805894)
XLA Ops:
  0.7 2.0 pack.1
  2.7 4.0 %collective-permute-start.2 = (bf16[296,768]{1,0:T(8,128)(2,1)}, bf16[296,768]{1,0:T(8,128)(2,1)S(1)}, u32[]{:S(2)}, u32[]{:S(2)}) collective-permute-start(bf16[296,768]{1,0:T(8,128)(2,1)} %pack.1), channel_id=1, source_target_pairs={{0,4},{1,17},{2,6},{3,19},{4,0},{5,21},{6,2},{7,23},{8,12},{9,25},... | collective-permute-start | bytes 1363976 | tf_op jit(solution)/shard_map/ppermute | solution.py:751
  6.6 0.7 collective-permute-start.1
  7.3 1.3 collective-permute-start
  8.7 1.0 slice_bitcast_fusion.3
  9.6 3.7 %collective-permute-done.2 = bf16[296,768]{1,0:T(8,128)(2,1)S(1)} collective-permute-done((bf16[296,768]{1,0:T(8,128)(2,1)}, bf16[296,768]{1,0:T(8,128)(2,1)S(1)}, u32[]{:S(2)}, u32[]{:S(2)}) %collective-permute-start.2) | collective-permute-done | bytes 454688 | tf_op jit(solution)/shard_map/ppermute | solution.py:751
  13.4 5.8 %collective-permute-done.1 = bf16[296,768]{1,0:T(8,128)(2,1)S(1)} collective-permute-done((bf16[296,768]{1,0:T(8,128)(2,1)}, bf16[296,768]{1,0:T(8,128)(2,1)S(1)}, u32[]{:S(2)}, u32[]{:S(2)}) %collective-permute-start.1) | collective-permute-done | bytes 454688 | tf_op jit(solution)/shard_map/ppermute | solution.py:751
  19.3 3.1 %collective-permute-start.5 = (bf16[4,104,768]{2,1,0:T(8,128)(2,1)S(1)}, bf16[4,104,768]{2,1,0:T(8,128)(2,1)S(1)}, u32[]{:S(2)}, u32[]{:S(2)}) collective-permute-start(bf16[4,104,768]{2,1,0:T(8,128)(2,1)S(1)} %pad_maximum_fusion.1.p0), channel_id=1, source_target_pairs={{0,16},{1,5},{2,18},{3,7},{4,20},{5,1},{6,22},{7,3},{8,24},{9,13},... | collective-permute-start | bytes 1916936 | tf_op jit(solution)/shard_map/ppermute | solution.py:751
  22.4 1.1 collective-permute-start.4
  23.6 0.9 collective-permute-start.3
  24.5 7.0 %collective-permute-done.5.p3 = bf16[4,104,768]{2,1,0:T(8,128)(2,1)S(1)} collective-permute-done((bf16[4,104,768]{2,1,0:T(8,128)(2,1)S(1)}, bf16[4,104,768]{2,1,0:T(8,128)(2,1)S(1)}, u32[]{:S(2)}, u32[]{:S(2)}) %collective-permute-start.5) | collective-permute-done | bytes 639008 | tf_op jit(solution)/shard_map/ppermute | solution.py:751
  31.6 0.8 copy-done.13
  32.8 3.1 %collective-permute-start.12 = (bf16[4,8,24,768]{3,2,1,0:T(8,128)(2,1)S(1)}, bf16[4,8,24,768]{3,2,1,0:T(8,128)(2,1)S(1)}, u32[]{:S(2)}, u32[]{:S(2)}) collective-permute-start(bf16[4,8,24,768]{3,2,1,0:T(8,128)(2,1)S(1)} %pad_maximum_fusion.p0), channel_id=1, source_target_pairs={{0,16},{1,5},{2,18},{3,7},{4,20},{5,1},{6,22},{7,3},{8,24},{9,13},... | collective-permute-start | bytes 3538952 | tf_op jit(solution)/shard_map/ppermute | solution.py:751
  35.9 1.1 collective-permute-start.11
  37.1 1.4 collective-permute-done.4.p2
  38.4 1.4 collective-permute-start.10
  39.8 0.6 collective-permute-start.7
  40.6 0.6 pad_add_fusion.pos
  41.2 0.8 collective-permute-done.8.p6
  42.2 0.9 collective-permute-done.7.p5
  43.1 19.0 %attention_forward.1 = (bf16[640,768]{1,0:T(8,128)(2,1)}, bf16[640,768]{1,0:T(8,128)(2,1)}, bf16[640,768]{1,0:T(8,128)(2,1)}, bf16[640,768]{1,0:T(8,128)(2,1)}, ...) custom-call(s32[2]{0:T(128)} %slen.3, s32[2]{0:T(128)} %llen.3, ...), custom_call_target="tpu_custom_call" | custom-call | flops 3019898880 | bytes 20000000 | tf_op jit(solution)/shard_map/attention_forward/pallas_call | solution.py:289
  62.1 1.6 collective-permute-done.11.p2
  63.7 0.5 collective-permute-start.15
  64.3 2.5 %collective-permute-done.14.p5 = bf16[4,8,24,768]{3,2,1,0:T(8,128)(2,1)S(1)} collective-permute-done((bf16[4,8,24,768]{3,2,1,0:T(8,128)(2,1)}, bf16[4,8,24,768]{3,2,1,0:T(8,128)(2,1)S(1)}, u32[]{:S(2)}, u32[]{:S(2)}) %collective-permute-start.14) | collective-permute-done | bytes 1179680 | tf_op jit(solution)/shard_map/ppermute | solution.py:747
  66.8 3.4 %collective-permute-done.15.p6 = bf16[4,8,24,768]{3,2,1,0:T(8,128)(2,1)S(1)} collective-permute-done((bf16[4,8,24,768]{3,2,1,0:T(8,128)(2,1)}, bf16[4,8,24,768]{3,2,1,0:T(8,128)(2,1)S(1)}, u32[]{:S(2)}, u32[]{:S(2)}) %collective-permute-start.15) | collective-permute-done | bytes 1179680 | tf_op jit(solution)/shard_map/ppermute | solution.py:747
  70.2 1.0 copy-done.11
  71.2 1.0 copy-done.12
  72.2 37.3 %feed.1 = (bf16[16,8,24,768]{3,2,1,0:T(8,128)(2,1)}, bf16[16,8,24,768]{3,2,1,0:T(8,128)(2,1)}, bf16[128,768]{1,0:T(8,128)(2,1)}, bf16[512,768]{1,0:T(8,128)(2,1)...) custom-call(s32[2]{0:T(128)} %slen.3, s32[2]{0:T(128)} %llen.3, ...), custom_call_target="tpu_custom_call" | custom-call | flops 18119393280 | bytes 30000000 | tf_op jit(solution)/shard_map/feed/pallas_call | solution.py:506
  109.7 11.8 %attention_back.1 = (bf16[640,768]{1,0:T(8,128)(2,1)}, bf16[640,768]{1,0:T(8,128)(2,1)}, bf16[640,768]{1,0:T(8,128)(2,1)}) custom-call(bf16[640,768]{1,0:T(8,128)(2,1)} %get-tuple-element.100.gatt.gatt_cols, bf16[32,104,768]{2,1,0:T(8,128)(2,1)} %get-tuple-element.102.wo_block.wq.wk.wv, bf16[640,768]{1,0:T(8,128)(2,1)} %get-tuple-element.103.q, ...), custom_call_target="tpu_custom_call" | custom-call | flops 3019898880 | bytes 15000000 | tf_op jit(solution)/shard_map/attention_back/pallas_call | solution.py:571
  121.6 3.9 %add_convert_fusion = (bf16[4,8,24,768]{3,2,1,0:T(8,128)(2,1)}, bf16[4,8,24,768]{3,2,1,0:T(8,128)(2,1)}, bf16[4,8,24,768]{3,2,1,0:T(8,128)(2,1)}, bf16[4,8,24,768]{3,2,1,0:T(8,128)(2,1)S(1)}) fusion(bf16[16,8,24,768]{3,2,1,0:T(8,128)(2,1)} %collective-permute-done.17, bf16[16,8,24,768]{3,2,1,0:T(8,128)(2,1)S(1)} %bitcast.66), kind=kLoop, calls=%fused_computation | loop fusion | flops 9437184 | bytes 14155776 | tf_op jit(solution)/shard_map/convert_element_type | solution.py:718
  125.5 1.4 collective-permute-start.18
  126.9 1.8 collective-permute-start.19
  128.7 1.7 collective-permute-start.20
  130.4 11.2 %weight_back.1 = (bf16[16,104,768]{2,1,0:T(8,128)(2,1)}, bf16[4,104,768]{2,1,0:T(8,128)(2,1)}, bf16[4,104,768]{2,1,0:T(8,128)(2,1)}, bf16[4,104,768]{2,1,0:T(8,128)(2,1)}, bf16[4,104,768]{2,1,0:T(8,128)(2,1)}) custom-call(s32[3]{0:T(128)} %pad_add_fusion.pos, bf16[640,768]{1,0:T(8,128)(2,1)} %get-tuple-element.100.gatt.gatt_cols, ...), custom_call_target="tpu_custom_call" | custom-call | flops 3019898880 | bytes 12000000 | tf_op jit(solution)/shard_map/weight_back/pallas_call | solution.py:643
  141.7 0.5 collective-permute-start.22
  142.2 0.9 collective-permute-done.18
  143.1 12.3 %collective-permute-done.19 = bf16[4,8,24,768]{3,2,1,0:T(8,128)(2,1)S(1)} collective-permute-done((bf16[4,8,24,768]{3,2,1,0:T(8,128)(2,1)}, bf16[4,8,24,768]{3,2,1,0:T(8,128)(2,1)S(1)}, u32[]{:S(2)}, u32[]{:S(2)}) %collective-permute-start.19) | collective-permute-done | bytes 1179680 | tf_op jit(solution)/shard_map/ppermute | solution.py:751
  155.4 1.2 collective-permute-done.20
  157.1 2.5 %collective-permute-start.28 = (bf16[8,24,768]{2,1,0:T(8,128)(2,1)S(1)}, bf16[8,24,768]{2,1,0:T(8,128)(2,1)S(1)}, u32[]{:S(2)}, u32[]{:S(2)}) collective-permute-start(bf16[8,24,768]{2,1,0:T(8,128)(2,1)S(1)} %get-tuple-element.161), channel_id=1, source_target_pairs={{0,4},{1,17},{2,6},{3,19},{4,0},{5,21},{6,2},{7,23},{8,12},{9,25},... | collective-permute-start | bytes 884744 | tf_op jit(solution)/shard_map/ppermute | solution.py:751
  159.6 2.4 %add_convert_fusion.4 = (bf16[4,104,768]{2,1,0:T(8,128)(2,1)S(1)}, bf16[4,104,768]{2,1,0:T(8,128)(2,1)S(1)}, bf16[4,104,768]{2,1,0:T(8,128)(2,1)S(1)}, bf16[4,104,768]{2,1,0:T(8,128)(2,1)S(1)}) fusion(bf16[4,104,768]{2,1,0:T(8,128)(2,1)S(1)} %collective-permute-done.24, bf16[16,104,768]{2,1,0:T(8,128)(2,1)} %get-tuple-element.120, ...), kind=kLoop, calls=%fused_computation.4 | loop fusion | flops 5111808 | bytes 7667712 | tf_op jit(solution)/shard_map/convert_element_type | solution.py:724
  162.1 1.5 collective-permute-start.25
  163.5 1.8 collective-permute-start.26
  165.4 0.6 collective-permute-start.27
  166.0 1.9 collective-permute-start.30
  168.1 5.4 %input_back.1 = (f32[128,768]{1,0:T(8,128)}, f32[512,768]{1,0:T(8,128)}) custom-call(f32[640,768]{1,0:T(8,128)S(1)} %copy-done, bf16[640,768]{1,0:T(8,128)(2,1)S(1)} %copy-done.1, bf16[640,768]{1,0:T(8,128)(2,1)S(1)} %copy-done.2, bf16[640,768]{1,0:T(8,128)(2,1)S(1)} %copy-done.3, bf16[32,104,768]{2,1,0:T(8,128)(2,1)S(1)} %bitcast.64, ...), custom_call_target="tpu_custom_call" | custom-call | flops 2264924160 | bytes 12000000 | tf_op jit(solution)/shard_map/input_back/pallas_call | solution.py:698
  173.4 8.0 %collective-permute-done.30 = bf16[8,24,768]{2,1,0:T(8,128)(2,1)S(1)} collective-permute-done((bf16[8,24,768]{2,1,0:T(8,128)(2,1)S(1)}, bf16[8,24,768]{2,1,0:T(8,128)(2,1)S(1)}, u32[]{:S(2)}, u32[]{:S(2)}) %collective-permute-start.30) | collective-permute-done | bytes 294944 | tf_op jit(solution)/shard_map/ppermute | solution.py:751
  181.5 1.2 collective-permute-done.29
  183.3 1.0 collective-permute-done.27
  184.6 1.8 collective-permute-start.31
  186.4 2.0 collective-permute-start.33
  188.4 3.2 %collective-permute-start.39 = (bf16[8,24,768]{2,1,0:T(8,128)(2,1)S(1)}, bf16[8,24,768]{2,1,0:T(8,128)(2,1)S(1)}, u32[]{:S(2)}, u32[]{:S(2)}) collective-permute-start(bf16[8,24,768]{2,1,0:T(8,128)(2,1)S(1)} %fusion.1.own), channel_id=1, source_target_pairs={{0,64},{32,96},{64,0},{96,32},{1,65},{33,97},{65,1},{97,33},{2,66}... | collective-permute-start | bytes 884744 | tf_op jit(solution)/shard_map/ppermute | solution.py:764
  191.6 1.1 collective-permute-start.38
  192.7 1.0 collective-permute-start.37
  193.6 1.3 collective-permute-done.32
  195.0 3.3 %collective-permute-start.36 = (bf16[104,768]{1,0:T(8,128)(2,1)S(1)}, bf16[104,768]{1,0:T(8,128)(2,1)S(1)}, u32[]{:S(2)}, u32[]{:S(2)}) collective-permute-start(bf16[104,768]{1,0:T(8,128)(2,1)S(1)} %fusion.3.own), channel_id=1, source_target_pairs={{0,64},{32,96},{64,0},{96,32},{1,65},{33,97},{65,1},{97,33},{2,66}... | collective-permute-start | bytes 479240 | tf_op jit(solution)/shard_map/ppermute | solution.py:764
  198.3 1.1 collective-permute-start.35
  199.4 0.5 collective-permute-done.39.far
  199.9 1.6 collective-permute-start.34
  201.4 5.1 %collective-permute-done.38.right = bf16[8,24,768]{2,1,0:T(8,128)(2,1)S(1)} collective-permute-done((bf16[8,24,768]{2,1,0:T(8,128)(2,1)S(1)}, bf16[8,24,768]{2,1,0:T(8,128)(2,1)S(1)}, u32[]{:S(2)}, u32[]{:S(2)}) %collective-permute-start.38) | collective-permute-done | bytes 294944 | tf_op jit(solution)/shard_map/ppermute | solution.py:764
  206.5 0.8 collective-permute-done.37.left
  207.3 0.9 finish_feed.1
  208.2 0.7 collective-permute-done.36.far
  208.9 2.0 collective-permute-done.35.right
  210.9 0.8 finish_attention.1
  (86 shorter events, 3.1 us)
Async XLA Ops:
  2.7 10.7 %collective-permute-start.2 = (bf16[296,768]{1,0:T(8,128)(2,1)}, bf16[296,768]{1,0:T(8,128)(2,1)S(1)}, u32[]{:S(2)}, u32[]{:S(2)}) collective-permute-start(bf16[296,768]{1,0:T(8,128)(2,1)} %pack.1), channel_id=1, source_target_pairs={{0,4},{1,17},{2,6},{3,19},{4,0},{5,21},{6,2},{7,23},{8,12},{9,25},... | collective-permute-start | bytes 1363976 | tf_op jit(solution)/shard_map/ppermute | solution.py:751
  6.6 12.6 %collective-permute-start.1 = (bf16[296,768]{1,0:T(8,128)(2,1)}, bf16[296,768]{1,0:T(8,128)(2,1)S(1)}, u32[]{:S(2)}, u32[]{:S(2)}) collective-permute-start(bf16[296,768]{1,0:T(8,128)(2,1)} %pack.1), channel_id=1, source_target_pairs={{0,6},{1,25},{2,0},{3,27},{4,2},{5,29},{6,4},{7,31},{8,14},{9,1},{... | collective-permute-start | bytes 1363976 | tf_op jit(solution)/shard_map/ppermute | solution.py:751
  7.3 11.9 %collective-permute-start = (bf16[296,768]{1,0:T(8,128)(2,1)}, bf16[296,768]{1,0:T(8,128)(2,1)S(1)}, u32[]{:S(2)}, u32[]{:S(2)}) collective-permute-start(bf16[296,768]{1,0:T(8,128)(2,1)} %pack.1), channel_id=1, source_target_pairs={{0,2},{1,9},{2,4},{3,11},{4,6},{5,13},{6,0},{7,15},{8,10},{9,17},{... | collective-permute-start | bytes 1363976 | tf_op jit(solution)/shard_map/ppermute | solution.py:751
  9.6 21.8 %copy-start.4 = (bf16[296,768]{1,0:T(8,128)(2,1)S(1)}, bf16[296,768]{1,0:T(8,128)(2,1)}, u32[]{:S(2)}) copy-start(bf16[296,768]{1,0:T(8,128)(2,1)} %pack.1) | copy-start | bytes 1363972
  13.4 18.1 %copy-start.5 = (bf16[296,768]{1,0:T(8,128)(2,1)}, bf16[296,768]{1,0:T(8,128)(2,1)S(1)}, u32[]{:S(2)}) copy-start(bf16[296,768]{1,0:T(8,128)(2,1)S(1)} %collective-permute-done.2) | copy-start | bytes 1363972
  19.3 12.2 %copy-start.7 = (bf16[4,104,768]{2,1,0:T(8,128)(2,1)}, bf16[4,104,768]{2,1,0:T(8,128)(2,1)S(1)}, u32[]{:S(2)}) copy-start(bf16[4,104,768]{2,1,0:T(8,128)(2,1)S(1)} %pad_maximum_fusion.1.p0) | copy-start | bytes 1916932
  19.3 12.1 %collective-permute-start.5 = (bf16[4,104,768]{2,1,0:T(8,128)(2,1)S(1)}, bf16[4,104,768]{2,1,0:T(8,128)(2,1)S(1)}, u32[]{:S(2)}, u32[]{:S(2)}) collective-permute-start(bf16[4,104,768]{2,1,0:T(8,128)(2,1)S(1)} %pad_maximum_fusion.1.p0), channel_id=1, source_target_pairs={{0,16},{1,5},{2,18},{3,7},{4,20},{5,1},{6,22},{7,3},{8,24},{9,13},... | collective-permute-start | bytes 1916936 | tf_op jit(solution)/shard_map/ppermute | solution.py:751
  22.4 13.5 %collective-permute-start.6 = (bf16[4,104,768]{2,1,0:T(8,128)(2,1)S(1)}, bf16[4,104,768]{2,1,0:T(8,128)(2,1)S(1)}, u32[]{:S(2)}, u32[]{:S(2)}) collective-permute-start(bf16[4,104,768]{2,1,0:T(8,128)(2,1)S(1)} %pad_maximum_fusion.1.p0), channel_id=1, source_target_pairs={{0,1},{1,0},{2,3},{3,2},{4,5},{5,4},{6,7},{7,6},{8,9},{9,8},{10,11... | collective-permute-start | bytes 1916936 | tf_op jit(solution)/shard_map/ppermute | solution.py:747
  22.4 16.0 %collective-permute-start.4 = (bf16[4,104,768]{2,1,0:T(8,128)(2,1)S(1)}, bf16[4,104,768]{2,1,0:T(8,128)(2,1)}, u32[]{:S(2)}, u32[]{:S(2)}) collective-permute-start(bf16[4,104,768]{2,1,0:T(8,128)(2,1)S(1)} %pad_maximum_fusion.1.p0), channel_id=1, source_target_pairs={{0,24},{1,7},{2,26},{3,1},{4,28},{5,3},{6,30},{7,5},{8,0},{9,15},{... | collective-permute-start | bytes 1916936 | tf_op jit(solution)/shard_map/ppermute | solution.py:751
  23.6 16.2 %collective-permute-start.3 = (bf16[4,104,768]{2,1,0:T(8,128)(2,1)S(1)}, bf16[4,104,768]{2,1,0:T(8,128)(2,1)}, u32[]{:S(2)}, u32[]{:S(2)}) collective-permute-start(bf16[4,104,768]{2,1,0:T(8,128)(2,1)S(1)} %pad_maximum_fusion.1.p0), channel_id=1, source_target_pairs={{0,8},{1,3},{2,10},{3,5},{4,12},{5,7},{6,14},{7,1},{8,16},{9,11},{... | collective-permute-start | bytes 1916936 | tf_op jit(solution)/shard_map/ppermute | solution.py:751
  31.4 0.9 copy-start.13
  31.4 8.3 %collective-permute-start.9 = (bf16[4,104,768]{2,1,0:T(8,128)(2,1)S(1)}, bf16[4,104,768]{2,1,0:T(8,128)(2,1)S(1)}, u32[]{:S(2)}, u32[]{:S(2)}) collective-permute-start(bf16[4,104,768]{2,1,0:T(8,128)(2,1)S(1)} %collective-permute-done.5.p3), channel_id=1, source_target_pairs={{0,1},{1,0},{2,3},{3,2},{4,5},{5,4},{6,7},{7,6},{8,9},{9,8},{10,11... | collective-permute-start | bytes 1916936 | tf_op jit(solution)/shard_map/ppermute | solution.py:747
  31.5 1.2 slice-start.4
  32.8 29.3 %copy-start.6 = (bf16[4,8,24,768]{3,2,1,0:T(8,128)(2,1)}, bf16[4,8,24,768]{3,2,1,0:T(8,128)(2,1)S(1)}, u32[]{:S(2)}) copy-start(bf16[4,8,24,768]{3,2,1,0:T(8,128)(2,1)S(1)} %pad_maximum_fusion.p0) | copy-start | bytes 3538948
  32.8 29.3 %collective-permute-start.12 = (bf16[4,8,24,768]{3,2,1,0:T(8,128)(2,1)S(1)}, bf16[4,8,24,768]{3,2,1,0:T(8,128)(2,1)S(1)}, u32[]{:S(2)}, u32[]{:S(2)}) collective-permute-start(bf16[4,8,24,768]{3,2,1,0:T(8,128)(2,1)S(1)} %pad_maximum_fusion.p0), channel_id=1, source_target_pairs={{0,16},{1,5},{2,18},{3,7},{4,20},{5,1},{6,22},{7,3},{8,24},{9,13},... | collective-permute-start | bytes 3538952 | tf_op jit(solution)/shard_map/ppermute | solution.py:751
  35.9 3.9 %copy-start.14 = (bf16[4,104,768]{2,1,0:T(8,128)(2,1)}, bf16[4,104,768]{2,1,0:T(8,128)(2,1)S(1)}, u32[]{:S(2)}) copy-start(bf16[4,104,768]{2,1,0:T(8,128)(2,1)S(1)} %collective-permute-done.6.p4) | copy-start | bytes 1916932
  35.9 27.8 %collective-permute-start.11 = (bf16[4,8,24,768]{3,2,1,0:T(8,128)(2,1)S(1)}, bf16[4,8,24,768]{3,2,1,0:T(8,128)(2,1)}, u32[]{:S(2)}, u32[]{:S(2)}) collective-permute-start(bf16[4,8,24,768]{3,2,1,0:T(8,128)(2,1)S(1)} %pad_maximum_fusion.p0), channel_id=1, source_target_pairs={{0,24},{1,7},{2,26},{3,1},{4,28},{5,3},{6,30},{7,5},{8,0},{9,15},{... | collective-permute-start | bytes 3538952 | tf_op jit(solution)/shard_map/ppermute | solution.py:751
  38.4 25.3 %collective-permute-start.10 = (bf16[4,8,24,768]{3,2,1,0:T(8,128)(2,1)S(1)}, bf16[4,8,24,768]{3,2,1,0:T(8,128)(2,1)}, u32[]{:S(2)}, u32[]{:S(2)}) collective-permute-start(bf16[4,8,24,768]{3,2,1,0:T(8,128)(2,1)S(1)} %pad_maximum_fusion.p0), channel_id=1, source_target_pairs={{0,8},{1,3},{2,10},{3,5},{4,12},{5,7},{6,14},{7,1},{8,16},{9,11},{... | collective-permute-start | bytes 3538952 | tf_op jit(solution)/shard_map/ppermute | solution.py:751
  39.8 2.3 %collective-permute-start.8 = (bf16[4,104,768]{2,1,0:T(8,128)(2,1)}, bf16[4,104,768]{2,1,0:T(8,128)(2,1)S(1)}, u32[]{:S(2)}, u32[]{:S(2)}) collective-permute-start(bf16[4,104,768]{2,1,0:T(8,128)(2,1)} %collective-permute-done.4.p2), channel_id=1, source_target_pairs={{0,1},{1,0},{2,3},{3,2},{4,5},{5,4},{6,7},{7,6},{8,9},{9,8},{10,11... | collective-permute-start | bytes 1916936 | tf_op jit(solution)/shard_map/ppermute | solution.py:747
  39.8 0.8 copy-start.15
  39.8 3.3 %collective-permute-start.7 = (bf16[4,104,768]{2,1,0:T(8,128)(2,1)}, bf16[4,104,768]{2,1,0:T(8,128)(2,1)}, u32[]{:S(2)}, u32[]{:S(2)}) collective-permute-start(bf16[4,104,768]{2,1,0:T(8,128)(2,1)} %collective-permute-done.3.p1), channel_id=1, source_target_pairs={{0,1},{1,0},{2,3},{3,2},{4,5},{5,4},{6,7},{7,6},{8,9},{9,8},{10,11... | collective-permute-start | bytes 1916936 | tf_op jit(solution)/shard_map/ppermute | solution.py:747
  42.1 1.0 copy-start.16
  42.1 22.2 %collective-permute-start.13 = (bf16[4,8,24,768]{3,2,1,0:T(8,128)(2,1)S(1)}, bf16[4,8,24,768]{3,2,1,0:T(8,128)(2,1)S(1)}, u32[]{:S(2)}, u32[]{:S(2)}) collective-permute-start(bf16[4,8,24,768]{3,2,1,0:T(8,128)(2,1)S(1)} %pad_maximum_fusion.p0), channel_id=1, source_target_pairs={{0,1},{1,0},{2,3},{3,2},{4,5},{5,4},{6,7},{7,6},{8,9},{9,8},{10,11... | collective-permute-start | bytes 3538952 | tf_op jit(solution)/shard_map/ppermute | solution.py:747
  62.1 10.1 %copy-start.8 = (bf16[4,8,24,768]{3,2,1,0:T(8,128)(2,1)}, bf16[4,8,24,768]{3,2,1,0:T(8,128)(2,1)S(1)}, u32[]{:S(2)}) copy-start(bf16[4,8,24,768]{3,2,1,0:T(8,128)(2,1)S(1)} %collective-permute-done.12.p3) | copy-start | bytes 3538948
  63.7 3.1 %collective-permute-start.14 = (bf16[4,8,24,768]{3,2,1,0:T(8,128)(2,1)}, bf16[4,8,24,768]{3,2,1,0:T(8,128)(2,1)S(1)}, u32[]{:S(2)}, u32[]{:S(2)}) collective-permute-start(bf16[4,8,24,768]{3,2,1,0:T(8,128)(2,1)} %collective-permute-done.10.p1), channel_id=1, source_target_pairs={{0,1},{1,0},{2,3},{3,2},{4,5},{5,4},{6,7},{7,6},{8,9},{9,8},{10,11... | collective-permute-start | bytes 3538952 | tf_op jit(solution)/shard_map/ppermute | solution.py:747
  63.7 6.4 %collective-permute-start.15 = (bf16[4,8,24,768]{3,2,1,0:T(8,128)(2,1)}, bf16[4,8,24,768]{3,2,1,0:T(8,128)(2,1)S(1)}, u32[]{:S(2)}, u32[]{:S(2)}) collective-permute-start(bf16[4,8,24,768]{3,2,1,0:T(8,128)(2,1)} %collective-permute-done.11.p2), channel_id=1, source_target_pairs={{0,1},{1,0},{2,3},{3,2},{4,5},{5,4},{6,7},{7,6},{8,9},{9,8},{10,11... | collective-permute-start | bytes 3538952 | tf_op jit(solution)/shard_map/ppermute | solution.py:747
  64.3 5.9 %collective-permute-start.16 = (bf16[4,8,24,768]{3,2,1,0:T(8,128)(2,1)S(1)}, bf16[4,8,24,768]{3,2,1,0:T(8,128)(2,1)S(1)}, u32[]{:S(2)}, u32[]{:S(2)}) collective-permute-start(bf16[4,8,24,768]{3,2,1,0:T(8,128)(2,1)S(1)} %collective-permute-done.12.p3), channel_id=1, source_target_pairs={{0,1},{1,0},{2,3},{3,2},{4,5},{5,4},{6,7},{7,6},{8,9},{9,8},{10,11... | collective-permute-start | bytes 3538952 | tf_op jit(solution)/shard_map/ppermute | solution.py:747
  64.3 8.0 %copy-start.9 = (bf16[4,8,24,768]{3,2,1,0:T(8,128)(2,1)}, bf16[4,8,24,768]{3,2,1,0:T(8,128)(2,1)S(1)}, u32[]{:S(2)}) copy-start(bf16[4,8,24,768]{3,2,1,0:T(8,128)(2,1)S(1)} %collective-permute-done.13.p4) | copy-start | bytes 3538948
  66.8 5.4 %copy-start.10 = (bf16[4,8,24,768]{3,2,1,0:T(8,128)(2,1)}, bf16[4,8,24,768]{3,2,1,0:T(8,128)(2,1)S(1)}, u32[]{:S(2)}) copy-start(bf16[4,8,24,768]{3,2,1,0:T(8,128)(2,1)S(1)} %collective-permute-done.14.p5) | copy-start | bytes 3538948
  70.2 1.0 copy-start.11
  71.2 1.0 copy-start.12
  109.5 12.1 %collective-permute-start.17 = (bf16[16,8,24,768]{3,2,1,0:T(8,128)(2,1)}, bf16[16,8,24,768]{3,2,1,0:T(8,128)(2,1)}, u32[]{:S(2)}, u32[]{:S(2)}) collective-permute-start(bf16[16,8,24,768]{3,2,1,0:T(8,128)(2,1)} %get-tuple-element.112), channel_id=1, source_target_pairs={{0,1},{1,0},{2,3},{3,2},{4,5},{5,4},{6,7},{7,6},{8,9},{9,8},{10,11... | collective-permute-start | bytes 14155784 | tf_op jit(solution)/shard_map/ppermute | solution.py:747
  109.7 11.9 %slice-start.2 = ((s8[4718592]{0:T(1024)(128)(4,1)}), s8[4194304]{0:T(1024)(128)(4,1)S(1)}, s32[]{:S(2)}) async-start(s8[4718592]{0:T(1024)(128)(4,1)} %bitcast.65), calls=%async_computation.2 | async-start | bytes 8388608
  109.7 11.9 %slice-start.3 = ((s8[4718592]{0:T(1024)(128)(4,1)}), s8[524288]{0:T(1024)(128)(4,1)S(1)}, s32[]{:S(2)}) async-start(s8[4718592]{0:T(1024)(128)(4,1)} %bitcast.65), calls=%async_computation.3 | async-start | bytes 1048576
  125.5 17.6 %collective-permute-start.18 = (bf16[4,8,24,768]{3,2,1,0:T(8,128)(2,1)}, bf16[4,8,24,768]{3,2,1,0:T(8,128)(2,1)S(1)}, u32[]{:S(2)}, u32[]{:S(2)}) collective-permute-start(bf16[4,8,24,768]{3,2,1,0:T(8,128)(2,1)} %get-tuple-element.117), channel_id=1, source_target_pairs={{0,8},{1,3},{2,10},{3,5},{4,12},{5,7},{6,14},{7,1},{8,16},{9,11},{... | collective-permute-start | bytes 3538952 | tf_op jit(solution)/shard_map/ppermute | solution.py:751
  126.9 28.5 %collective-permute-start.19 = (bf16[4,8,24,768]{3,2,1,0:T(8,128)(2,1)}, bf16[4,8,24,768]{3,2,1,0:T(8,128)(2,1)S(1)}, u32[]{:S(2)}, u32[]{:S(2)}) collective-permute-start(bf16[4,8,24,768]{3,2,1,0:T(8,128)(2,1)} %get-tuple-element.118), channel_id=1, source_target_pairs={{0,24},{1,7},{2,26},{3,1},{4,28},{5,3},{6,30},{7,5},{8,0},{9,15},{... | collective-permute-start | bytes 3538952 | tf_op jit(solution)/shard_map/ppermute | solution.py:751
  128.7 27.9 %collective-permute-start.20 = (bf16[4,8,24,768]{3,2,1,0:T(8,128)(2,1)}, bf16[4,8,24,768]{3,2,1,0:T(8,128)(2,1)S(1)}, u32[]{:S(2)}, u32[]{:S(2)}) collective-permute-start(bf16[4,8,24,768]{3,2,1,0:T(8,128)(2,1)} %get-tuple-element.119), channel_id=1, source_target_pairs={{0,16},{1,5},{2,18},{3,7},{4,20},{5,1},{6,22},{7,3},{8,24},{9,13},... | collective-permute-start | bytes 3538952 | tf_op jit(solution)/shard_map/ppermute | solution.py:751
  141.6 18.0 %collective-permute-start.21 = (bf16[4,104,768]{2,1,0:T(8,128)(2,1)}, bf16[4,104,768]{2,1,0:T(8,128)(2,1)S(1)}, u32[]{:S(2)}, u32[]{:S(2)}) collective-permute-start(bf16[4,104,768]{2,1,0:T(8,128)(2,1)} %get-tuple-element.121), channel_id=1, source_target_pairs={{0,1},{1,0},{2,3},{3,2},{4,5},{5,4},{6,7},{7,6},{8,9},{9,8},{10,11... | collective-permute-start | bytes 1916936 | tf_op jit(solution)/shard_map/ppermute | solution.py:747
  141.7 17.9 %collective-permute-start.22 = (bf16[4,104,768]{2,1,0:T(8,128)(2,1)}, bf16[4,104,768]{2,1,0:T(8,128)(2,1)S(1)}, u32[]{:S(2)}, u32[]{:S(2)}) collective-permute-start(bf16[4,104,768]{2,1,0:T(8,128)(2,1)} %get-tuple-element.122), channel_id=1, source_target_pairs={{0,1},{1,0},{2,3},{3,2},{4,5},{5,4},{6,7},{7,6},{8,9},{9,8},{10,11... | collective-permute-start | bytes 1916936 | tf_op jit(solution)/shard_map/ppermute | solution.py:747
  143.1 16.5 %collective-permute-start.23 = (bf16[4,104,768]{2,1,0:T(8,128)(2,1)}, bf16[4,104,768]{2,1,0:T(8,128)(2,1)S(1)}, u32[]{:S(2)}, u32[]{:S(2)}) collective-permute-start(bf16[4,104,768]{2,1,0:T(8,128)(2,1)} %get-tuple-element.123), channel_id=1, source_target_pairs={{0,1},{1,0},{2,3},{3,2},{4,5},{5,4},{6,7},{7,6},{8,9},{9,8},{10,11... | collective-permute-start | bytes 1916936 | tf_op jit(solution)/shard_map/ppermute | solution.py:747
  155.4 4.2 %collective-permute-start.24 = (bf16[4,104,768]{2,1,0:T(8,128)(2,1)}, bf16[4,104,768]{2,1,0:T(8,128)(2,1)S(1)}, u32[]{:S(2)}, u32[]{:S(2)}) collective-permute-start(bf16[4,104,768]{2,1,0:T(8,128)(2,1)} %get-tuple-element.124), channel_id=1, source_target_pairs={{0,1},{1,0},{2,3},{3,2},{4,5},{5,4},{6,7},{7,6},{8,9},{9,8},{10,11... | collective-permute-start | bytes 1916936 | tf_op jit(solution)/shard_map/ppermute | solution.py:747
  156.6 11.4 %slice-start = ((s8[5111808]{0:T(1024)(128)(4,1)}), s8[4194304]{0:T(1024)(128)(4,1)S(1)}, s32[]{:S(2)}) async-start(s8[5111808]{0:T(1024)(128)(4,1)} %bitcast.63), calls=%async_computation | async-start | bytes 8388608
  157.0 11.0 %slice-start.1 = ((s8[5111808]{0:T(1024)(128)(4,1)}), s8[917504]{0:T(1024)(128)(4,1)S(1)}, s32[]{:S(2)}) async-start(s8[5111808]{0:T(1024)(128)(4,1)} %bitcast.63), calls=%async_computation.1 | async-start | bytes 1835008
  157.0 11.0 %copy-start.1 = (bf16[640,768]{1,0:T(8,128)(2,1)S(1)}, bf16[640,768]{1,0:T(8,128)(2,1)}, u32[]{:S(2)}) copy-start(bf16[640,768]{1,0:T(8,128)(2,1)} %get-tuple-element.108.dq) | copy-start | bytes 2949124
  157.1 11.0 %copy-start.2 = (bf16[640,768]{1,0:T(8,128)(2,1)S(1)}, bf16[640,768]{1,0:T(8,128)(2,1)}, u32[]{:S(2)}) copy-start(bf16[640,768]{1,0:T(8,128)(2,1)} %get-tuple-element.109.dk) | copy-start | bytes 2949124
  157.1 11.0 %copy-start.3 = (bf16[640,768]{1,0:T(8,128)(2,1)S(1)}, bf16[640,768]{1,0:T(8,128)(2,1)}, u32[]{:S(2)}) copy-start(bf16[640,768]{1,0:T(8,128)(2,1)} %get-tuple-element.113.dv) | copy-start | bytes 2949124
  157.1 10.8 %collective-permute-start.28 = (bf16[8,24,768]{2,1,0:T(8,128)(2,1)S(1)}, bf16[8,24,768]{2,1,0:T(8,128)(2,1)S(1)}, u32[]{:S(2)}, u32[]{:S(2)}) collective-permute-start(bf16[8,24,768]{2,1,0:T(8,128)(2,1)S(1)} %get-tuple-element.161), channel_id=1, source_target_pairs={{0,4},{1,17},{2,6},{3,19},{4,0},{5,21},{6,2},{7,23},{8,12},{9,25},... | collective-permute-start | bytes 884744 | tf_op jit(solution)/shard_map/ppermute | solution.py:751
  159.6 8.4 %copy-start = (f32[640,768]{1,0:T(8,128)S(1)}, f32[640,768]{1,0:T(8,128)}, u32[]{:S(2)}) copy-start(f32[640,768]{1,0:T(8,128)} %get-tuple-element.125.gfs) | copy-start | bytes 5898244
  162.1 20.9 %collective-permute-start.25 = (bf16[4,104,768]{2,1,0:T(8,128)(2,1)S(1)}, bf16[4,104,768]{2,1,0:T(8,128)(2,1)S(1)}, u32[]{:S(2)}, u32[]{:S(2)}) collective-permute-start(bf16[4,104,768]{2,1,0:T(8,128)(2,1)S(1)} %get-tuple-element.127), channel_id=1, source_target_pairs={{0,8},{1,3},{2,10},{3,5},{4,12},{5,7},{6,14},{7,1},{8,16},{9,11},{... | collective-permute-start | bytes 1916936 | tf_op jit(solution)/shard_map/ppermute | solution.py:751
  163.5 19.8 %collective-permute-start.26 = (bf16[4,104,768]{2,1,0:T(8,128)(2,1)S(1)}, bf16[4,104,768]{2,1,0:T(8,128)(2,1)S(1)}, u32[]{:S(2)}, u32[]{:S(2)}) collective-permute-start(bf16[4,104,768]{2,1,0:T(8,128)(2,1)S(1)} %get-tuple-element.128), channel_id=1, source_target_pairs={{0,24},{1,7},{2,26},{3,1},{4,28},{5,3},{6,30},{7,5},{8,0},{9,15},{... | collective-permute-start | bytes 1916936 | tf_op jit(solution)/shard_map/ppermute | solution.py:751
  165.4 19.0 %collective-permute-start.27 = (bf16[4,104,768]{2,1,0:T(8,128)(2,1)S(1)}, bf16[4,104,768]{2,1,0:T(8,128)(2,1)S(1)}, u32[]{:S(2)}, u32[]{:S(2)}) collective-permute-start(bf16[4,104,768]{2,1,0:T(8,128)(2,1)S(1)} %get-tuple-element.129), channel_id=1, source_target_pairs={{0,16},{1,5},{2,18},{3,7},{4,20},{5,1},{6,22},{7,3},{8,24},{9,13},... | collective-permute-start | bytes 1916936 | tf_op jit(solution)/shard_map/ppermute | solution.py:751
  166.0 15.5 %collective-permute-start.30 = (bf16[8,24,768]{2,1,0:T(8,128)(2,1)S(1)}, bf16[8,24,768]{2,1,0:T(8,128)(2,1)S(1)}, u32[]{:S(2)}, u32[]{:S(2)}) collective-permute-start(bf16[8,24,768]{2,1,0:T(8,128)(2,1)S(1)} %get-tuple-element.162), channel_id=1, source_target_pairs={{0,6},{1,25},{2,0},{3,27},{4,2},{5,29},{6,4},{7,31},{8,14},{9,1},{... | collective-permute-start | bytes 884744 | tf_op jit(solution)/shard_map/ppermute | solution.py:751
  167.9 14.8 %collective-permute-start.29 = (bf16[8,24,768]{2,1,0:T(8,128)(2,1)S(1)}, bf16[8,24,768]{2,1,0:T(8,128)(2,1)S(1)}, u32[]{:S(2)}, u32[]{:S(2)}) collective-permute-start(bf16[8,24,768]{2,1,0:T(8,128)(2,1)S(1)} %get-tuple-element.163), channel_id=1, source_target_pairs={{0,2},{1,9},{2,4},{3,11},{4,6},{5,13},{6,0},{7,15},{8,10},{9,17},{... | collective-permute-start | bytes 884744 | tf_op jit(solution)/shard_map/ppermute | solution.py:751
  184.6 8.0 %collective-permute-start.31 = (bf16[104,768]{1,0:T(8,128)(2,1)S(1)}, bf16[104,768]{1,0:T(8,128)(2,1)S(1)}, u32[]{:S(2)}, u32[]{:S(2)}) collective-permute-start(bf16[104,768]{1,0:T(8,128)(2,1)S(1)} %get-tuple-element.164), channel_id=1, source_target_pairs={{0,4},{1,17},{2,6},{3,19},{4,0},{5,21},{6,2},{7,23},{8,12},{9,25},... | collective-permute-start | bytes 479240 | tf_op jit(solution)/shard_map/ppermute | solution.py:751
  186.4 7.3 %collective-permute-start.33 = (bf16[104,768]{1,0:T(8,128)(2,1)S(1)}, bf16[104,768]{1,0:T(8,128)(2,1)S(1)}, u32[]{:S(2)}, u32[]{:S(2)}) collective-permute-start(bf16[104,768]{1,0:T(8,128)(2,1)S(1)} %get-tuple-element.165), channel_id=1, source_target_pairs={{0,6},{1,25},{2,0},{3,27},{4,2},{5,29},{6,4},{7,31},{8,14},{9,1},{... | collective-permute-start | bytes 479240 | tf_op jit(solution)/shard_map/ppermute | solution.py:751
  188.4 6.5 %collective-permute-start.32 = (bf16[104,768]{1,0:T(8,128)(2,1)S(1)}, bf16[104,768]{1,0:T(8,128)(2,1)S(1)}, u32[]{:S(2)}, u32[]{:S(2)}) collective-permute-start(bf16[104,768]{1,0:T(8,128)(2,1)S(1)} %get-tuple-element.166), channel_id=1, source_target_pairs={{0,2},{1,9},{2,4},{3,11},{4,6},{5,13},{6,0},{7,15},{8,10},{9,17},{... | collective-permute-start | bytes 479240 | tf_op jit(solution)/shard_map/ppermute | solution.py:751
  188.4 11.5 %collective-permute-start.39 = (bf16[8,24,768]{2,1,0:T(8,128)(2,1)S(1)}, bf16[8,24,768]{2,1,0:T(8,128)(2,1)S(1)}, u32[]{:S(2)}, u32[]{:S(2)}) collective-permute-start(bf16[8,24,768]{2,1,0:T(8,128)(2,1)S(1)} %fusion.1.own), channel_id=1, source_target_pairs={{0,64},{32,96},{64,0},{96,32},{1,65},{33,97},{65,1},{97,33},{2,66}... | collective-permute-start | bytes 884744 | tf_op jit(solution)/shard_map/ppermute | solution.py:764
  191.6 14.9 %collective-permute-start.38 = (bf16[8,24,768]{2,1,0:T(8,128)(2,1)S(1)}, bf16[8,24,768]{2,1,0:T(8,128)(2,1)S(1)}, u32[]{:S(2)}, u32[]{:S(2)}) collective-permute-start(bf16[8,24,768]{2,1,0:T(8,128)(2,1)S(1)} %fusion.1.own), channel_id=1, source_target_pairs={{0,96},{32,0},{64,32},{96,64},{1,97},{33,1},{65,33},{97,65},{2,98}... | collective-permute-start | bytes 884744 | tf_op jit(solution)/shard_map/ppermute | solution.py:764
  192.7 14.6 %collective-permute-start.37 = (bf16[8,24,768]{2,1,0:T(8,128)(2,1)S(1)}, bf16[8,24,768]{2,1,0:T(8,128)(2,1)S(1)}, u32[]{:S(2)}, u32[]{:S(2)}) collective-permute-start(bf16[8,24,768]{2,1,0:T(8,128)(2,1)S(1)} %fusion.1.own), channel_id=1, source_target_pairs={{0,32},{32,64},{64,96},{96,0},{1,33},{33,65},{65,97},{97,1},{2,34}... | collective-permute-start | bytes 884744 | tf_op jit(solution)/shard_map/ppermute | solution.py:764
  195.0 13.8 %collective-permute-start.36 = (bf16[104,768]{1,0:T(8,128)(2,1)S(1)}, bf16[104,768]{1,0:T(8,128)(2,1)S(1)}, u32[]{:S(2)}, u32[]{:S(2)}) collective-permute-start(bf16[104,768]{1,0:T(8,128)(2,1)S(1)} %fusion.3.own), channel_id=1, source_target_pairs={{0,64},{32,96},{64,0},{96,32},{1,65},{33,97},{65,1},{97,33},{2,66}... | collective-permute-start | bytes 479240 | tf_op jit(solution)/shard_map/ppermute | solution.py:764
  198.3 12.6 %collective-permute-start.35 = (bf16[104,768]{1,0:T(8,128)(2,1)S(1)}, bf16[104,768]{1,0:T(8,128)(2,1)S(1)}, u32[]{:S(2)}, u32[]{:S(2)}) collective-permute-start(bf16[104,768]{1,0:T(8,128)(2,1)S(1)} %fusion.3.own), channel_id=1, source_target_pairs={{0,96},{32,0},{64,32},{96,64},{1,97},{33,1},{65,33},{97,65},{2,98}... | collective-permute-start | bytes 479240 | tf_op jit(solution)/shard_map/ppermute | solution.py:764
  199.9 11.0 %collective-permute-start.34 = (bf16[104,768]{1,0:T(8,128)(2,1)S(1)}, bf16[104,768]{1,0:T(8,128)(2,1)S(1)}, u32[]{:S(2)}, u32[]{:S(2)}) collective-permute-start(bf16[104,768]{1,0:T(8,128)(2,1)S(1)} %fusion.3.own), channel_id=1, source_target_pairs={{0,32},{32,64},{64,96},{96,0},{1,33},{33,65},{65,97},{97,1},{2,34}... | collective-permute-start | bytes 479240 | tf_op jit(solution)/shard_map/ppermute | solution.py:764

commit v4 on v3

--- a/solution.py
+++ b/solution.py
@@ -757,7 +757,7 @@
 
 def second_turn(own, left, right, far):
     parts = [four_sum(own[d], left[d], right[d], far[d]).astype(BF16) for d in range(RING)]
-    return four_sum(parts[0], *around(parts, 1)).astype(BF16)
+    return parts[0], *around(parts, 1)
 
 
 def across_replicas(own):
@@ -860,10 +860,13 @@
     around_a = around(parts_a, 0)
     grad_s, grad_l = input_back(gfs, dq, dk, dv, gathered_a, dims)
     grad_s, *around_a = lax.optimization_barrier((grad_s, *around_a))
-    own_f = second_turn(parts_f[0], *around_f)
+    own_f = four_sum(*second_turn(parts_f[0], *around_f)).astype(BF16)
     own_f, *around_a = lax.optimization_barrier((own_f, *around_a))
-    up, down = finish_feed(across_replicas(own_f), each, inner, tall)
-    own_a = second_turn(parts_a[0], *around_a)
+    own_f, *others_f = across_replicas(own_f)
+    last_a = second_turn(parts_a[0], *around_a)
+    *last_a, left_f, right_f = lax.optimization_barrier((*last_a, *others_f[:2]))
+    up, down = finish_feed((own_f, left_f, right_f, others_f[2]), each, inner, tall)
+    own_a = four_sum(*last_a).astype(BF16)
     w_in, w_out, *vectors = finish_attention(across_replicas(own_a), tall)
     vectors = [x.reshape(-1) for x in vectors]
     return (

time: 212 us -> 211 us (level)
    ppermute x21, waiting for transfers between devices: 45.8 us -> 48.8 us  [around(): lax.ppermute(v[d] if isinstance(v, (list, tuple)) else v, 'shard', turn(d...]
    ppermute x6, waiting for transfers between devices: 9 us -> 6.39 us  [across_replicas(): lax.ppermute(own, 'rep', [(i, (i + d) % RING) for i in range(RING)])]
  transfers between devices with their start and end apart: 40 -> 40, of which waited for: 22 -> 21; matrix products, arithmetic and copies ran while one was open for 2% -> 3% of each run, Pallas kernels for 23% -> 23%
where the time goes in v4:
time: 211 us
  Pallas kernels  88.4 us (42%)
  waiting for transfers between devices  62.9 us (30%)
  starting transfers between devices  45.4 us (22%)
  other arithmetic  8.25 us (4%)
  local copies, waits for them, and re-layouts  4.52 us (2%)
    ppermute x21, waiting for transfers between devices, around(): lax.ppermute(v[d] if isinstance(v, (list, tuple)) else v, 'shard', turn(d...  48.8 us
    pallas_call x1, Pallas kernels, feed(): pl.pallas_call(functools.partial(feed_body, dims), in_specs=[SCALARS] * 3...  37.3 us
    ppermute x21, starting transfers between devices, around(): lax.ppermute(v[d] if isinstance(v, (list, tuple)) else v, 'shard', turn(d...  33.9 us
    pallas_call x1, Pallas kernels, attention_forward(): pl.pallas_call(functools.partial(attention_forward_body, dims), grid_spec...  19 us
    pallas_call x1, Pallas kernels, attention_back(): pl.pallas_call(functools.partial(attention_back_body, dims), grid=(width...  11.8 us
    pallas_call x1, Pallas kernels, weight_back(): pl.pallas_call(functools.partial(weight_back_body, dims), grid_spec=pltpu...  11.2 us
    ppermute x6, starting transfers between devices, across_replicas(): lax.ppermute(own, 'rep', [(i, (i + d) % RING) for i in range(RING)])  9.53 us
    ppermute x13, waiting for transfers between devices, swap_cores(): return lax.ppermute(v, 'shard', [(i, i ^ 1) for i in range(SHARDS)])  7.67 us
  transfers between devices with their start and end apart: 40, of which 21 were waited for; matrix products, arithmetic and copies ran while one was open for 3% of the time, Pallas kernels for 23%

profile of v4, /device:TPU:0, one launch (start us, length us, event | category | flops | bytes accessed | tf_op | source)
XLA Modules:
  0.0 210.5 jit_solution(17168420603161763219)
XLA Ops:
  0.7 2.0 pack.1
  2.7 4.0 %collective-permute-start.2 = (bf16[296,768]{1,0:T(8,128)(2,1)}, bf16[296,768]{1,0:T(8,128)(2,1)S(1)}, u32[]{:S(2)}, u32[]{:S(2)}) collective-permute-start(bf16[296,768]{1,0:T(8,128)(2,1)} %pack.1), channel_id=1, source_target_pairs={{0,4},{1,17},{2,6},{3,19},{4,0},{5,21},{6,2},{7,23},{8,12},{9,25},... | collective-permute-start | bytes 1363976 | tf_op jit(solution)/shard_map/ppermute | solution.py:751
  6.6 0.7 collective-permute-start.1
  7.3 1.3 collective-permute-start
  8.7 1.0 slice_bitcast_fusion.3
  9.6 3.7 %collective-permute-done.2 = bf16[296,768]{1,0:T(8,128)(2,1)S(1)} collective-permute-done((bf16[296,768]{1,0:T(8,128)(2,1)}, bf16[296,768]{1,0:T(8,128)(2,1)S(1)}, u32[]{:S(2)}, u32[]{:S(2)}) %collective-permute-start.2) | collective-permute-done | bytes 454688 | tf_op jit(solution)/shard_map/ppermute | solution.py:751
  13.4 5.8 %collective-permute-done.1 = bf16[296,768]{1,0:T(8,128)(2,1)S(1)} collective-permute-done((bf16[296,768]{1,0:T(8,128)(2,1)}, bf16[296,768]{1,0:T(8,128)(2,1)S(1)}, u32[]{:S(2)}, u32[]{:S(2)}) %collective-permute-start.1) | collective-permute-done | bytes 454688 | tf_op jit(solution)/shard_map/ppermute | solution.py:751
  19.3 3.1 %collective-permute-start.5 = (bf16[4,104,768]{2,1,0:T(8,128)(2,1)S(1)}, bf16[4,104,768]{2,1,0:T(8,128)(2,1)S(1)}, u32[]{:S(2)}, u32[]{:S(2)}) collective-permute-start(bf16[4,104,768]{2,1,0:T(8,128)(2,1)S(1)} %pad_maximum_fusion.1.p0), channel_id=1, source_target_pairs={{0,16},{1,5},{2,18},{3,7},{4,20},{5,1},{6,22},{7,3},{8,24},{9,13},... | collective-permute-start | bytes 1916936 | tf_op jit(solution)/shard_map/ppermute | solution.py:751
  22.4 1.1 collective-permute-start.4
  23.6 0.9 collective-permute-start.3
  24.5 7.0 %collective-permute-done.5.p3 = bf16[4,104,768]{2,1,0:T(8,128)(2,1)S(1)} collective-permute-done((bf16[4,104,768]{2,1,0:T(8,128)(2,1)S(1)}, bf16[4,104,768]{2,1,0:T(8,128)(2,1)S(1)}, u32[]{:S(2)}, u32[]{:S(2)}) %collective-permute-start.5) | collective-permute-done | bytes 639008 | tf_op jit(solution)/shard_map/ppermute | solution.py:751
  31.6 0.8 copy-done.13
  32.8 3.1 %collective-permute-start.12 = (bf16[4,8,24,768]{3,2,1,0:T(8,128)(2,1)S(1)}, bf16[4,8,24,768]{3,2,1,0:T(8,128)(2,1)S(1)}, u32[]{:S(2)}, u32[]{:S(2)}) collective-permute-start(bf16[4,8,24,768]{3,2,1,0:T(8,128)(2,1)S(1)} %pad_maximum_fusion.p0), channel_id=1, source_target_pairs={{0,16},{1,5},{2,18},{3,7},{4,20},{5,1},{6,22},{7,3},{8,24},{9,13},... | collective-permute-start | bytes 3538952 | tf_op jit(solution)/shard_map/ppermute | solution.py:751
  35.9 1.1 collective-permute-start.11
  37.1 1.4 collective-permute-done.4.p2
  38.4 1.4 collective-permute-start.10
  39.8 0.6 collective-permute-start.7
  40.6 0.6 pad_add_fusion.pos
  41.2 0.8 collective-permute-done.8.p6
  42.2 0.9 collective-permute-done.7.p5
  43.1 19.0 %attention_forward.1 = (bf16[640,768]{1,0:T(8,128)(2,1)}, bf16[640,768]{1,0:T(8,128)(2,1)}, bf16[640,768]{1,0:T(8,128)(2,1)}, bf16[640,768]{1,0:T(8,128)(2,1)}, ...) custom-call(s32[2]{0:T(128)} %slen.3, s32[2]{0:T(128)} %llen.3, ...), custom_call_target="tpu_custom_call" | custom-call | flops 3019898880 | bytes 20000000 | tf_op jit(solution)/shard_map/attention_forward/pallas_call | solution.py:289
  62.1 1.6 collective-permute-done.11.p2
  63.7 0.5 collective-permute-start.15
  64.3 2.5 %collective-permute-done.14.p5 = bf16[4,8,24,768]{3,2,1,0:T(8,128)(2,1)S(1)} collective-permute-done((bf16[4,8,24,768]{3,2,1,0:T(8,128)(2,1)}, bf16[4,8,24,768]{3,2,1,0:T(8,128)(2,1)S(1)}, u32[]{:S(2)}, u32[]{:S(2)}) %collective-permute-start.14) | collective-permute-done | bytes 1179680 | tf_op jit(solution)/shard_map/ppermute | solution.py:747
  66.8 3.4 %collective-permute-done.15.p6 = bf16[4,8,24,768]{3,2,1,0:T(8,128)(2,1)S(1)} collective-permute-done((bf16[4,8,24,768]{3,2,1,0:T(8,128)(2,1)}, bf16[4,8,24,768]{3,2,1,0:T(8,128)(2,1)S(1)}, u32[]{:S(2)}, u32[]{:S(2)}) %collective-permute-start.15) | collective-permute-done | bytes 1179680 | tf_op jit(solution)/shard_map/ppermute | solution.py:747
  70.2 1.0 copy-done.11
  71.2 1.0 copy-done.12
  72.2 37.3 %feed.1 = (bf16[16,8,24,768]{3,2,1,0:T(8,128)(2,1)}, bf16[16,8,24,768]{3,2,1,0:T(8,128)(2,1)}, bf16[128,768]{1,0:T(8,128)(2,1)}, bf16[512,768]{1,0:T(8,128)(2,1)...) custom-call(s32[2]{0:T(128)} %slen.3, s32[2]{0:T(128)} %llen.3, ...), custom_call_target="tpu_custom_call" | custom-call | flops 18119393280 | bytes 30000000 | tf_op jit(solution)/shard_map/feed/pallas_call | solution.py:506
  109.7 11.8 %attention_back.1 = (bf16[640,768]{1,0:T(8,128)(2,1)}, bf16[640,768]{1,0:T(8,128)(2,1)}, bf16[640,768]{1,0:T(8,128)(2,1)}) custom-call(bf16[640,768]{1,0:T(8,128)(2,1)} %get-tuple-element.106.gatt.gatt_cols, bf16[32,104,768]{2,1,0:T(8,128)(2,1)} %get-tuple-element.108.wo_block.wq.wk.wv, bf16[640,768]{1,0:T(8,128)(2,1)} %get-tuple-element.109.q, ...), custom_call_target="tpu_custom_call" | custom-call | flops 3019898880 | bytes 15000000 | tf_op jit(solution)/shard_map/attention_back/pallas_call | solution.py:571
  121.6 3.9 %add_convert_fusion = (bf16[4,8,24,768]{3,2,1,0:T(8,128)(2,1)}, bf16[4,8,24,768]{3,2,1,0:T(8,128)(2,1)}, bf16[4,8,24,768]{3,2,1,0:T(8,128)(2,1)}, bf16[4,8,24,768]{3,2,1,0:T(8,128)(2,1)S(1)}) fusion(bf16[16,8,24,768]{3,2,1,0:T(8,128)(2,1)} %collective-permute-done.17, bf16[16,8,24,768]{3,2,1,0:T(8,128)(2,1)S(1)} %bitcast.63), kind=kLoop, calls=%fused_computation | loop fusion | flops 9437184 | bytes 14155776 | tf_op jit(solution)/shard_map/convert_element_type | solution.py:718
  125.5 1.4 collective-permute-start.18
  126.9 1.8 collective-permute-start.19
  128.7 1.7 collective-permute-start.20
  130.4 11.2 %weight_back.1 = (bf16[16,104,768]{2,1,0:T(8,128)(2,1)}, bf16[4,104,768]{2,1,0:T(8,128)(2,1)}, bf16[4,104,768]{2,1,0:T(8,128)(2,1)}, bf16[4,104,768]{2,1,0:T(8,128)(2,1)}, bf16[4,104,768]{2,1,0:T(8,128)(2,1)}) custom-call(s32[3]{0:T(128)} %pad_add_fusion.pos, bf16[640,768]{1,0:T(8,128)(2,1)} %get-tuple-element.106.gatt.gatt_cols, ...), custom_call_target="tpu_custom_call" | custom-call | flops 3019898880 | bytes 12000000 | tf_op jit(solution)/shard_map/weight_back/pallas_call | solution.py:643
  141.7 0.5 collective-permute-start.22
  142.2 0.9 collective-permute-done.18
  143.1 12.3 %collective-permute-done.19 = bf16[4,8,24,768]{3,2,1,0:T(8,128)(2,1)S(1)} collective-permute-done((bf16[4,8,24,768]{3,2,1,0:T(8,128)(2,1)}, bf16[4,8,24,768]{3,2,1,0:T(8,128)(2,1)S(1)}, u32[]{:S(2)}, u32[]{:S(2)}) %collective-permute-start.19) | collective-permute-done | bytes 1179680 | tf_op jit(solution)/shard_map/ppermute | solution.py:751
  155.4 1.2 collective-permute-done.20
  156.6 0.4 fusion.3
  157.1 2.5 %collective-permute-start.28 = (bf16[8,24,768]{2,1,0:T(8,128)(2,1)S(1)}, bf16[8,24,768]{2,1,0:T(8,128)(2,1)S(1)}, u32[]{:S(2)}, u32[]{:S(2)}) collective-permute-start(bf16[8,24,768]{2,1,0:T(8,128)(2,1)S(1)} %get-tuple-element.173), channel_id=1, source_target_pairs={{0,4},{1,17},{2,6},{3,19},{4,0},{5,21},{6,2},{7,23},{8,12},{9,25},... | collective-permute-start | bytes 884744 | tf_op jit(solution)/shard_map/ppermute | solution.py:751
  159.6 2.4 %add_convert_fusion.4 = (bf16[4,104,768]{2,1,0:T(8,128)(2,1)S(1)}, bf16[4,104,768]{2,1,0:T(8,128)(2,1)S(1)}, bf16[4,104,768]{2,1,0:T(8,128)(2,1)S(1)}, bf16[4,104,768]{2,1,0:T(8,128)(2,1)S(1)}) fusion(bf16[4,104,768]{2,1,0:T(8,128)(2,1)S(1)} %collective-permute-done.24, bf16[16,104,768]{2,1,0:T(8,128)(2,1)} %get-tuple-element.126, ...), kind=kLoop, calls=%fused_computation.4 | loop fusion | flops 5111808 | bytes 7667712 | tf_op jit(solution)/shard_map/convert_element_type | solution.py:724
  162.1 1.5 collective-permute-start.25
  163.5 1.8 collective-permute-start.26
  165.4 0.6 collective-permute-start.27
  166.0 1.9 collective-permute-start.30
  168.1 5.4 %input_back.1 = (f32[128,768]{1,0:T(8,128)}, f32[512,768]{1,0:T(8,128)}) custom-call(f32[640,768]{1,0:T(8,128)S(1)} %copy-done, bf16[640,768]{1,0:T(8,128)(2,1)S(1)} %copy-done.1, bf16[640,768]{1,0:T(8,128)(2,1)S(1)} %copy-done.2, bf16[640,768]{1,0:T(8,128)(2,1)S(1)} %copy-done.3, bf16[32,104,768]{2,1,0:T(8,128)(2,1)S(1)} %bitcast.61, ...), custom_call_target="tpu_custom_call" | custom-call | flops 2264924160 | bytes 12000000 | tf_op jit(solution)/shard_map/input_back/pallas_call | solution.py:698
  173.4 8.0 %collective-permute-done.30 = bf16[8,24,768]{2,1,0:T(8,128)(2,1)S(1)} collective-permute-done((bf16[8,24,768]{2,1,0:T(8,128)(2,1)S(1)}, bf16[8,24,768]{2,1,0:T(8,128)(2,1)S(1)}, u32[]{:S(2)}, u32[]{:S(2)}) %collective-permute-start.30) | collective-permute-done | bytes 294944 | tf_op jit(solution)/shard_map/ppermute | solution.py:751
  181.5 1.2 collective-permute-done.29
  182.9 0.4 collective-permute-done.26
  183.3 1.0 collective-permute-done.27
  184.4 3.0 %collective-permute-start.35 = (bf16[8,24,768]{2,1,0:T(8,128)(2,1)S(1)}, bf16[8,24,768]{2,1,0:T(8,128)(2,1)S(1)}, u32[]{:S(2)}, u32[]{:S(2)}) collective-permute-start(bf16[8,24,768]{2,1,0:T(8,128)(2,1)S(1)} %fusion.1.own), channel_id=1, source_target_pairs={{0,96},{32,0},{64,32},{96,64},{1,97},{33,1},{65,33},{97,65},{2,98}... | collective-permute-start | bytes 884744 | tf_op jit(solution)/shard_map/ppermute | solution.py:764
  187.7 1.8 collective-permute-start.33
  189.5 2.0 collective-permute-start.32
  191.5 3.1 %collective-permute-done.33 = bf16[104,768]{1,0:T(8,128)(2,1)S(1)} collective-permute-done((bf16[104,768]{1,0:T(8,128)(2,1)S(1)}, bf16[104,768]{1,0:T(8,128)(2,1)S(1)}, u32[]{:S(2)}, u32[]{:S(2)}) %collective-permute-start.33) | collective-permute-done | bytes 159776 | tf_op jit(solution)/shard_map/ppermute | solution.py:751
  194.6 2.2 %collective-permute-start.39 = (bf16[8,24,768]{2,1,0:T(8,128)(2,1)S(1)}, bf16[8,24,768]{2,1,0:T(8,128)(2,1)S(1)}, u32[]{:S(2)}, u32[]{:S(2)}) collective-permute-start(bf16[8,24,768]{2,1,0:T(8,128)(2,1)S(1)} %fusion.1.own), channel_id=1, source_target_pairs={{0,64},{32,96},{64,0},{96,32},{1,65},{33,97},{65,1},{97,33},{2,66}... | collective-permute-start | bytes 884744 | tf_op jit(solution)/shard_map/ppermute | solution.py:764
  196.8 1.2 collective-permute-done.31
  198.1 2.3 %collective-permute-start.38 = (bf16[104,768]{1,0:T(8,128)(2,1)S(1)}, bf16[104,768]{1,0:T(8,128)(2,1)S(1)}, u32[]{:S(2)}, u32[]{:S(2)}) collective-permute-start(bf16[104,768]{1,0:T(8,128)(2,1)S(1)} %add_convert_fusion.12.own), channel_id=1, source_target_pairs={{0,64},{32,96},{64,0},{96,32},{1,65},{33,97},{65,1},{97,33},{2,66}... | collective-permute-start | bytes 479240 | tf_op jit(solution)/shard_map/ppermute | solution.py:764
  200.4 1.2 collective-permute-start.37
  201.6 0.9 collective-permute-start.36
  202.4 3.6 %collective-permute-done.39.far = bf16[8,24,768]{2,1,0:T(8,128)(2,1)S(1)} collective-permute-done((bf16[8,24,768]{2,1,0:T(8,128)(2,1)S(1)}, bf16[8,24,768]{2,1,0:T(8,128)(2,1)S(1)}, u32[]{:S(2)}, u32[]{:S(2)}) %collective-permute-start.39) | collective-permute-done | bytes 294944 | tf_op jit(solution)/shard_map/ppermute | solution.py:764
  206.0 0.9 finish_feed.1
  206.9 1.1 collective-permute-done.38.far
  208.0 1.7 collective-permute-done.37.right
  209.7 0.8 finish_attention.1
  (86 shorter events, 2.3 us)
Async XLA Ops:
  2.7 10.7 %collective-permute-start.2 = (bf16[296,768]{1,0:T(8,128)(2,1)}, bf16[296,768]{1,0:T(8,128)(2,1)S(1)}, u32[]{:S(2)}, u32[]{:S(2)}) collective-permute-start(bf16[296,768]{1,0:T(8,128)(2,1)} %pack.1), channel_id=1, source_target_pairs={{0,4},{1,17},{2,6},{3,19},{4,0},{5,21},{6,2},{7,23},{8,12},{9,25},... | collective-permute-start | bytes 1363976 | tf_op jit(solution)/shard_map/ppermute | solution.py:751
  6.6 12.6 %collective-permute-start.1 = (bf16[296,768]{1,0:T(8,128)(2,1)}, bf16[296,768]{1,0:T(8,128)(2,1)S(1)}, u32[]{:S(2)}, u32[]{:S(2)}) collective-permute-start(bf16[296,768]{1,0:T(8,128)(2,1)} %pack.1), channel_id=1, source_target_pairs={{0,6},{1,25},{2,0},{3,27},{4,2},{5,29},{6,4},{7,31},{8,14},{9,1},{... | collective-permute-start | bytes 1363976 | tf_op jit(solution)/shard_map/ppermute | solution.py:751
  7.3 11.9 %collective-permute-start = (bf16[296,768]{1,0:T(8,128)(2,1)}, bf16[296,768]{1,0:T(8,128)(2,1)S(1)}, u32[]{:S(2)}, u32[]{:S(2)}) collective-permute-start(bf16[296,768]{1,0:T(8,128)(2,1)} %pack.1), channel_id=1, source_target_pairs={{0,2},{1,9},{2,4},{3,11},{4,6},{5,13},{6,0},{7,15},{8,10},{9,17},{... | collective-permute-start | bytes 1363976 | tf_op jit(solution)/shard_map/ppermute | solution.py:751
  9.6 21.8 %copy-start.4 = (bf16[296,768]{1,0:T(8,128)(2,1)S(1)}, bf16[296,768]{1,0:T(8,128)(2,1)}, u32[]{:S(2)}) copy-start(bf16[296,768]{1,0:T(8,128)(2,1)} %pack.1) | copy-start | bytes 1363972
  13.4 18.1 %copy-start.5 = (bf16[296,768]{1,0:T(8,128)(2,1)}, bf16[296,768]{1,0:T(8,128)(2,1)S(1)}, u32[]{:S(2)}) copy-start(bf16[296,768]{1,0:T(8,128)(2,1)S(1)} %collective-permute-done.2) | copy-start | bytes 1363972
  19.3 12.2 %copy-start.7 = (bf16[4,104,768]{2,1,0:T(8,128)(2,1)}, bf16[4,104,768]{2,1,0:T(8,128)(2,1)S(1)}, u32[]{:S(2)}) copy-start(bf16[4,104,768]{2,1,0:T(8,128)(2,1)S(1)} %pad_maximum_fusion.1.p0) | copy-start | bytes 1916932
  19.3 12.1 %collective-permute-start.5 = (bf16[4,104,768]{2,1,0:T(8,128)(2,1)S(1)}, bf16[4,104,768]{2,1,0:T(8,128)(2,1)S(1)}, u32[]{:S(2)}, u32[]{:S(2)}) collective-permute-start(bf16[4,104,768]{2,1,0:T(8,128)(2,1)S(1)} %pad_maximum_fusion.1.p0), channel_id=1, source_target_pairs={{0,16},{1,5},{2,18},{3,7},{4,20},{5,1},{6,22},{7,3},{8,24},{9,13},... | collective-permute-start | bytes 1916936 | tf_op jit(solution)/shard_map/ppermute | solution.py:751
  22.4 13.5 %collective-permute-start.6 = (bf16[4,104,768]{2,1,0:T(8,128)(2,1)S(1)}, bf16[4,104,768]{2,1,0:T(8,128)(2,1)S(1)}, u32[]{:S(2)}, u32[]{:S(2)}) collective-permute-start(bf16[4,104,768]{2,1,0:T(8,128)(2,1)S(1)} %pad_maximum_fusion.1.p0), channel_id=1, source_target_pairs={{0,1},{1,0},{2,3},{3,2},{4,5},{5,4},{6,7},{7,6},{8,9},{9,8},{10,11... | collective-permute-start | bytes 1916936 | tf_op jit(solution)/shard_map/ppermute | solution.py:747
  22.4 16.0 %collective-permute-start.4 = (bf16[4,104,768]{2,1,0:T(8,128)(2,1)S(1)}, bf16[4,104,768]{2,1,0:T(8,128)(2,1)}, u32[]{:S(2)}, u32[]{:S(2)}) collective-permute-start(bf16[4,104,768]{2,1,0:T(8,128)(2,1)S(1)} %pad_maximum_fusion.1.p0), channel_id=1, source_target_pairs={{0,24},{1,7},{2,26},{3,1},{4,28},{5,3},{6,30},{7,5},{8,0},{9,15},{... | collective-permute-start | bytes 1916936 | tf_op jit(solution)/shard_map/ppermute | solution.py:751
  23.6 16.2 %collective-permute-start.3 = (bf16[4,104,768]{2,1,0:T(8,128)(2,1)S(1)}, bf16[4,104,768]{2,1,0:T(8,128)(2,1)}, u32[]{:S(2)}, u32[]{:S(2)}) collective-permute-start(bf16[4,104,768]{2,1,0:T(8,128)(2,1)S(1)} %pad_maximum_fusion.1.p0), channel_id=1, source_target_pairs={{0,8},{1,3},{2,10},{3,5},{4,12},{5,7},{6,14},{7,1},{8,16},{9,11},{... | collective-permute-start | bytes 1916936 | tf_op jit(solution)/shard_map/ppermute | solution.py:751
  31.4 0.9 copy-start.13
  31.4 8.3 %collective-permute-start.9 = (bf16[4,104,768]{2,1,0:T(8,128)(2,1)S(1)}, bf16[4,104,768]{2,1,0:T(8,128)(2,1)S(1)}, u32[]{:S(2)}, u32[]{:S(2)}) collective-permute-start(bf16[4,104,768]{2,1,0:T(8,128)(2,1)S(1)} %collective-permute-done.5.p3), channel_id=1, source_target_pairs={{0,1},{1,0},{2,3},{3,2},{4,5},{5,4},{6,7},{7,6},{8,9},{9,8},{10,11... | collective-permute-start | bytes 1916936 | tf_op jit(solution)/shard_map/ppermute | solution.py:747
  31.5 1.2 slice-start.4
  32.8 29.3 %copy-start.6 = (bf16[4,8,24,768]{3,2,1,0:T(8,128)(2,1)}, bf16[4,8,24,768]{3,2,1,0:T(8,128)(2,1)S(1)}, u32[]{:S(2)}) copy-start(bf16[4,8,24,768]{3,2,1,0:T(8,128)(2,1)S(1)} %pad_maximum_fusion.p0) | copy-start | bytes 3538948
  32.8 29.3 %collective-permute-start.12 = (bf16[4,8,24,768]{3,2,1,0:T(8,128)(2,1)S(1)}, bf16[4,8,24,768]{3,2,1,0:T(8,128)(2,1)S(1)}, u32[]{:S(2)}, u32[]{:S(2)}) collective-permute-start(bf16[4,8,24,768]{3,2,1,0:T(8,128)(2,1)S(1)} %pad_maximum_fusion.p0), channel_id=1, source_target_pairs={{0,16},{1,5},{2,18},{3,7},{4,20},{5,1},{6,22},{7,3},{8,24},{9,13},... | collective-permute-start | bytes 3538952 | tf_op jit(solution)/shard_map/ppermute | solution.py:751
  35.9 3.9 %copy-start.14 = (bf16[4,104,768]{2,1,0:T(8,128)(2,1)}, bf16[4,104,768]{2,1,0:T(8,128)(2,1)S(1)}, u32[]{:S(2)}) copy-start(bf16[4,104,768]{2,1,0:T(8,128)(2,1)S(1)} %collective-permute-done.6.p4) | copy-start | bytes 1916932
  35.9 27.8 %collective-permute-start.11 = (bf16[4,8,24,768]{3,2,1,0:T(8,128)(2,1)S(1)}, bf16[4,8,24,768]{3,2,1,0:T(8,128)(2,1)}, u32[]{:S(2)}, u32[]{:S(2)}) collective-permute-start(bf16[4,8,24,768]{3,2,1,0:T(8,128)(2,1)S(1)} %pad_maximum_fusion.p0), channel_id=1, source_target_pairs={{0,24},{1,7},{2,26},{3,1},{4,28},{5,3},{6,30},{7,5},{8,0},{9,15},{... | collective-permute-start | bytes 3538952 | tf_op jit(solution)/shard_map/ppermute | solution.py:751
  38.4 25.3 %collective-permute-start.10 = (bf16[4,8,24,768]{3,2,1,0:T(8,128)(2,1)S(1)}, bf16[4,8,24,768]{3,2,1,0:T(8,128)(2,1)}, u32[]{:S(2)}, u32[]{:S(2)}) collective-permute-start(bf16[4,8,24,768]{3,2,1,0:T(8,128)(2,1)S(1)} %pad_maximum_fusion.p0), channel_id=1, source_target_pairs={{0,8},{1,3},{2,10},{3,5},{4,12},{5,7},{6,14},{7,1},{8,16},{9,11},{... | collective-permute-start | bytes 3538952 | tf_op jit(solution)/shard_map/ppermute | solution.py:751
  39.8 2.3 %collective-permute-start.8 = (bf16[4,104,768]{2,1,0:T(8,128)(2,1)}, bf16[4,104,768]{2,1,0:T(8,128)(2,1)S(1)}, u32[]{:S(2)}, u32[]{:S(2)}) collective-permute-start(bf16[4,104,768]{2,1,0:T(8,128)(2,1)} %collective-permute-done.4.p2), channel_id=1, source_target_pairs={{0,1},{1,0},{2,3},{3,2},{4,5},{5,4},{6,7},{7,6},{8,9},{9,8},{10,11... | collective-permute-start | bytes 1916936 | tf_op jit(solution)/shard_map/ppermute | solution.py:747
  39.8 0.8 copy-start.15
  39.8 3.3 %collective-permute-start.7 = (bf16[4,104,768]{2,1,0:T(8,128)(2,1)}, bf16[4,104,768]{2,1,0:T(8,128)(2,1)}, u32[]{:S(2)}, u32[]{:S(2)}) collective-permute-start(bf16[4,104,768]{2,1,0:T(8,128)(2,1)} %collective-permute-done.3.p1), channel_id=1, source_target_pairs={{0,1},{1,0},{2,3},{3,2},{4,5},{5,4},{6,7},{7,6},{8,9},{9,8},{10,11... | collective-permute-start | bytes 1916936 | tf_op jit(solution)/shard_map/ppermute | solution.py:747
  42.1 1.0 copy-start.16
  42.1 22.2 %collective-permute-start.13 = (bf16[4,8,24,768]{3,2,1,0:T(8,128)(2,1)S(1)}, bf16[4,8,24,768]{3,2,1,0:T(8,128)(2,1)S(1)}, u32[]{:S(2)}, u32[]{:S(2)}) collective-permute-start(bf16[4,8,24,768]{3,2,1,0:T(8,128)(2,1)S(1)} %pad_maximum_fusion.p0), channel_id=1, source_target_pairs={{0,1},{1,0},{2,3},{3,2},{4,5},{5,4},{6,7},{7,6},{8,9},{9,8},{10,11... | collective-permute-start | bytes 3538952 | tf_op jit(solution)/shard_map/ppermute | solution.py:747
  62.1 10.1 %copy-start.8 = (bf16[4,8,24,768]{3,2,1,0:T(8,128)(2,1)}, bf16[4,8,24,768]{3,2,1,0:T(8,128)(2,1)S(1)}, u32[]{:S(2)}) copy-start(bf16[4,8,24,768]{3,2,1,0:T(8,128)(2,1)S(1)} %collective-permute-done.12.p3) | copy-start | bytes 3538948
  63.7 3.1 %collective-permute-start.14 = (bf16[4,8,24,768]{3,2,1,0:T(8,128)(2,1)}, bf16[4,8,24,768]{3,2,1,0:T(8,128)(2,1)S(1)}, u32[]{:S(2)}, u32[]{:S(2)}) collective-permute-start(bf16[4,8,24,768]{3,2,1,0:T(8,128)(2,1)} %collective-permute-done.10.p1), channel_id=1, source_target_pairs={{0,1},{1,0},{2,3},{3,2},{4,5},{5,4},{6,7},{7,6},{8,9},{9,8},{10,11... | collective-permute-start | bytes 3538952 | tf_op jit(solution)/shard_map/ppermute | solution.py:747
  63.7 6.4 %collective-permute-start.15 = (bf16[4,8,24,768]{3,2,1,0:T(8,128)(2,1)}, bf16[4,8,24,768]{3,2,1,0:T(8,128)(2,1)S(1)}, u32[]{:S(2)}, u32[]{:S(2)}) collective-permute-start(bf16[4,8,24,768]{3,2,1,0:T(8,128)(2,1)} %collective-permute-done.11.p2), channel_id=1, source_target_pairs={{0,1},{1,0},{2,3},{3,2},{4,5},{5,4},{6,7},{7,6},{8,9},{9,8},{10,11... | collective-permute-start | bytes 3538952 | tf_op jit(solution)/shard_map/ppermute | solution.py:747
  64.3 5.9 %collective-permute-start.16 = (bf16[4,8,24,768]{3,2,1,0:T(8,128)(2,1)S(1)}, bf16[4,8,24,768]{3,2,1,0:T(8,128)(2,1)S(1)}, u32[]{:S(2)}, u32[]{:S(2)}) collective-permute-start(bf16[4,8,24,768]{3,2,1,0:T(8,128)(2,1)S(1)} %collective-permute-done.12.p3), channel_id=1, source_target_pairs={{0,1},{1,0},{2,3},{3,2},{4,5},{5,4},{6,7},{7,6},{8,9},{9,8},{10,11... | collective-permute-start | bytes 3538952 | tf_op jit(solution)/shard_map/ppermute | solution.py:747
  64.3 8.0 %copy-start.9 = (bf16[4,8,24,768]{3,2,1,0:T(8,128)(2,1)}, bf16[4,8,24,768]{3,2,1,0:T(8,128)(2,1)S(1)}, u32[]{:S(2)}) copy-start(bf16[4,8,24,768]{3,2,1,0:T(8,128)(2,1)S(1)} %collective-permute-done.13.p4) | copy-start | bytes 3538948
  66.8 5.4 %copy-start.10 = (bf16[4,8,24,768]{3,2,1,0:T(8,128)(2,1)}, bf16[4,8,24,768]{3,2,1,0:T(8,128)(2,1)S(1)}, u32[]{:S(2)}) copy-start(bf16[4,8,24,768]{3,2,1,0:T(8,128)(2,1)S(1)} %collective-permute-done.14.p5) | copy-start | bytes 3538948
  70.2 1.0 copy-start.11
  71.2 1.0 copy-start.12
  109.5 12.1 %collective-permute-start.17 = (bf16[16,8,24,768]{3,2,1,0:T(8,128)(2,1)}, bf16[16,8,24,768]{3,2,1,0:T(8,128)(2,1)}, u32[]{:S(2)}, u32[]{:S(2)}) collective-permute-start(bf16[16,8,24,768]{3,2,1,0:T(8,128)(2,1)} %get-tuple-element.118), channel_id=1, source_target_pairs={{0,1},{1,0},{2,3},{3,2},{4,5},{5,4},{6,7},{7,6},{8,9},{9,8},{10,11... | collective-permute-start | bytes 14155784 | tf_op jit(solution)/shard_map/ppermute | solution.py:747
  109.7 11.9 %slice-start.2 = ((s8[4718592]{0:T(1024)(128)(4,1)}), s8[4194304]{0:T(1024)(128)(4,1)S(1)}, s32[]{:S(2)}) async-start(s8[4718592]{0:T(1024)(128)(4,1)} %bitcast.62), calls=%async_computation.2 | async-start | bytes 8388608
  109.7 11.9 %slice-start.3 = ((s8[4718592]{0:T(1024)(128)(4,1)}), s8[524288]{0:T(1024)(128)(4,1)S(1)}, s32[]{:S(2)}) async-start(s8[4718592]{0:T(1024)(128)(4,1)} %bitcast.62), calls=%async_computation.3 | async-start | bytes 1048576
  125.5 17.6 %collective-permute-start.18 = (bf16[4,8,24,768]{3,2,1,0:T(8,128)(2,1)}, bf16[4,8,24,768]{3,2,1,0:T(8,128)(2,1)S(1)}, u32[]{:S(2)}, u32[]{:S(2)}) collective-permute-start(bf16[4,8,24,768]{3,2,1,0:T(8,128)(2,1)} %get-tuple-element.123), channel_id=1, source_target_pairs={{0,8},{1,3},{2,10},{3,5},{4,12},{5,7},{6,14},{7,1},{8,16},{9,11},{... | collective-permute-start | bytes 3538952 | tf_op jit(solution)/shard_map/ppermute | solution.py:751
  126.9 28.5 %collective-permute-start.19 = (bf16[4,8,24,768]{3,2,1,0:T(8,128)(2,1)}, bf16[4,8,24,768]{3,2,1,0:T(8,128)(2,1)S(1)}, u32[]{:S(2)}, u32[]{:S(2)}) collective-permute-start(bf16[4,8,24,768]{3,2,1,0:T(8,128)(2,1)} %get-tuple-element.124), channel_id=1, source_target_pairs={{0,24},{1,7},{2,26},{3,1},{4,28},{5,3},{6,30},{7,5},{8,0},{9,15},{... | collective-permute-start | bytes 3538952 | tf_op jit(solution)/shard_map/ppermute | solution.py:751
  128.7 27.9 %collective-permute-start.20 = (bf16[4,8,24,768]{3,2,1,0:T(8,128)(2,1)}, bf16[4,8,24,768]{3,2,1,0:T(8,128)(2,1)S(1)}, u32[]{:S(2)}, u32[]{:S(2)}) collective-permute-start(bf16[4,8,24,768]{3,2,1,0:T(8,128)(2,1)} %get-tuple-element.125), channel_id=1, source_target_pairs={{0,16},{1,5},{2,18},{3,7},{4,20},{5,1},{6,22},{7,3},{8,24},{9,13},... | collective-permute-start | bytes 3538952 | tf_op jit(solution)/shard_map/ppermute | solution.py:751
  141.6 18.0 %collective-permute-start.21 = (bf16[4,104,768]{2,1,0:T(8,128)(2,1)}, bf16[4,104,768]{2,1,0:T(8,128)(2,1)S(1)}, u32[]{:S(2)}, u32[]{:S(2)}) collective-permute-start(bf16[4,104,768]{2,1,0:T(8,128)(2,1)} %get-tuple-element.127), channel_id=1, source_target_pairs={{0,1},{1,0},{2,3},{3,2},{4,5},{5,4},{6,7},{7,6},{8,9},{9,8},{10,11... | collective-permute-start | bytes 1916936 | tf_op jit(solution)/shard_map/ppermute | solution.py:747
  141.7 17.9 %collective-permute-start.22 = (bf16[4,104,768]{2,1,0:T(8,128)(2,1)}, bf16[4,104,768]{2,1,0:T(8,128)(2,1)S(1)}, u32[]{:S(2)}, u32[]{:S(2)}) collective-permute-start(bf16[4,104,768]{2,1,0:T(8,128)(2,1)} %get-tuple-element.128), channel_id=1, source_target_pairs={{0,1},{1,0},{2,3},{3,2},{4,5},{5,4},{6,7},{7,6},{8,9},{9,8},{10,11... | collective-permute-start | bytes 1916936 | tf_op jit(solution)/shard_map/ppermute | solution.py:747
  143.1 16.5 %collective-permute-start.23 = (bf16[4,104,768]{2,1,0:T(8,128)(2,1)}, bf16[4,104,768]{2,1,0:T(8,128)(2,1)S(1)}, u32[]{:S(2)}, u32[]{:S(2)}) collective-permute-start(bf16[4,104,768]{2,1,0:T(8,128)(2,1)} %get-tuple-element.129), channel_id=1, source_target_pairs={{0,1},{1,0},{2,3},{3,2},{4,5},{5,4},{6,7},{7,6},{8,9},{9,8},{10,11... | collective-permute-start | bytes 1916936 | tf_op jit(solution)/shard_map/ppermute | solution.py:747
  155.4 4.2 %collective-permute-start.24 = (bf16[4,104,768]{2,1,0:T(8,128)(2,1)}, bf16[4,104,768]{2,1,0:T(8,128)(2,1)S(1)}, u32[]{:S(2)}, u32[]{:S(2)}) collective-permute-start(bf16[4,104,768]{2,1,0:T(8,128)(2,1)} %get-tuple-element.130), channel_id=1, source_target_pairs={{0,1},{1,0},{2,3},{3,2},{4,5},{5,4},{6,7},{7,6},{8,9},{9,8},{10,11... | collective-permute-start | bytes 1916936 | tf_op jit(solution)/shard_map/ppermute | solution.py:747
  156.6 11.4 %slice-start = ((s8[5111808]{0:T(1024)(128)(4,1)}), s8[4194304]{0:T(1024)(128)(4,1)S(1)}, s32[]{:S(2)}) async-start(s8[5111808]{0:T(1024)(128)(4,1)} %bitcast.60), calls=%async_computation | async-start | bytes 8388608
  157.0 11.0 %slice-start.1 = ((s8[5111808]{0:T(1024)(128)(4,1)}), s8[917504]{0:T(1024)(128)(4,1)S(1)}, s32[]{:S(2)}) async-start(s8[5111808]{0:T(1024)(128)(4,1)} %bitcast.60), calls=%async_computation.1 | async-start | bytes 1835008
  157.0 11.0 %copy-start.1 = (bf16[640,768]{1,0:T(8,128)(2,1)S(1)}, bf16[640,768]{1,0:T(8,128)(2,1)}, u32[]{:S(2)}) copy-start(bf16[640,768]{1,0:T(8,128)(2,1)} %get-tuple-element.114.dq) | copy-start | bytes 2949124
  157.1 11.0 %copy-start.2 = (bf16[640,768]{1,0:T(8,128)(2,1)S(1)}, bf16[640,768]{1,0:T(8,128)(2,1)}, u32[]{:S(2)}) copy-start(bf16[640,768]{1,0:T(8,128)(2,1)} %get-tuple-element.115.dk) | copy-start | bytes 2949124
  157.1 11.0 %copy-start.3 = (bf16[640,768]{1,0:T(8,128)(2,1)S(1)}, bf16[640,768]{1,0:T(8,128)(2,1)}, u32[]{:S(2)}) copy-start(bf16[640,768]{1,0:T(8,128)(2,1)} %get-tuple-element.119.dv) | copy-start | bytes 2949124
  157.1 10.8 %collective-permute-start.28 = (bf16[8,24,768]{2,1,0:T(8,128)(2,1)S(1)}, bf16[8,24,768]{2,1,0:T(8,128)(2,1)S(1)}, u32[]{:S(2)}, u32[]{:S(2)}) collective-permute-start(bf16[8,24,768]{2,1,0:T(8,128)(2,1)S(1)} %get-tuple-element.173), channel_id=1, source_target_pairs={{0,4},{1,17},{2,6},{3,19},{4,0},{5,21},{6,2},{7,23},{8,12},{9,25},... | collective-permute-start | bytes 884744 | tf_op jit(solution)/shard_map/ppermute | solution.py:751
  159.6 8.4 %copy-start = (f32[640,768]{1,0:T(8,128)S(1)}, f32[640,768]{1,0:T(8,128)}, u32[]{:S(2)}) copy-start(f32[640,768]{1,0:T(8,128)} %get-tuple-element.131.gfs) | copy-start | bytes 5898244
  162.1 20.9 %collective-permute-start.25 = (bf16[4,104,768]{2,1,0:T(8,128)(2,1)S(1)}, bf16[4,104,768]{2,1,0:T(8,128)(2,1)S(1)}, u32[]{:S(2)}, u32[]{:S(2)}) collective-permute-start(bf16[4,104,768]{2,1,0:T(8,128)(2,1)S(1)} %get-tuple-element.133), channel_id=1, source_target_pairs={{0,8},{1,3},{2,10},{3,5},{4,12},{5,7},{6,14},{7,1},{8,16},{9,11},{... | collective-permute-start | bytes 1916936 | tf_op jit(solution)/shard_map/ppermute | solution.py:751
  163.5 19.8 %collective-permute-start.26 = (bf16[4,104,768]{2,1,0:T(8,128)(2,1)S(1)}, bf16[4,104,768]{2,1,0:T(8,128)(2,1)S(1)}, u32[]{:S(2)}, u32[]{:S(2)}) collective-permute-start(bf16[4,104,768]{2,1,0:T(8,128)(2,1)S(1)} %get-tuple-element.134), channel_id=1, source_target_pairs={{0,24},{1,7},{2,26},{3,1},{4,28},{5,3},{6,30},{7,5},{8,0},{9,15},{... | collective-permute-start | bytes 1916936 | tf_op jit(solution)/shard_map/ppermute | solution.py:751
  165.4 19.0 %collective-permute-start.27 = (bf16[4,104,768]{2,1,0:T(8,128)(2,1)S(1)}, bf16[4,104,768]{2,1,0:T(8,128)(2,1)S(1)}, u32[]{:S(2)}, u32[]{:S(2)}) collective-permute-start(bf16[4,104,768]{2,1,0:T(8,128)(2,1)S(1)} %get-tuple-element.135), channel_id=1, source_target_pairs={{0,16},{1,5},{2,18},{3,7},{4,20},{5,1},{6,22},{7,3},{8,24},{9,13},... | collective-permute-start | bytes 1916936 | tf_op jit(solution)/shard_map/ppermute | solution.py:751
  166.0 15.5 %collective-permute-start.30 = (bf16[8,24,768]{2,1,0:T(8,128)(2,1)S(1)}, bf16[8,24,768]{2,1,0:T(8,128)(2,1)S(1)}, u32[]{:S(2)}, u32[]{:S(2)}) collective-permute-start(bf16[8,24,768]{2,1,0:T(8,128)(2,1)S(1)} %get-tuple-element.174), channel_id=1, source_target_pairs={{0,6},{1,25},{2,0},{3,27},{4,2},{5,29},{6,4},{7,31},{8,14},{9,1},{... | collective-permute-start | bytes 884744 | tf_op jit(solution)/shard_map/ppermute | solution.py:751
  167.9 14.8 %collective-permute-start.29 = (bf16[8,24,768]{2,1,0:T(8,128)(2,1)S(1)}, bf16[8,24,768]{2,1,0:T(8,128)(2,1)S(1)}, u32[]{:S(2)}, u32[]{:S(2)}) collective-permute-start(bf16[8,24,768]{2,1,0:T(8,128)(2,1)S(1)} %get-tuple-element.175), channel_id=1, source_target_pairs={{0,2},{1,9},{2,4},{3,11},{4,6},{5,13},{6,0},{7,15},{8,10},{9,17},{... | collective-permute-start | bytes 884744 | tf_op jit(solution)/shard_map/ppermute | solution.py:751
  184.4 13.6 %collective-permute-start.35 = (bf16[8,24,768]{2,1,0:T(8,128)(2,1)S(1)}, bf16[8,24,768]{2,1,0:T(8,128)(2,1)S(1)}, u32[]{:S(2)}, u32[]{:S(2)}) collective-permute-start(bf16[8,24,768]{2,1,0:T(8,128)(2,1)S(1)} %fusion.1.own), channel_id=1, source_target_pairs={{0,96},{32,0},{64,32},{96,64},{1,97},{33,1},{65,33},{97,65},{2,98}... | collective-permute-start | bytes 884744 | tf_op jit(solution)/shard_map/ppermute | solution.py:764
  187.4 10.6 %collective-permute-start.34 = (bf16[8,24,768]{2,1,0:T(8,128)(2,1)S(1)}, bf16[8,24,768]{2,1,0:T(8,128)(2,1)S(1)}, u32[]{:S(2)}, u32[]{:S(2)}) collective-permute-start(bf16[8,24,768]{2,1,0:T(8,128)(2,1)S(1)} %fusion.1.own), channel_id=1, source_target_pairs={{0,32},{32,64},{64,96},{96,0},{1,33},{33,65},{65,97},{97,1},{2,34}... | collective-permute-start | bytes 884744 | tf_op jit(solution)/shard_map/ppermute | solution.py:764
  187.7 6.9 %collective-permute-start.33 = (bf16[104,768]{1,0:T(8,128)(2,1)S(1)}, bf16[104,768]{1,0:T(8,128)(2,1)S(1)}, u32[]{:S(2)}, u32[]{:S(2)}) collective-permute-start(bf16[104,768]{1,0:T(8,128)(2,1)S(1)} %get-tuple-element.176), channel_id=1, source_target_pairs={{0,4},{1,17},{2,6},{3,19},{4,0},{5,21},{6,2},{7,23},{8,12},{9,25},... | collective-permute-start | bytes 479240 | tf_op jit(solution)/shard_map/ppermute | solution.py:751
  189.5 7.3 %collective-permute-start.32 = (bf16[104,768]{1,0:T(8,128)(2,1)S(1)}, bf16[104,768]{1,0:T(8,128)(2,1)S(1)}, u32[]{:S(2)}, u32[]{:S(2)}) collective-permute-start(bf16[104,768]{1,0:T(8,128)(2,1)S(1)} %get-tuple-element.177), channel_id=1, source_target_pairs={{0,6},{1,25},{2,0},{3,27},{4,2},{5,29},{6,4},{7,31},{8,14},{9,1},{... | collective-permute-start | bytes 479240 | tf_op jit(solution)/shard_map/ppermute | solution.py:751
  191.5 6.5 %collective-permute-start.31 = (bf16[104,768]{1,0:T(8,128)(2,1)S(1)}, bf16[104,768]{1,0:T(8,128)(2,1)S(1)}, u32[]{:S(2)}, u32[]{:S(2)}) collective-permute-start(bf16[104,768]{1,0:T(8,128)(2,1)S(1)} %get-tuple-element.178), channel_id=1, source_target_pairs={{0,2},{1,9},{2,4},{3,11},{4,6},{5,13},{6,0},{7,15},{8,10},{9,17},{... | collective-permute-start | bytes 479240 | tf_op jit(solution)/shard_map/ppermute | solution.py:751
  194.6 11.4 %collective-permute-start.39 = (bf16[8,24,768]{2,1,0:T(8,128)(2,1)S(1)}, bf16[8,24,768]{2,1,0:T(8,128)(2,1)S(1)}, u32[]{:S(2)}, u32[]{:S(2)}) collective-permute-start(bf16[8,24,768]{2,1,0:T(8,128)(2,1)S(1)} %fusion.1.own), channel_id=1, source_target_pairs={{0,64},{32,96},{64,0},{96,32},{1,65},{33,97},{65,1},{97,33},{2,66}... | collective-permute-start | bytes 884744 | tf_op jit(solution)/shard_map/ppermute | solution.py:764
  198.1 9.9 %collective-permute-start.38 = (bf16[104,768]{1,0:T(8,128)(2,1)S(1)}, bf16[104,768]{1,0:T(8,128)(2,1)S(1)}, u32[]{:S(2)}, u32[]{:S(2)}) collective-permute-start(bf16[104,768]{1,0:T(8,128)(2,1)S(1)} %add_convert_fusion.12.own), channel_id=1, source_target_pairs={{0,64},{32,96},{64,0},{96,32},{1,65},{33,97},{65,1},{97,33},{2,66}... | collective-permute-start | bytes 479240 | tf_op jit(solution)/shard_map/ppermute | solution.py:764
  200.4 9.3 %collective-permute-start.37 = (bf16[104,768]{1,0:T(8,128)(2,1)S(1)}, bf16[104,768]{1,0:T(8,128)(2,1)S(1)}, u32[]{:S(2)}, u32[]{:S(2)}) collective-permute-start(bf16[104,768]{1,0:T(8,128)(2,1)S(1)} %add_convert_fusion.12.own), channel_id=1, source_target_pairs={{0,96},{32,0},{64,32},{96,64},{1,97},{33,1},{65,33},{97,65},{2,98}... | collective-permute-start | bytes 479240 | tf_op jit(solution)/shard_map/ppermute | solution.py:764
  201.6 8.2 %collective-permute-start.36 = (bf16[104,768]{1,0:T(8,128)(2,1)S(1)}, bf16[104,768]{1,0:T(8,128)(2,1)S(1)}, u32[]{:S(2)}, u32[]{:S(2)}) collective-permute-start(bf16[104,768]{1,0:T(8,128)(2,1)S(1)} %add_convert_fusion.12.own), channel_id=1, source_target_pairs={{0,32},{32,64},{64,96},{96,0},{1,33},{33,65},{65,97},{97,1},{2,34}... | collective-permute-start | bytes 479240 | tf_op jit(solution)/shard_map/ppermute | solution.py:764

commit v5 on v4

--- a/solution.py
+++ b/solution.py
@@ -861,11 +861,11 @@
     grad_s, grad_l = input_back(gfs, dq, dk, dv, gathered_a, dims)
     grad_s, *around_a = lax.optimization_barrier((grad_s, *around_a))
     own_f = four_sum(*second_turn(parts_f[0], *around_f)).astype(BF16)
-    own_f, *around_a = lax.optimization_barrier((own_f, *around_a))
+    _, *around_a = lax.optimization_barrier((own_f, *around_a))
     own_f, *others_f = across_replicas(own_f)
     last_a = second_turn(parts_a[0], *around_a)
-    *last_a, left_f, right_f = lax.optimization_barrier((*last_a, *others_f[:2]))
-    up, down = finish_feed((own_f, left_f, right_f, others_f[2]), each, inner, tall)
+    *last_a, far_f = lax.optimization_barrier((*last_a, others_f[2]))
+    up, down = finish_feed((own_f, *others_f[:2], far_f), each, inner, tall)
     own_a = four_sum(*last_a).astype(BF16)
     w_in, w_out, *vectors = finish_attention(across_replicas(own_a), tall)
     vectors = [x.reshape(-1) for x in vectors]

time: 211 us -> 208 us (0.986)
  waiting for transfers between devices: 62.9 us -> 59.2 us
    ppermute x21, waiting for transfers between devices: 48.8 us -> 45.5 us  [around(): lax.ppermute(v[d] if isinstance(v, (list, tuple)) else v, 'shard', turn(d...]
where the time goes in v5:
time: 208 us
  Pallas kernels  88.4 us (42%)
  waiting for transfers between devices  59.2 us (28%)
  starting transfers between devices  46.7 us (22%)
  other arithmetic  8.27 us (4%)
  local copies, waits for them, and re-layouts  4.52 us (2%)
    ppermute x21, waiting for transfers between devices, around(): lax.ppermute(v[d] if isinstance(v, (list, tuple)) else v, 'shard', turn(d...  45.5 us
    pallas_call x1, Pallas kernels, feed(): pl.pallas_call(functools.partial(feed_body, dims), in_specs=[SCALARS] * 3...  37.3 us
    ppermute x21, starting transfers between devices, around(): lax.ppermute(v[d] if isinstance(v, (list, tuple)) else v, 'shard', turn(d...  33.6 us
    pallas_call x1, Pallas kernels, attention_forward(): pl.pallas_call(functools.partial(attention_forward_body, dims), grid_spec...  19 us
    pallas_call x1, Pallas kernels, attention_back(): pl.pallas_call(functools.partial(attention_back_body, dims), grid=(width...  11.8 us
    pallas_call x1, Pallas kernels, weight_back(): pl.pallas_call(functools.partial(weight_back_body, dims), grid_spec=pltpu...  11.2 us
    ppermute x6, starting transfers between devices, across_replicas(): lax.ppermute(own, 'rep', [(i, (i + d) % RING) for i in range(RING)])  11.1 us
    ppermute x13, waiting for transfers between devices, swap_cores(): return lax.ppermute(v, 'shard', [(i, i ^ 1) for i in range(SHARDS)])  7.67 us
  transfers between devices with their start and end apart: 40, of which 21 were waited for; matrix products, arithmetic and copies ran while one was open for 3% of the time, Pallas kernels for 23%

profile of v5, /device:TPU:0, one launch (start us, length us, event | category | flops | bytes accessed | tf_op | source)
XLA Modules:
  0.0 208.1 jit_solution(4449202572136931978)
XLA Ops:
  0.7 2.0 pack.1
  2.7 4.0 %collective-permute-start.2 = (bf16[296,768]{1,0:T(8,128)(2,1)}, bf16[296,768]{1,0:T(8,128)(2,1)S(1)}, u32[]{:S(2)}, u32[]{:S(2)}) collective-permute-start(bf16[296,768]{1,0:T(8,128)(2,1)} %pack.1), channel_id=1, source_target_pairs={{0,4},{1,17},{2,6},{3,19},{4,0},{5,21},{6,2},{7,23},{8,12},{9,25},... | collective-permute-start | bytes 1363976 | tf_op jit(solution)/shard_map/ppermute | solution.py:751
  6.6 0.7 collective-permute-start.1
  7.3 1.3 collective-permute-start
  8.7 1.0 slice_bitcast_fusion.3
  9.6 3.7 %collective-permute-done.2 = bf16[296,768]{1,0:T(8,128)(2,1)S(1)} collective-permute-done((bf16[296,768]{1,0:T(8,128)(2,1)}, bf16[296,768]{1,0:T(8,128)(2,1)S(1)}, u32[]{:S(2)}, u32[]{:S(2)}) %collective-permute-start.2) | collective-permute-done | bytes 454688 | tf_op jit(solution)/shard_map/ppermute | solution.py:751
  13.4 5.8 %collective-permute-done.1 = bf16[296,768]{1,0:T(8,128)(2,1)S(1)} collective-permute-done((bf16[296,768]{1,0:T(8,128)(2,1)}, bf16[296,768]{1,0:T(8,128)(2,1)S(1)}, u32[]{:S(2)}, u32[]{:S(2)}) %collective-permute-start.1) | collective-permute-done | bytes 454688 | tf_op jit(solution)/shard_map/ppermute | solution.py:751
  19.3 3.1 %collective-permute-start.5 = (bf16[4,104,768]{2,1,0:T(8,128)(2,1)S(1)}, bf16[4,104,768]{2,1,0:T(8,128)(2,1)S(1)}, u32[]{:S(2)}, u32[]{:S(2)}) collective-permute-start(bf16[4,104,768]{2,1,0:T(8,128)(2,1)S(1)} %pad_maximum_fusion.1.p0), channel_id=1, source_target_pairs={{0,16},{1,5},{2,18},{3,7},{4,20},{5,1},{6,22},{7,3},{8,24},{9,13},... | collective-permute-start | bytes 1916936 | tf_op jit(solution)/shard_map/ppermute | solution.py:751
  22.4 1.1 collective-permute-start.4
  23.6 0.9 collective-permute-start.3
  24.5 7.0 %collective-permute-done.5.p3 = bf16[4,104,768]{2,1,0:T(8,128)(2,1)S(1)} collective-permute-done((bf16[4,104,768]{2,1,0:T(8,128)(2,1)S(1)}, bf16[4,104,768]{2,1,0:T(8,128)(2,1)S(1)}, u32[]{:S(2)}, u32[]{:S(2)}) %collective-permute-start.5) | collective-permute-done | bytes 639008 | tf_op jit(solution)/shard_map/ppermute | solution.py:751
  31.6 0.8 copy-done.13
  32.8 3.1 %collective-permute-start.12 = (bf16[4,8,24,768]{3,2,1,0:T(8,128)(2,1)S(1)}, bf16[4,8,24,768]{3,2,1,0:T(8,128)(2,1)S(1)}, u32[]{:S(2)}, u32[]{:S(2)}) collective-permute-start(bf16[4,8,24,768]{3,2,1,0:T(8,128)(2,1)S(1)} %pad_maximum_fusion.p0), channel_id=1, source_target_pairs={{0,16},{1,5},{2,18},{3,7},{4,20},{5,1},{6,22},{7,3},{8,24},{9,13},... | collective-permute-start | bytes 3538952 | tf_op jit(solution)/shard_map/ppermute | solution.py:751
  35.9 1.1 collective-permute-start.11
  37.1 1.4 collective-permute-done.4.p2
  38.4 1.4 collective-permute-start.10
  39.8 0.6 collective-permute-start.7
  40.6 0.6 pad_add_fusion.pos
  41.2 0.8 collective-permute-done.8.p6
  42.2 0.9 collective-permute-done.7.p5
  43.1 19.0 %attention_forward.1 = (bf16[640,768]{1,0:T(8,128)(2,1)}, bf16[640,768]{1,0:T(8,128)(2,1)}, bf16[640,768]{1,0:T(8,128)(2,1)}, bf16[640,768]{1,0:T(8,128)(2,1)}, ...) custom-call(s32[2]{0:T(128)} %slen.3, s32[2]{0:T(128)} %llen.3, ...), custom_call_target="tpu_custom_call" | custom-call | flops 3019898880 | bytes 20000000 | tf_op jit(solution)/shard_map/attention_forward/pallas_call | solution.py:289
  62.1 1.6 collective-permute-done.11.p2
  63.7 0.5 collective-permute-start.15
  64.3 2.5 %collective-permute-done.14.p5 = bf16[4,8,24,768]{3,2,1,0:T(8,128)(2,1)S(1)} collective-permute-done((bf16[4,8,24,768]{3,2,1,0:T(8,128)(2,1)}, bf16[4,8,24,768]{3,2,1,0:T(8,128)(2,1)S(1)}, u32[]{:S(2)}, u32[]{:S(2)}) %collective-permute-start.14) | collective-permute-done | bytes 1179680 | tf_op jit(solution)/shard_map/ppermute | solution.py:747
  66.8 3.4 %collective-permute-done.15.p6 = bf16[4,8,24,768]{3,2,1,0:T(8,128)(2,1)S(1)} collective-permute-done((bf16[4,8,24,768]{3,2,1,0:T(8,128)(2,1)}, bf16[4,8,24,768]{3,2,1,0:T(8,128)(2,1)S(1)}, u32[]{:S(2)}, u32[]{:S(2)}) %collective-permute-start.15) | collective-permute-done | bytes 1179680 | tf_op jit(solution)/shard_map/ppermute | solution.py:747
  70.2 1.0 copy-done.11
  71.2 1.0 copy-done.12
  72.2 37.3 %feed.1 = (bf16[16,8,24,768]{3,2,1,0:T(8,128)(2,1)}, bf16[16,8,24,768]{3,2,1,0:T(8,128)(2,1)}, bf16[128,768]{1,0:T(8,128)(2,1)}, bf16[512,768]{1,0:T(8,128)(2,1)...) custom-call(s32[2]{0:T(128)} %slen.3, s32[2]{0:T(128)} %llen.3, ...), custom_call_target="tpu_custom_call" | custom-call | flops 18119393280 | bytes 30000000 | tf_op jit(solution)/shard_map/feed/pallas_call | solution.py:506
  109.7 11.8 %attention_back.1 = (bf16[640,768]{1,0:T(8,128)(2,1)}, bf16[640,768]{1,0:T(8,128)(2,1)}, bf16[640,768]{1,0:T(8,128)(2,1)}) custom-call(bf16[640,768]{1,0:T(8,128)(2,1)} %get-tuple-element.104.gatt.gatt_cols, bf16[32,104,768]{2,1,0:T(8,128)(2,1)} %get-tuple-element.106.wo_block.wq.wk.wv, bf16[640,768]{1,0:T(8,128)(2,1)} %get-tuple-element.107.q, ...), custom_call_target="tpu_custom_call" | custom-call | flops 3019898880 | bytes 15000000 | tf_op jit(solution)/shard_map/attention_back/pallas_call | solution.py:571
  121.6 3.9 %add_convert_fusion = (bf16[4,8,24,768]{3,2,1,0:T(8,128)(2,1)}, bf16[4,8,24,768]{3,2,1,0:T(8,128)(2,1)}, bf16[4,8,24,768]{3,2,1,0:T(8,128)(2,1)}, bf16[4,8,24,768]{3,2,1,0:T(8,128)(2,1)S(1)}) fusion(bf16[16,8,24,768]{3,2,1,0:T(8,128)(2,1)} %collective-permute-done.17, bf16[16,8,24,768]{3,2,1,0:T(8,128)(2,1)S(1)} %bitcast.63), kind=kLoop, calls=%fused_computation | loop fusion | flops 9437184 | bytes 14155776 | tf_op jit(solution)/shard_map/convert_element_type | solution.py:718
  125.5 1.4 collective-permute-start.18
  126.9 1.8 collective-permute-start.19
  128.7 1.7 collective-permute-start.20
  130.4 11.2 %weight_back.1 = (bf16[16,104,768]{2,1,0:T(8,128)(2,1)}, bf16[4,104,768]{2,1,0:T(8,128)(2,1)}, bf16[4,104,768]{2,1,0:T(8,128)(2,1)}, bf16[4,104,768]{2,1,0:T(8,128)(2,1)}, bf16[4,104,768]{2,1,0:T(8,128)(2,1)}) custom-call(s32[3]{0:T(128)} %pad_add_fusion.pos, bf16[640,768]{1,0:T(8,128)(2,1)} %get-tuple-element.104.gatt.gatt_cols, ...), custom_call_target="tpu_custom_call" | custom-call | flops 3019898880 | bytes 12000000 | tf_op jit(solution)/shard_map/weight_back/pallas_call | solution.py:643
  141.7 0.5 collective-permute-start.22
  142.2 0.9 collective-permute-done.18
  143.1 12.3 %collective-permute-done.19 = bf16[4,8,24,768]{3,2,1,0:T(8,128)(2,1)S(1)} collective-permute-done((bf16[4,8,24,768]{3,2,1,0:T(8,128)(2,1)}, bf16[4,8,24,768]{3,2,1,0:T(8,128)(2,1)S(1)}, u32[]{:S(2)}, u32[]{:S(2)}) %collective-permute-start.19) | collective-permute-done | bytes 1179680 | tf_op jit(solution)/shard_map/ppermute | solution.py:751
  155.4 1.2 collective-permute-done.20
  156.6 0.4 fusion.3
  157.1 2.5 %collective-permute-start.28 = (bf16[8,24,768]{2,1,0:T(8,128)(2,1)S(1)}, bf16[8,24,768]{2,1,0:T(8,128)(2,1)S(1)}, u32[]{:S(2)}, u32[]{:S(2)}) collective-permute-start(bf16[8,24,768]{2,1,0:T(8,128)(2,1)S(1)} %get-tuple-element.169), channel_id=1, source_target_pairs={{0,4},{1,17},{2,6},{3,19},{4,0},{5,21},{6,2},{7,23},{8,12},{9,25},... | collective-permute-start | bytes 884744 | tf_op jit(solution)/shard_map/ppermute | solution.py:751
  159.6 2.4 %add_convert_fusion.4 = (bf16[4,104,768]{2,1,0:T(8,128)(2,1)S(1)}, bf16[4,104,768]{2,1,0:T(8,128)(2,1)S(1)}, bf16[4,104,768]{2,1,0:T(8,128)(2,1)S(1)}, bf16[4,104,768]{2,1,0:T(8,128)(2,1)S(1)}) fusion(bf16[4,104,768]{2,1,0:T(8,128)(2,1)S(1)} %collective-permute-done.24, bf16[16,104,768]{2,1,0:T(8,128)(2,1)} %get-tuple-element.124, ...), kind=kLoop, calls=%fused_computation.4 | loop fusion | flops 5111808 | bytes 7667712 | tf_op jit(solution)/shard_map/convert_element_type | solution.py:724
  162.1 1.5 collective-permute-start.25
  163.5 1.8 collective-permute-start.26
  165.4 0.6 collective-permute-start.27
  166.0 1.9 collective-permute-start.30
  168.1 5.4 %input_back.1 = (f32[128,768]{1,0:T(8,128)}, f32[512,768]{1,0:T(8,128)}) custom-call(f32[640,768]{1,0:T(8,128)S(1)} %copy-done, bf16[640,768]{1,0:T(8,128)(2,1)S(1)} %copy-done.1, bf16[640,768]{1,0:T(8,128)(2,1)S(1)} %copy-done.2, bf16[640,768]{1,0:T(8,128)(2,1)S(1)} %copy-done.3, bf16[32,104,768]{2,1,0:T(8,128)(2,1)S(1)} %bitcast.61, ...), custom_call_target="tpu_custom_call" | custom-call | flops 2264924160 | bytes 12000000 | tf_op jit(solution)/shard_map/input_back/pallas_call | solution.py:698
  173.4 8.0 %collective-permute-done.30 = bf16[8,24,768]{2,1,0:T(8,128)(2,1)S(1)} collective-permute-done((bf16[8,24,768]{2,1,0:T(8,128)(2,1)S(1)}, bf16[8,24,768]{2,1,0:T(8,128)(2,1)S(1)}, u32[]{:S(2)}, u32[]{:S(2)}) %collective-permute-start.30) | collective-permute-done | bytes 294944 | tf_op jit(solution)/shard_map/ppermute | solution.py:751
  181.5 1.2 collective-permute-done.29
  182.9 3.3 %collective-permute-start.34 = (bf16[8,24,768]{2,1,0:T(8,128)(2,1)S(1)}, bf16[8,24,768]{2,1,0:T(8,128)(2,1)S(1)}, u32[]{:S(2)}, u32[]{:S(2)}) collective-permute-start(bf16[8,24,768]{2,1,0:T(8,128)(2,1)S(1)} %fusion.1.own), channel_id=1, source_target_pairs={{0,64},{32,96},{64,0},{96,32},{1,65},{33,97},{65,1},{97,33},{2,66}... | collective-permute-start | bytes 884744 | tf_op jit(solution)/shard_map/ppermute | solution.py:764
  186.2 0.3 fusion.9
  186.6 2.6 %collective-permute-start.32 = (bf16[104,768]{1,0:T(8,128)(2,1)S(1)}, bf16[104,768]{1,0:T(8,128)(2,1)S(1)}, u32[]{:S(2)}, u32[]{:S(2)}) collective-permute-start(bf16[104,768]{1,0:T(8,128)(2,1)S(1)} %get-tuple-element.173), channel_id=1, source_target_pairs={{0,6},{1,25},{2,0},{3,27},{4,2},{5,29},{6,4},{7,31},{8,14},{9,1},{... | collective-permute-start | bytes 479240 | tf_op jit(solution)/shard_map/ppermute | solution.py:751
  189.2 0.8 collective-permute-start.31
  190.0 1.5 collective-permute-start.39
  191.5 1.8 collective-permute-start.38
  193.4 1.6 collective-permute-done.32
  195.0 0.7 collective-permute-done.31
  195.8 2.5 %collective-permute-start.37 = (bf16[104,768]{1,0:T(8,128)(2,1)S(1)}, bf16[104,768]{1,0:T(8,128)(2,1)S(1)}, u32[]{:S(2)}, u32[]{:S(2)}) collective-permute-start(bf16[104,768]{1,0:T(8,128)(2,1)S(1)} %add_convert_fusion.12.own), channel_id=1, source_target_pairs={{0,64},{32,96},{64,0},{96,32},{1,65},{33,97},{65,1},{97,33},{2,66}... | collective-permute-start | bytes 479240 | tf_op jit(solution)/shard_map/ppermute | solution.py:764
  198.4 1.1 collective-permute-start.36
  199.4 1.0 collective-permute-start.35
  200.5 2.8 %collective-permute-done.38.left = bf16[8,24,768]{2,1,0:T(8,128)(2,1)S(1)} collective-permute-done((bf16[8,24,768]{2,1,0:T(8,128)(2,1)S(1)}, bf16[8,24,768]{2,1,0:T(8,128)(2,1)S(1)}, u32[]{:S(2)}, u32[]{:S(2)}) %collective-permute-start.38) | collective-permute-done | bytes 294944 | tf_op jit(solution)/shard_map/ppermute | solution.py:764
  203.2 0.9 finish_feed.1
  204.2 1.6 collective-permute-done.37.far
  205.7 1.6 collective-permute-done.35.left
  207.3 0.8 finish_attention.1
  (86 shorter events, 2.2 us)
Async XLA Ops:
  2.7 10.7 %collective-permute-start.2 = (bf16[296,768]{1,0:T(8,128)(2,1)}, bf16[296,768]{1,0:T(8,128)(2,1)S(1)}, u32[]{:S(2)}, u32[]{:S(2)}) collective-permute-start(bf16[296,768]{1,0:T(8,128)(2,1)} %pack.1), channel_id=1, source_target_pairs={{0,4},{1,17},{2,6},{3,19},{4,0},{5,21},{6,2},{7,23},{8,12},{9,25},... | collective-permute-start | bytes 1363976 | tf_op jit(solution)/shard_map/ppermute | solution.py:751
  6.6 12.6 %collective-permute-start.1 = (bf16[296,768]{1,0:T(8,128)(2,1)}, bf16[296,768]{1,0:T(8,128)(2,1)S(1)}, u32[]{:S(2)}, u32[]{:S(2)}) collective-permute-start(bf16[296,768]{1,0:T(8,128)(2,1)} %pack.1), channel_id=1, source_target_pairs={{0,6},{1,25},{2,0},{3,27},{4,2},{5,29},{6,4},{7,31},{8,14},{9,1},{... | collective-permute-start | bytes 1363976 | tf_op jit(solution)/shard_map/ppermute | solution.py:751
  7.3 11.9 %collective-permute-start = (bf16[296,768]{1,0:T(8,128)(2,1)}, bf16[296,768]{1,0:T(8,128)(2,1)S(1)}, u32[]{:S(2)}, u32[]{:S(2)}) collective-permute-start(bf16[296,768]{1,0:T(8,128)(2,1)} %pack.1), channel_id=1, source_target_pairs={{0,2},{1,9},{2,4},{3,11},{4,6},{5,13},{6,0},{7,15},{8,10},{9,17},{... | collective-permute-start | bytes 1363976 | tf_op jit(solution)/shard_map/ppermute | solution.py:751
  9.6 21.8 %copy-start.4 = (bf16[296,768]{1,0:T(8,128)(2,1)S(1)}, bf16[296,768]{1,0:T(8,128)(2,1)}, u32[]{:S(2)}) copy-start(bf16[296,768]{1,0:T(8,128)(2,1)} %pack.1) | copy-start | bytes 1363972
  13.4 18.1 %copy-start.5 = (bf16[296,768]{1,0:T(8,128)(2,1)}, bf16[296,768]{1,0:T(8,128)(2,1)S(1)}, u32[]{:S(2)}) copy-start(bf16[296,768]{1,0:T(8,128)(2,1)S(1)} %collective-permute-done.2) | copy-start | bytes 1363972
  19.3 12.2 %copy-start.7 = (bf16[4,104,768]{2,1,0:T(8,128)(2,1)}, bf16[4,104,768]{2,1,0:T(8,128)(2,1)S(1)}, u32[]{:S(2)}) copy-start(bf16[4,104,768]{2,1,0:T(8,128)(2,1)S(1)} %pad_maximum_fusion.1.p0) | copy-start | bytes 1916932
  19.3 12.1 %collective-permute-start.5 = (bf16[4,104,768]{2,1,0:T(8,128)(2,1)S(1)}, bf16[4,104,768]{2,1,0:T(8,128)(2,1)S(1)}, u32[]{:S(2)}, u32[]{:S(2)}) collective-permute-start(bf16[4,104,768]{2,1,0:T(8,128)(2,1)S(1)} %pad_maximum_fusion.1.p0), channel_id=1, source_target_pairs={{0,16},{1,5},{2,18},{3,7},{4,20},{5,1},{6,22},{7,3},{8,24},{9,13},... | collective-permute-start | bytes 1916936 | tf_op jit(solution)/shard_map/ppermute | solution.py:751
  22.4 13.5 %collective-permute-start.6 = (bf16[4,104,768]{2,1,0:T(8,128)(2,1)S(1)}, bf16[4,104,768]{2,1,0:T(8,128)(2,1)S(1)}, u32[]{:S(2)}, u32[]{:S(2)}) collective-permute-start(bf16[4,104,768]{2,1,0:T(8,128)(2,1)S(1)} %pad_maximum_fusion.1.p0), channel_id=1, source_target_pairs={{0,1},{1,0},{2,3},{3,2},{4,5},{5,4},{6,7},{7,6},{8,9},{9,8},{10,11... | collective-permute-start | bytes 1916936 | tf_op jit(solution)/shard_map/ppermute | solution.py:747
  22.4 16.0 %collective-permute-start.4 = (bf16[4,104,768]{2,1,0:T(8,128)(2,1)S(1)}, bf16[4,104,768]{2,1,0:T(8,128)(2,1)}, u32[]{:S(2)}, u32[]{:S(2)}) collective-permute-start(bf16[4,104,768]{2,1,0:T(8,128)(2,1)S(1)} %pad_maximum_fusion.1.p0), channel_id=1, source_target_pairs={{0,24},{1,7},{2,26},{3,1},{4,28},{5,3},{6,30},{7,5},{8,0},{9,15},{... | collective-permute-start | bytes 1916936 | tf_op jit(solution)/shard_map/ppermute | solution.py:751
  23.6 16.2 %collective-permute-start.3 = (bf16[4,104,768]{2,1,0:T(8,128)(2,1)S(1)}, bf16[4,104,768]{2,1,0:T(8,128)(2,1)}, u32[]{:S(2)}, u32[]{:S(2)}) collective-permute-start(bf16[4,104,768]{2,1,0:T(8,128)(2,1)S(1)} %pad_maximum_fusion.1.p0), channel_id=1, source_target_pairs={{0,8},{1,3},{2,10},{3,5},{4,12},{5,7},{6,14},{7,1},{8,16},{9,11},{... | collective-permute-start | bytes 1916936 | tf_op jit(solution)/shard_map/ppermute | solution.py:751
  31.4 0.9 copy-start.13
  31.4 8.3 %collective-permute-start.9 = (bf16[4,104,768]{2,1,0:T(8,128)(2,1)S(1)}, bf16[4,104,768]{2,1,0:T(8,128)(2,1)S(1)}, u32[]{:S(2)}, u32[]{:S(2)}) collective-permute-start(bf16[4,104,768]{2,1,0:T(8,128)(2,1)S(1)} %collective-permute-done.5.p3), channel_id=1, source_target_pairs={{0,1},{1,0},{2,3},{3,2},{4,5},{5,4},{6,7},{7,6},{8,9},{9,8},{10,11... | collective-permute-start | bytes 1916936 | tf_op jit(solution)/shard_map/ppermute | solution.py:747
  31.5 1.2 slice-start.4
  32.8 29.3 %copy-start.6 = (bf16[4,8,24,768]{3,2,1,0:T(8,128)(2,1)}, bf16[4,8,24,768]{3,2,1,0:T(8,128)(2,1)S(1)}, u32[]{:S(2)}) copy-start(bf16[4,8,24,768]{3,2,1,0:T(8,128)(2,1)S(1)} %pad_maximum_fusion.p0) | copy-start | bytes 3538948
  32.8 29.3 %collective-permute-start.12 = (bf16[4,8,24,768]{3,2,1,0:T(8,128)(2,1)S(1)}, bf16[4,8,24,768]{3,2,1,0:T(8,128)(2,1)S(1)}, u32[]{:S(2)}, u32[]{:S(2)}) collective-permute-start(bf16[4,8,24,768]{3,2,1,0:T(8,128)(2,1)S(1)} %pad_maximum_fusion.p0), channel_id=1, source_target_pairs={{0,16},{1,5},{2,18},{3,7},{4,20},{5,1},{6,22},{7,3},{8,24},{9,13},... | collective-permute-start | bytes 3538952 | tf_op jit(solution)/shard_map/ppermute | solution.py:751
  35.9 3.9 %copy-start.14 = (bf16[4,104,768]{2,1,0:T(8,128)(2,1)}, bf16[4,104,768]{2,1,0:T(8,128)(2,1)S(1)}, u32[]{:S(2)}) copy-start(bf16[4,104,768]{2,1,0:T(8,128)(2,1)S(1)} %collective-permute-done.6.p4) | copy-start | bytes 1916932
  35.9 27.8 %collective-permute-start.11 = (bf16[4,8,24,768]{3,2,1,0:T(8,128)(2,1)S(1)}, bf16[4,8,24,768]{3,2,1,0:T(8,128)(2,1)}, u32[]{:S(2)}, u32[]{:S(2)}) collective-permute-start(bf16[4,8,24,768]{3,2,1,0:T(8,128)(2,1)S(1)} %pad_maximum_fusion.p0), channel_id=1, source_target_pairs={{0,24},{1,7},{2,26},{3,1},{4,28},{5,3},{6,30},{7,5},{8,0},{9,15},{... | collective-permute-start | bytes 3538952 | tf_op jit(solution)/shard_map/ppermute | solution.py:751
  38.4 25.3 %collective-permute-start.10 = (bf16[4,8,24,768]{3,2,1,0:T(8,128)(2,1)S(1)}, bf16[4,8,24,768]{3,2,1,0:T(8,128)(2,1)}, u32[]{:S(2)}, u32[]{:S(2)}) collective-permute-start(bf16[4,8,24,768]{3,2,1,0:T(8,128)(2,1)S(1)} %pad_maximum_fusion.p0), channel_id=1, source_target_pairs={{0,8},{1,3},{2,10},{3,5},{4,12},{5,7},{6,14},{7,1},{8,16},{9,11},{... | collective-permute-start | bytes 3538952 | tf_op jit(solution)/shard_map/ppermute | solution.py:751
  39.8 2.3 %collective-permute-start.8 = (bf16[4,104,768]{2,1,0:T(8,128)(2,1)}, bf16[4,104,768]{2,1,0:T(8,128)(2,1)S(1)}, u32[]{:S(2)}, u32[]{:S(2)}) collective-permute-start(bf16[4,104,768]{2,1,0:T(8,128)(2,1)} %collective-permute-done.4.p2), channel_id=1, source_target_pairs={{0,1},{1,0},{2,3},{3,2},{4,5},{5,4},{6,7},{7,6},{8,9},{9,8},{10,11... | collective-permute-start | bytes 1916936 | tf_op jit(solution)/shard_map/ppermute | solution.py:747
  39.8 0.8 copy-start.15
  39.8 3.3 %collective-permute-start.7 = (bf16[4,104,768]{2,1,0:T(8,128)(2,1)}, bf16[4,104,768]{2,1,0:T(8,128)(2,1)}, u32[]{:S(2)}, u32[]{:S(2)}) collective-permute-start(bf16[4,104,768]{2,1,0:T(8,128)(2,1)} %collective-permute-done.3.p1), channel_id=1, source_target_pairs={{0,1},{1,0},{2,3},{3,2},{4,5},{5,4},{6,7},{7,6},{8,9},{9,8},{10,11... | collective-permute-start | bytes 1916936 | tf_op jit(solution)/shard_map/ppermute | solution.py:747
  42.1 1.0 copy-start.16
  42.1 22.2 %collective-permute-start.13 = (bf16[4,8,24,768]{3,2,1,0:T(8,128)(2,1)S(1)}, bf16[4,8,24,768]{3,2,1,0:T(8,128)(2,1)S(1)}, u32[]{:S(2)}, u32[]{:S(2)}) collective-permute-start(bf16[4,8,24,768]{3,2,1,0:T(8,128)(2,1)S(1)} %pad_maximum_fusion.p0), channel_id=1, source_target_pairs={{0,1},{1,0},{2,3},{3,2},{4,5},{5,4},{6,7},{7,6},{8,9},{9,8},{10,11... | collective-permute-start | bytes 3538952 | tf_op jit(solution)/shard_map/ppermute | solution.py:747
  62.1 10.1 %copy-start.8 = (bf16[4,8,24,768]{3,2,1,0:T(8,128)(2,1)}, bf16[4,8,24,768]{3,2,1,0:T(8,128)(2,1)S(1)}, u32[]{:S(2)}) copy-start(bf16[4,8,24,768]{3,2,1,0:T(8,128)(2,1)S(1)} %collective-permute-done.12.p3) | copy-start | bytes 3538948
  63.7 3.1 %collective-permute-start.14 = (bf16[4,8,24,768]{3,2,1,0:T(8,128)(2,1)}, bf16[4,8,24,768]{3,2,1,0:T(8,128)(2,1)S(1)}, u32[]{:S(2)}, u32[]{:S(2)}) collective-permute-start(bf16[4,8,24,768]{3,2,1,0:T(8,128)(2,1)} %collective-permute-done.10.p1), channel_id=1, source_target_pairs={{0,1},{1,0},{2,3},{3,2},{4,5},{5,4},{6,7},{7,6},{8,9},{9,8},{10,11... | collective-permute-start | bytes 3538952 | tf_op jit(solution)/shard_map/ppermute | solution.py:747
  63.7 6.4 %collective-permute-start.15 = (bf16[4,8,24,768]{3,2,1,0:T(8,128)(2,1)}, bf16[4,8,24,768]{3,2,1,0:T(8,128)(2,1)S(1)}, u32[]{:S(2)}, u32[]{:S(2)}) collective-permute-start(bf16[4,8,24,768]{3,2,1,0:T(8,128)(2,1)} %collective-permute-done.11.p2), channel_id=1, source_target_pairs={{0,1},{1,0},{2,3},{3,2},{4,5},{5,4},{6,7},{7,6},{8,9},{9,8},{10,11... | collective-permute-start | bytes 3538952 | tf_op jit(solution)/shard_map/ppermute | solution.py:747
  64.3 5.9 %collective-permute-start.16 = (bf16[4,8,24,768]{3,2,1,0:T(8,128)(2,1)S(1)}, bf16[4,8,24,768]{3,2,1,0:T(8,128)(2,1)S(1)}, u32[]{:S(2)}, u32[]{:S(2)}) collective-permute-start(bf16[4,8,24,768]{3,2,1,0:T(8,128)(2,1)S(1)} %collective-permute-done.12.p3), channel_id=1, source_target_pairs={{0,1},{1,0},{2,3},{3,2},{4,5},{5,4},{6,7},{7,6},{8,9},{9,8},{10,11... | collective-permute-start | bytes 3538952 | tf_op jit(solution)/shard_map/ppermute | solution.py:747
  64.3 8.0 %copy-start.9 = (bf16[4,8,24,768]{3,2,1,0:T(8,128)(2,1)}, bf16[4,8,24,768]{3,2,1,0:T(8,128)(2,1)S(1)}, u32[]{:S(2)}) copy-start(bf16[4,8,24,768]{3,2,1,0:T(8,128)(2,1)S(1)} %collective-permute-done.13.p4) | copy-start | bytes 3538948
  66.8 5.4 %copy-start.10 = (bf16[4,8,24,768]{3,2,1,0:T(8,128)(2,1)}, bf16[4,8,24,768]{3,2,1,0:T(8,128)(2,1)S(1)}, u32[]{:S(2)}) copy-start(bf16[4,8,24,768]{3,2,1,0:T(8,128)(2,1)S(1)} %collective-permute-done.14.p5) | copy-start | bytes 3538948
  70.2 1.0 copy-start.11
  71.2 1.0 copy-start.12
  109.5 12.1 %collective-permute-start.17 = (bf16[16,8,24,768]{3,2,1,0:T(8,128)(2,1)}, bf16[16,8,24,768]{3,2,1,0:T(8,128)(2,1)}, u32[]{:S(2)}, u32[]{:S(2)}) collective-permute-start(bf16[16,8,24,768]{3,2,1,0:T(8,128)(2,1)} %get-tuple-element.116), channel_id=1, source_target_pairs={{0,1},{1,0},{2,3},{3,2},{4,5},{5,4},{6,7},{7,6},{8,9},{9,8},{10,11... | collective-permute-start | bytes 14155784 | tf_op jit(solution)/shard_map/ppermute | solution.py:747
  109.7 11.9 %slice-start.2 = ((s8[4718592]{0:T(1024)(128)(4,1)}), s8[4194304]{0:T(1024)(128)(4,1)S(1)}, s32[]{:S(2)}) async-start(s8[4718592]{0:T(1024)(128)(4,1)} %bitcast.62), calls=%async_computation.2 | async-start | bytes 8388608
  109.7 11.9 %slice-start.3 = ((s8[4718592]{0:T(1024)(128)(4,1)}), s8[524288]{0:T(1024)(128)(4,1)S(1)}, s32[]{:S(2)}) async-start(s8[4718592]{0:T(1024)(128)(4,1)} %bitcast.62), calls=%async_computation.3 | async-start | bytes 1048576
  125.5 17.6 %collective-permute-start.18 = (bf16[4,8,24,768]{3,2,1,0:T(8,128)(2,1)}, bf16[4,8,24,768]{3,2,1,0:T(8,128)(2,1)S(1)}, u32[]{:S(2)}, u32[]{:S(2)}) collective-permute-start(bf16[4,8,24,768]{3,2,1,0:T(8,128)(2,1)} %get-tuple-element.121), channel_id=1, source_target_pairs={{0,8},{1,3},{2,10},{3,5},{4,12},{5,7},{6,14},{7,1},{8,16},{9,11},{... | collective-permute-start | bytes 3538952 | tf_op jit(solution)/shard_map/ppermute | solution.py:751
  126.9 28.5 %collective-permute-start.19 = (bf16[4,8,24,768]{3,2,1,0:T(8,128)(2,1)}, bf16[4,8,24,768]{3,2,1,0:T(8,128)(2,1)S(1)}, u32[]{:S(2)}, u32[]{:S(2)}) collective-permute-start(bf16[4,8,24,768]{3,2,1,0:T(8,128)(2,1)} %get-tuple-element.122), channel_id=1, source_target_pairs={{0,24},{1,7},{2,26},{3,1},{4,28},{5,3},{6,30},{7,5},{8,0},{9,15},{... | collective-permute-start | bytes 3538952 | tf_op jit(solution)/shard_map/ppermute | solution.py:751
  128.7 27.9 %collective-permute-start.20 = (bf16[4,8,24,768]{3,2,1,0:T(8,128)(2,1)}, bf16[4,8,24,768]{3,2,1,0:T(8,128)(2,1)S(1)}, u32[]{:S(2)}, u32[]{:S(2)}) collective-permute-start(bf16[4,8,24,768]{3,2,1,0:T(8,128)(2,1)} %get-tuple-element.123), channel_id=1, source_target_pairs={{0,16},{1,5},{2,18},{3,7},{4,20},{5,1},{6,22},{7,3},{8,24},{9,13},... | collective-permute-start | bytes 3538952 | tf_op jit(solution)/shard_map/ppermute | solution.py:751
  141.6 18.0 %collective-permute-start.21 = (bf16[4,104,768]{2,1,0:T(8,128)(2,1)}, bf16[4,104,768]{2,1,0:T(8,128)(2,1)S(1)}, u32[]{:S(2)}, u32[]{:S(2)}) collective-permute-start(bf16[4,104,768]{2,1,0:T(8,128)(2,1)} %get-tuple-element.125), channel_id=1, source_target_pairs={{0,1},{1,0},{2,3},{3,2},{4,5},{5,4},{6,7},{7,6},{8,9},{9,8},{10,11... | collective-permute-start | bytes 1916936 | tf_op jit(solution)/shard_map/ppermute | solution.py:747
  141.7 17.9 %collective-permute-start.22 = (bf16[4,104,768]{2,1,0:T(8,128)(2,1)}, bf16[4,104,768]{2,1,0:T(8,128)(2,1)S(1)}, u32[]{:S(2)}, u32[]{:S(2)}) collective-permute-start(bf16[4,104,768]{2,1,0:T(8,128)(2,1)} %get-tuple-element.126), channel_id=1, source_target_pairs={{0,1},{1,0},{2,3},{3,2},{4,5},{5,4},{6,7},{7,6},{8,9},{9,8},{10,11... | collective-permute-start | bytes 1916936 | tf_op jit(solution)/shard_map/ppermute | solution.py:747
  143.1 16.5 %collective-permute-start.23 = (bf16[4,104,768]{2,1,0:T(8,128)(2,1)}, bf16[4,104,768]{2,1,0:T(8,128)(2,1)S(1)}, u32[]{:S(2)}, u32[]{:S(2)}) collective-permute-start(bf16[4,104,768]{2,1,0:T(8,128)(2,1)} %get-tuple-element.127), channel_id=1, source_target_pairs={{0,1},{1,0},{2,3},{3,2},{4,5},{5,4},{6,7},{7,6},{8,9},{9,8},{10,11... | collective-permute-start | bytes 1916936 | tf_op jit(solution)/shard_map/ppermute | solution.py:747
  155.4 4.2 %collective-permute-start.24 = (bf16[4,104,768]{2,1,0:T(8,128)(2,1)}, bf16[4,104,768]{2,1,0:T(8,128)(2,1)S(1)}, u32[]{:S(2)}, u32[]{:S(2)}) collective-permute-start(bf16[4,104,768]{2,1,0:T(8,128)(2,1)} %get-tuple-element.128), channel_id=1, source_target_pairs={{0,1},{1,0},{2,3},{3,2},{4,5},{5,4},{6,7},{7,6},{8,9},{9,8},{10,11... | collective-permute-start | bytes 1916936 | tf_op jit(solution)/shard_map/ppermute | solution.py:747
  156.6 11.4 %slice-start = ((s8[5111808]{0:T(1024)(128)(4,1)}), s8[4194304]{0:T(1024)(128)(4,1)S(1)}, s32[]{:S(2)}) async-start(s8[5111808]{0:T(1024)(128)(4,1)} %bitcast.60), calls=%async_computation | async-start | bytes 8388608
  157.0 11.0 %slice-start.1 = ((s8[5111808]{0:T(1024)(128)(4,1)}), s8[917504]{0:T(1024)(128)(4,1)S(1)}, s32[]{:S(2)}) async-start(s8[5111808]{0:T(1024)(128)(4,1)} %bitcast.60), calls=%async_computation.1 | async-start | bytes 1835008
  157.0 11.0 %copy-start.1 = (bf16[640,768]{1,0:T(8,128)(2,1)S(1)}, bf16[640,768]{1,0:T(8,128)(2,1)}, u32[]{:S(2)}) copy-start(bf16[640,768]{1,0:T(8,128)(2,1)} %get-tuple-element.112.dq) | copy-start | bytes 2949124
  157.1 11.0 %copy-start.2 = (bf16[640,768]{1,0:T(8,128)(2,1)S(1)}, bf16[640,768]{1,0:T(8,128)(2,1)}, u32[]{:S(2)}) copy-start(bf16[640,768]{1,0:T(8,128)(2,1)} %get-tuple-element.113.dk) | copy-start | bytes 2949124
  157.1 11.0 %copy-start.3 = (bf16[640,768]{1,0:T(8,128)(2,1)S(1)}, bf16[640,768]{1,0:T(8,128)(2,1)}, u32[]{:S(2)}) copy-start(bf16[640,768]{1,0:T(8,128)(2,1)} %get-tuple-element.117.dv) | copy-start | bytes 2949124
  157.1 10.8 %collective-permute-start.28 = (bf16[8,24,768]{2,1,0:T(8,128)(2,1)S(1)}, bf16[8,24,768]{2,1,0:T(8,128)(2,1)S(1)}, u32[]{:S(2)}, u32[]{:S(2)}) collective-permute-start(bf16[8,24,768]{2,1,0:T(8,128)(2,1)S(1)} %get-tuple-element.169), channel_id=1, source_target_pairs={{0,4},{1,17},{2,6},{3,19},{4,0},{5,21},{6,2},{7,23},{8,12},{9,25},... | collective-permute-start | bytes 884744 | tf_op jit(solution)/shard_map/ppermute | solution.py:751
  159.6 8.4 %copy-start = (f32[640,768]{1,0:T(8,128)S(1)}, f32[640,768]{1,0:T(8,128)}, u32[]{:S(2)}) copy-start(f32[640,768]{1,0:T(8,128)} %get-tuple-element.129.gfs) | copy-start | bytes 5898244
  162.1 24.1 %collective-permute-start.25 = (bf16[4,104,768]{2,1,0:T(8,128)(2,1)S(1)}, bf16[4,104,768]{2,1,0:T(8,128)(2,1)S(1)}, u32[]{:S(2)}, u32[]{:S(2)}) collective-permute-start(bf16[4,104,768]{2,1,0:T(8,128)(2,1)S(1)} %get-tuple-element.131), channel_id=1, source_target_pairs={{0,8},{1,3},{2,10},{3,5},{4,12},{5,7},{6,14},{7,1},{8,16},{9,11},{... | collective-permute-start | bytes 1916936 | tf_op jit(solution)/shard_map/ppermute | solution.py:751
  163.5 22.7 %collective-permute-start.26 = (bf16[4,104,768]{2,1,0:T(8,128)(2,1)S(1)}, bf16[4,104,768]{2,1,0:T(8,128)(2,1)S(1)}, u32[]{:S(2)}, u32[]{:S(2)}) collective-permute-start(bf16[4,104,768]{2,1,0:T(8,128)(2,1)S(1)} %get-tuple-element.132), channel_id=1, source_target_pairs={{0,24},{1,7},{2,26},{3,1},{4,28},{5,3},{6,30},{7,5},{8,0},{9,15},{... | collective-permute-start | bytes 1916936 | tf_op jit(solution)/shard_map/ppermute | solution.py:751
  165.4 20.8 %collective-permute-start.27 = (bf16[4,104,768]{2,1,0:T(8,128)(2,1)S(1)}, bf16[4,104,768]{2,1,0:T(8,128)(2,1)S(1)}, u32[]{:S(2)}, u32[]{:S(2)}) collective-permute-start(bf16[4,104,768]{2,1,0:T(8,128)(2,1)S(1)} %get-tuple-element.133), channel_id=1, source_target_pairs={{0,16},{1,5},{2,18},{3,7},{4,20},{5,1},{6,22},{7,3},{8,24},{9,13},... | collective-permute-start | bytes 1916936 | tf_op jit(solution)/shard_map/ppermute | solution.py:751
  166.0 15.5 %collective-permute-start.30 = (bf16[8,24,768]{2,1,0:T(8,128)(2,1)S(1)}, bf16[8,24,768]{2,1,0:T(8,128)(2,1)S(1)}, u32[]{:S(2)}, u32[]{:S(2)}) collective-permute-start(bf16[8,24,768]{2,1,0:T(8,128)(2,1)S(1)} %get-tuple-element.170), channel_id=1, source_target_pairs={{0,6},{1,25},{2,0},{3,27},{4,2},{5,29},{6,4},{7,31},{8,14},{9,1},{... | collective-permute-start | bytes 884744 | tf_op jit(solution)/shard_map/ppermute | solution.py:751
  167.9 14.8 %collective-permute-start.29 = (bf16[8,24,768]{2,1,0:T(8,128)(2,1)S(1)}, bf16[8,24,768]{2,1,0:T(8,128)(2,1)S(1)}, u32[]{:S(2)}, u32[]{:S(2)}) collective-permute-start(bf16[8,24,768]{2,1,0:T(8,128)(2,1)S(1)} %get-tuple-element.171), channel_id=1, source_target_pairs={{0,2},{1,9},{2,4},{3,11},{4,6},{5,13},{6,0},{7,15},{8,10},{9,17},{... | collective-permute-start | bytes 884744 | tf_op jit(solution)/shard_map/ppermute | solution.py:751
  182.9 8.6 %collective-permute-start.34 = (bf16[8,24,768]{2,1,0:T(8,128)(2,1)S(1)}, bf16[8,24,768]{2,1,0:T(8,128)(2,1)S(1)}, u32[]{:S(2)}, u32[]{:S(2)}) collective-permute-start(bf16[8,24,768]{2,1,0:T(8,128)(2,1)S(1)} %fusion.1.own), channel_id=1, source_target_pairs={{0,64},{32,96},{64,0},{96,32},{1,65},{33,97},{65,1},{97,33},{2,66}... | collective-permute-start | bytes 884744 | tf_op jit(solution)/shard_map/ppermute | solution.py:764
  186.5 6.9 %collective-permute-start.33 = (bf16[104,768]{1,0:T(8,128)(2,1)S(1)}, bf16[104,768]{1,0:T(8,128)(2,1)S(1)}, u32[]{:S(2)}, u32[]{:S(2)}) collective-permute-start(bf16[104,768]{1,0:T(8,128)(2,1)S(1)} %get-tuple-element.172), channel_id=1, source_target_pairs={{0,4},{1,17},{2,6},{3,19},{4,0},{5,21},{6,2},{7,23},{8,12},{9,25},... | collective-permute-start | bytes 479240 | tf_op jit(solution)/shard_map/ppermute | solution.py:751
  186.6 8.4 %collective-permute-start.32 = (bf16[104,768]{1,0:T(8,128)(2,1)S(1)}, bf16[104,768]{1,0:T(8,128)(2,1)S(1)}, u32[]{:S(2)}, u32[]{:S(2)}) collective-permute-start(bf16[104,768]{1,0:T(8,128)(2,1)S(1)} %get-tuple-element.173), channel_id=1, source_target_pairs={{0,6},{1,25},{2,0},{3,27},{4,2},{5,29},{6,4},{7,31},{8,14},{9,1},{... | collective-permute-start | bytes 479240 | tf_op jit(solution)/shard_map/ppermute | solution.py:751
  189.2 6.5 %collective-permute-start.31 = (bf16[104,768]{1,0:T(8,128)(2,1)S(1)}, bf16[104,768]{1,0:T(8,128)(2,1)S(1)}, u32[]{:S(2)}, u32[]{:S(2)}) collective-permute-start(bf16[104,768]{1,0:T(8,128)(2,1)S(1)} %get-tuple-element.174), channel_id=1, source_target_pairs={{0,2},{1,9},{2,4},{3,11},{4,6},{5,13},{6,0},{7,15},{8,10},{9,17},{... | collective-permute-start | bytes 479240 | tf_op jit(solution)/shard_map/ppermute | solution.py:751
  190.0 10.4 %collective-permute-start.39 = (bf16[8,24,768]{2,1,0:T(8,128)(2,1)S(1)}, bf16[8,24,768]{2,1,0:T(8,128)(2,1)S(1)}, u32[]{:S(2)}, u32[]{:S(2)}) collective-permute-start(bf16[8,24,768]{2,1,0:T(8,128)(2,1)S(1)} %fusion.1.own), channel_id=1, source_target_pairs={{0,96},{32,0},{64,32},{96,64},{1,97},{33,1},{65,33},{97,65},{2,98}... | collective-permute-start | bytes 884744 | tf_op jit(solution)/shard_map/ppermute | solution.py:764
  191.5 11.7 %collective-permute-start.38 = (bf16[8,24,768]{2,1,0:T(8,128)(2,1)S(1)}, bf16[8,24,768]{2,1,0:T(8,128)(2,1)S(1)}, u32[]{:S(2)}, u32[]{:S(2)}) collective-permute-start(bf16[8,24,768]{2,1,0:T(8,128)(2,1)S(1)} %fusion.1.own), channel_id=1, source_target_pairs={{0,32},{32,64},{64,96},{96,0},{1,33},{33,65},{65,97},{97,1},{2,34}... | collective-permute-start | bytes 884744 | tf_op jit(solution)/shard_map/ppermute | solution.py:764
  195.8 9.9 %collective-permute-start.37 = (bf16[104,768]{1,0:T(8,128)(2,1)S(1)}, bf16[104,768]{1,0:T(8,128)(2,1)S(1)}, u32[]{:S(2)}, u32[]{:S(2)}) collective-permute-start(bf16[104,768]{1,0:T(8,128)(2,1)S(1)} %add_convert_fusion.12.own), channel_id=1, source_target_pairs={{0,64},{32,96},{64,0},{96,32},{1,65},{33,97},{65,1},{97,33},{2,66}... | collective-permute-start | bytes 479240 | tf_op jit(solution)/shard_map/ppermute | solution.py:764
  198.4 7.4 %collective-permute-start.36 = (bf16[104,768]{1,0:T(8,128)(2,1)S(1)}, bf16[104,768]{1,0:T(8,128)(2,1)S(1)}, u32[]{:S(2)}, u32[]{:S(2)}) collective-permute-start(bf16[104,768]{1,0:T(8,128)(2,1)S(1)} %add_convert_fusion.12.own), channel_id=1, source_target_pairs={{0,96},{32,0},{64,32},{96,64},{1,97},{33,1},{65,33},{97,65},{2,98}... | collective-permute-start | bytes 479240 | tf_op jit(solution)/shard_map/ppermute | solution.py:764
  199.4 7.9 %collective-permute-start.35 = (bf16[104,768]{1,0:T(8,128)(2,1)S(1)}, bf16[104,768]{1,0:T(8,128)(2,1)S(1)}, u32[]{:S(2)}, u32[]{:S(2)}) collective-permute-start(bf16[104,768]{1,0:T(8,128)(2,1)S(1)} %add_convert_fusion.12.own), channel_id=1, source_target_pairs={{0,32},{32,64},{64,96},{96,0},{1,33},{33,65},{65,97},{97,1},{2,34}... | collective-permute-start | bytes 479240 | tf_op jit(solution)/shard_map/ppermute | solution.py:764
